TPU v7x, 32 devices: a whole 2x2x4 slice. The times are simulated.
32 devices in a mesh: seq: 8 (over z, x), gate: 4 (over y, core).
Axes of the slice: x: 2, y: 2, z: 4, core: 2. Of those that a mesh axis runs over, the one named last changes fastest.
Arguments:
- layer_input: bfloat16 [8192, 2304], P('seq', 'gate'), may hold values from -6 to 6
- keep: int32 [8192], P('seq'), may hold values from 0 to 1, as said below
- w_now: bfloat16 [3, 2304, 2304], P(None, 'seq', 'gate'), may hold values from -0.09375 to 0.09375
- w_prev: bfloat16 [3, 2304, 2304], P(None, 'seq', 'gate'), may hold values from -0.09375 to 0.09375
- bias: float32 [3, 2304], P(None, 'gate'), may hold values from -2 to 10
- grad_out: bfloat16 [8192, 2304], P('seq', 'gate'), may hold values from -6 to 6
Outputs:
- hidden: bfloat16 [8192, 2304], P('seq', 'gate')
- grad_x: bfloat16 [8192, 2304], P('seq', 'gate')
- grad_now: float32 [3, 2304, 2304], P(None, 'seq', 'gate')
- grad_prev: float32 [3, 2304, 2304], P(None, 'seq', 'gate')
- grad_bias: float32 [3, 2304], P(None, 'gate')
Inputs may be any that keep to these rules, and one draw needn't show every extreme that they name: keep is 0 at the first token of every document and 1 elsewhere; the stream's first token begins a document; documents have uneven lengths and cross block ends.
All inputs are finite; a program needn't handle non-finite values.
Results may differ from a plain program's by a relative error of at most 0.0049.
Values may be sent and summed in bfloat16 or wider, within the bound.
No kernel may reach another device: no remote copies, remote signals or barrier semaphores. Data moves between devices by JAX's collectives and lax.ppermute only.
A program may use at most 320 MiB of HBM per device.

v0:
```python
import jax
import jax.numpy as jnp
from jax import lax
from jax.sharding import PartitionSpec as P


def from_behind(block, axis, distance):
    devices = range(lax.axis_size(axis))
    route = [(i - distance, i) for i in devices if i - distance in devices]
    return lax.ppermute(block, axis, route)


def combine(early, late):
    return (early[0] * late[0], early[1] * late[0] + late[1])


def on_device(layer_input, keep, w_now, w_prev, bias, grad_out):
    token_rows = lax.all_gather(layer_input, "gate", axis=1, tiled=True)
    from_prev = from_behind(token_rows[-1:], "seq", 1)
    keep_row = keep.astype(jnp.float32)[None, :]
    shifted = jnp.concatenate([from_prev, token_rows[:-1]], axis=0)
    prev_rows = jnp.where(keep[:, None] > 0, shifted, jnp.zeros_like(shifted))
    full_now, full_prev = (
        lax.all_gather(w_now, "seq", axis=1, tiled=True),
        lax.all_gather(w_prev, "seq", axis=1, tiled=True),
    )
    gates = jnp.einsum("td,kdc->kct", token_rows, full_now, preferred_element_type=jnp.float32)
    gates = gates + jnp.einsum(
        "td,kdc->kct", prev_rows, full_prev, preferred_element_type=jnp.float32
    )
    gates = gates + bias[:, :, None]
    cand = jnp.tanh(gates[0])
    forget = jax.nn.sigmoid(gates[1])
    intake = jax.nn.sigmoid(-gates[1])
    output = jax.nn.sigmoid(gates[2])
    closed = jax.nn.sigmoid(-gates[2])
    decays = keep_row * forget
    source = intake * cand
    long_decay, long_source = (
        lax.all_to_all(decays, "seq", split_axis=0, concat_axis=1, tiled=True),
        lax.all_to_all(source, "seq", split_axis=0, concat_axis=1, tiled=True),
    )
    factor, long_state = lax.associative_scan(combine, (long_decay, long_source), axis=1)
    long_prev = jnp.concatenate([jnp.zeros_like(long_state[:, :1]), long_state[:, :-1]], axis=1)
    states, prev_state = (
        lax.all_to_all(long_state, "seq", split_axis=1, concat_axis=0, tiled=True),
        lax.all_to_all(long_prev, "seq", split_axis=1, concat_axis=0, tiled=True),
    )
    hidden = (output * states).astype(jnp.bfloat16).T
    upstream = grad_out.T.astype(jnp.float32)
    direct = upstream * output
    output_grad = upstream * states * output * closed
    long_direct = lax.all_to_all(direct, "seq", split_axis=0, concat_axis=1, tiled=True)
    factor_back, long_back = lax.associative_scan(
        combine, (long_decay, long_decay * long_direct), reverse=True, axis=1
    )
    long_grads = long_direct + jnp.concatenate(
        [long_back[:, 1:], jnp.zeros_like(long_back[:, :1])], axis=1
    )
    grad_states = lax.all_to_all(long_grads, "seq", split_axis=1, concat_axis=0, tiled=True)
    update_grad = grad_states * intake * (1.0 - cand * cand)
    forget_grad = grad_states * (keep_row * prev_state - cand) * forget * intake
    gate_grads = jnp.stack([update_grad, forget_grad, output_grad], axis=0).astype(jnp.bfloat16)
    part_now = jnp.einsum("td,kct->kdc", token_rows, gate_grads, preferred_element_type=jnp.float32)
    part_prev = jnp.einsum("td,kct->kdc", prev_rows, gate_grads, preferred_element_type=jnp.float32)
    grad_now, grad_prev = (
        lax.psum_scatter(part_now, "seq", scatter_dimension=1, tiled=True),
        lax.psum_scatter(part_prev, "seq", scatter_dimension=1, tiled=True),
    )
    grad_bias = lax.psum(jnp.sum(gate_grads.astype(jnp.float32), axis=2), "seq")
    back_now = jnp.einsum("kct,kdc->td", gate_grads, full_now, preferred_element_type=jnp.float32)
    back_prev = jnp.einsum("kct,kdc->td", gate_grads, full_prev, preferred_element_type=jnp.float32)
    masked_prev = back_prev * keep.astype(jnp.float32)[:, None]
    from_next = from_behind(masked_prev[:1], "seq", -1)
    carried = jnp.concatenate([masked_prev[1:], from_next], axis=0)
    grad_x = lax.psum_scatter(back_now + carried, "gate", scatter_dimension=1, tiled=True).astype(
        jnp.bfloat16
    )
    return (hidden, grad_x, grad_now, grad_prev, grad_bias)


def solution(mesh):
    return jax.shard_map(
        on_device,
        mesh=mesh,
        in_specs=(
            P("seq", "gate"),
            P("seq"),
            P(None, "seq", "gate"),
            P(None, "seq", "gate"),
            P(None, "gate"),
            P("seq", "gate"),
        ),
        out_specs=(
            P("seq", "gate"),
            P("seq", "gate"),
            P(None, "seq", "gate"),
            P(None, "seq", "gate"),
            P(None, "gate"),
        ),
        check_vma=False,
    )
```

profile of v0, /device:TPU:0, one launch (start us, length us, event | category | flops | bytes accessed | tf_op | source)
XLA Modules:
  0.0 3067.2 jit_solution(17978084089852807589)
XLA Ops:
  9.4 40.4 %all-gather.6.cloned.1.call-done = bf16[1024,2304]{0,1:T(8,128)(2,1)} async-done(((bf16[1024,576]{0,1:T(8,128)(2,1)}), bf16[1024,2304]{0,1:T(8,128)(2,1)}) %all-gather.6.cloned.1.call-update) | async-done | bytes 4718608 | tf_op jit(solution)/shard_map/all_gather | solution.py:18
  56.4 126.4 %all-gather.4.cloned.1.call-done = bf16[3,2304,576]{2,1,0:T(8,128)(2,1)} async-done(((bf16[3,288,576]{2,1,0:T(8,128)(2,1)}), bf16[3,2304,576]{2,1,0:T(8,128)(2,1)}) %all-gather.4.cloned.1.call-update) | async-done | bytes 7962640 | tf_op jit(solution)/shard_map/all_gather | solution.py:24
  197.6 116.5 %all-gather.8.cloned.1.call-done = bf16[3,2304,576]{2,1,0:T(8,128)(2,1)} async-done(((bf16[3,288,576]{2,1,0:T(8,128)(2,1)}), bf16[3,2304,576]{2,1,0:T(8,128)(2,1)}) %all-gather.8.cloned.1.call-update) | async-done | bytes 7962640 | tf_op jit(solution)/shard_map/all_gather | solution.py:25
  314.1 16.6 fusion
  336.4 56.9 %all_to_all.108 = f32[8,72,1024]{2,1,0:T(8,128)} all-to-all(f32[8,72,1024]{2,1,0:T(8,128)S(1)} %broadcast_multiply_fusion), channel_id=1, replica_groups=mesh['seq'=8,'gate'=4] {'seq'}, dimensions={0} | all-to-all | bytes 4718592 | tf_op jit(solution)/shard_map/all_to_all | solution.py:40
  399.7 44.8 %slice.755 = f32[72,4095]{1,0:T(8,128)} slice(f32[72,8192]{1,0:T(8,128)S(1)} %bitcast.119), slice={[0:72:1], [2:8192:2]} | slice | bytes 2358720 | tf_op jit(solution)/shard_map/slice | solution.py:43
  444.5 44.0 %slice.664 = f32[72,4096]{1,0:T(8,128)S(1)} slice(f32[72,8192]{1,0:T(8,128)S(1)} %bitcast.120), slice={[0:72:1], [0:8191:2]} | slice | bytes 2359296 | tf_op jit(solution)/shard_map/slice | solution.py:43
  488.5 44.5 %slice.660 = f32[72,4096]{1,0:T(8,128)} slice(f32[72,8192]{1,0:T(8,128)S(1)} %bitcast.121), slice={[0:72:1], [1:8192:2]} | slice | bytes 2359296 | tf_op jit(solution)/shard_map/slice | solution.py:43
  536.4 45.6 %slice.756 = f32[72,4095]{1,0:T(8,128)} slice(f32[72,8192]{1,0:T(8,128)} %bitcast.126), slice={[0:72:1], [2:8192:2]} | slice | bytes 2358720 | tf_op jit(solution)/shard_map/slice | solution.py:43
  582.0 45.2 %slice.661 = f32[72,4096]{1,0:T(8,128)} slice(f32[72,8192]{1,0:T(8,128)} %bitcast.127), slice={[0:72:1], [1:8192:2]} | slice | bytes 2359296 | tf_op jit(solution)/shard_map/slice | solution.py:43
  627.2 45.2 %slice.659 = f32[72,4096]{1,0:T(8,128)} slice(f32[72,8192]{1,0:T(8,128)} %bitcast.128), slice={[0:72:1], [0:8191:2]} | slice | bytes 2359296 | tf_op jit(solution)/shard_map/slice | solution.py:43
  676.1 23.5 slice.669
  699.7 23.4 slice.665
  723.0 23.4 slice.666
  746.4 23.6 slice.663
  1024.3 23.3 slice.753
  1047.7 23.7 slice.752
  1194.6 24.1 pad.183
  1221.5 24.5 pad.182
  1251.9 47.8 %pad.184 = f32[72,8192]{1,0:T(8,128)} pad(f32[72,4096]{1,0:T(8,128)} %pad_maximum_fusion.1, f32[]{:T(128)} %constant.2.clone.1), padding=0_0_0x0_1_1 | pad | bytes 3538948 | tf_op jit(solution)/shard_map/pad | solution.py:43
  1299.6 48.0 %pad.185 = f32[72,8192]{1,0:T(8,128)} pad(f32[72,4096]{1,0:T(8,128)} %add.423, f32[]{:T(128)} %constant.2.clone.1), padding=0_0_0x1_0_1 | pad | bytes 3538948 | tf_op jit(solution)/shard_map/pad | solution.py:43
  1350.4 58.3 %all_to_all.109 = f32[72,8,1024]{2,0,1:T(8,128)S(1)} all-to-all(f32[72,8,1024]{2,0,1:T(8,128)S(1)} %bitcast.138), channel_id=1, replica_groups=mesh['seq'=8,'gate'=4] {'seq'}, dimensions={1} | all-to-all | bytes 4718592 | tf_op jit(solution)/shard_map/all_to_all | solution.py:46
  1418.5 16.4 slice.765
  1446.1 44.0 %slice.856 = f32[72,4095]{1,0:T(8,128)S(1)} slice(f32[72,8192]{1,0:T(8,128)S(1)} %bitcast.122), slice={[0:72:1], [1:8190:2]} | slice | bytes 2358720 | tf_op jit(solution)/shard_map/slice | solution.py:54
  1517.3 45.5 %slice.761 = f32[72,4096]{1,0:T(8,128)} slice(f32[72,8192]{1,0:T(8,128)} %mul.346), slice={[0:72:1], [0:8191:2]} | slice | bytes 2359296 | tf_op jit(solution)/shard_map/slice | solution.py:54
  1562.8 44.0 %slice.758 = f32[72,4096]{1,0:T(8,128)S(1)} slice(f32[72,8192]{1,0:T(8,128)S(1)} %copy-done.2), slice={[0:72:1], [1:8192:2]} | slice | bytes 2359296 | tf_op jit(solution)/shard_map/slice | solution.py:54
  1606.8 16.4 slice.762
  1638.2 23.4 slice.770
  1661.5 23.5 slice.766
  1685.1 22.5 slice.767
  1707.6 22.5 slice.764
  1985.0 22.5 slice.854
  2007.5 23.3 slice.853
  2031.5 44.2 %slice.858 = f32[72,4095]{1,0:T(8,128)S(1)} slice(f32[72,8192]{1,0:T(8,128)S(1)} %copy-done.2), slice={[0:72:1], [1:8190:2]} | slice | bytes 2358720 | tf_op jit(solution)/shard_map/slice | solution.py:54
  2127.2 21.6 pad.209
  2151.2 22.0 pad.208
  2187.2 44.2 %pad.269 = f32[72,8191]{1,0:T(8,128)} pad(f32[72,4096]{1,0:T(8,128)S(1)} %pad_maximum_fusion.2, f32[]{:T(128)} %constant.2.clone.1), padding=0_0_0x0_0_1 | pad | bytes 3538660 | tf_op jit(solution)/shard_map/slice | solution.py:58
  2231.5 44.1 %pad.356 = f32[72,8192]{1,0:T(8,128)} pad(f32[72,4096]{1,0:T(8,128)S(1)} %add.461, f32[]{:T(128)} %constant.2.clone.1), padding=0_0_0x1_0_1 | pad | bytes 3538948
  2278.2 22.6 reverse.10
  2303.8 57.8 %all_to_all.110 = f32[72,8,1024]{2,0,1:T(8,128)S(1)} all-to-all(f32[72,8,1024]{2,0,1:T(8,128)S(1)} %bitcast.137), channel_id=1, replica_groups=mesh['seq'=8,'gate'=4] {'seq'}, dimensions={1} | all-to-all | bytes 4718592 | tf_op jit(solution)/shard_map/all_to_all | solution.py:60
  2396.6 17.4 maximum_add_fusion
  2428.9 24.5 copy.93
  2453.3 28.1 reshape.102
  2496.7 24.1 copy.95
  2520.8 28.0 reshape.104
  2549.5 39.1 %psum.7 = f32[3,576]{1,0:T(4,128)} all-reduce(f32[3,576]{1,0:T(4,128)S(1)} %convert_reduce_fusion), channel_id=1, replica_groups=mesh['seq'=8,'gate'=4] {'seq'}, use_global_device_ids=true, to_apply=%region_4.5 | all-reduce | flops 1728 | bytes 13824 | tf_op jit(solution)/shard_map/psum | solution.py:70
  2591.6 183.7 %reduce-scatter.10.cloned.1.call-done = f32[288,1728]{1,0:T(8,128)} async-done(((f32[2304,1728]{1,0:T(8,128)}), f32[288,1728]{1,0:T(8,128)}) %reduce-scatter.10.cloned.1.call-update) | async-done | bytes 1990672
  2779.8 275.7 %reduce-scatter.12.cloned.1.call-done = f32[288,1728]{1,0:T(8,128)} async-done(((f32[2304,1728]{1,0:T(8,128)}), f32[288,1728]{1,0:T(8,128)}) %reduce-scatter.12.cloned.1.call-update) | async-done | bytes 1990672
  (401 shorter events, 901.0 us)
Async XLA Ops:
  7.2 47.5 %copy-start.32 = (s32[1024]{0:T(1024)S(1)}, s32[1024]{0:T(1024)}, u32[]{:S(2)}) copy-start(s32[1024]{0:T(1024)} %param.7) | copy-start | bytes 12292
  7.2 42.6 %all-gather.6.cloned.1.call-start = ((), (), s32[]{:S(2)}) async-start(), calls=%async_computation.10 | async-start | bytes 5898240 | tf_op jit(solution)/shard_map/all_gather | solution.py:18
  7.9 174.9 %all-gather.4.cloned.1.call-start = ((), (), s32[]{:S(2)}) async-start(), calls=%async_computation.9 | async-start | bytes 9953280 | tf_op jit(solution)/shard_map/all_gather | solution.py:24
  8.7 305.5 %all-gather.8.cloned.1.call-start = ((), (), s32[]{:S(2)}) async-start(), calls=%async_computation.11 | async-start | bytes 9953280 | tf_op jit(solution)/shard_map/all_gather | solution.py:25
  51.3 4.7 collective-permute-start
  54.7 259.4 %copy-start.33 = (pred[1024]{0:T(1024)(128)(4,1)}, pred[1024]{0:T(1024)(128)(4,1)S(1)}, u32[]{:S(2)}) copy-start(pred[1024]{0:T(1024)(128)(4,1)S(1)} %broadcast_compare_fusion) | copy-start | bytes 3076
  56.4 257.7 %copy-start.14 = (bf16[1,2304]{0,1:T(8,128)(2,1)}, bf16[1,2304]{0,1:T(8,128)(2,1)S(1)}, u32[]{:S(2)}) copy-start(bf16[1,2304]{0,1:T(8,128)(2,1)S(1)} %copy.73) | copy-start | bytes 13828
  56.4 257.7 %copy-start.35 = (f32[3,576]{1,0:T(4,128)S(1)}, f32[3,576]{1,0:T(4,128)}, u32[]{:S(2)}) copy-start(f32[3,576]{1,0:T(4,128)} %param.10) | copy-start | bytes 20740
  393.3 139.7 %all-to-all-start = ((f32[8,72,1024]{2,1,0:T(8,128)}), f32[8,72,1024]{2,1,0:T(8,128)}, u32[]{:S(2)}, u32[]{:S(2)}) async-start(f32[8,72,1024]{2,1,0:T(8,128)} %bitcast.4), calls=%async_computation | async-start | bytes 4718592 | tf_op jit(solution)/shard_map/all_to_all | solution.py:41
  1163.8 3.1 copy-start.22
  1218.7 1.7 copy-start.20
  1246.0 2.9 copy-start.4
  1246.0 2.9 copy-start.5
  1246.0 2.9 copy-start.8
  1248.9 1.6 copy-start.31
  1350.4 58.3 %copy-start.12 = (bf16[1024,576]{0,1:T(8,128)(2,1)S(1)}, bf16[1024,576]{0,1:T(8,128)(2,1)}, u32[]{:S(2)}) copy-start(bf16[1024,576]{0,1:T(8,128)(2,1)} %param.11) | copy-start | bytes 3538948
  1414.1 92.3 %all-to-all-start.3 = ((f32[8,72,1024]{2,1,0:T(8,128)}), f32[8,72,1024]{2,1,0:T(8,128)}, u32[]{:S(2)}, u32[]{:S(2)}) async-start(f32[8,72,1024]{2,1,0:T(8,128)} %bitcast.140), calls=%async_computation.3 | async-start | bytes 4718592 | tf_op jit(solution)/shard_map/all_to_all | solution.py:53
  1506.4 797.4 %all-to-all-start.5 = ((f32[72,8,1024]{2,0,1:T(8,128)}), f32[72,8,1024]{2,0,1:T(8,128)}, u32[]{:S(2)}, u32[]{:S(2)}) async-start(f32[72,8,1024]{2,0,1:T(8,128)} %bitcast.135), calls=%async_computation.5 | async-start | bytes 4718592 | tf_op jit(solution)/shard_map/all_to_all | solution.py:47
  1512.3 1076.3 %reduce-scatter.8.cloned.1.call-start = ((), (), s32[]{:S(2)}) async-start(), calls=%async_computation.12 | async-start | bytes 11796480 | tf_op jit(solution)/shard_map/reduce_scatter | solution.py:76
  1514.2 1.4 copy-start
  1517.3 45.5 %copy-start.2 = (f32[72,8192]{1,0:T(8,128)S(1)}, f32[72,8192]{1,0:T(8,128)}, u32[]{:S(2)}) copy-start(f32[72,8192]{1,0:T(8,128)} %mul.346) | copy-start | bytes 7077892
  2076.4 10.4 copy-start.24
  2076.4 10.4 copy-start.25
  2076.4 10.4 copy-start.13
  2076.4 13.1 copy-start.28
  2076.4 13.1 copy-start.29
  2076.4 13.2 copy-start.23
  2076.4 14.6 copy-start.17
  2076.4 14.6 copy-start.18
  2076.4 14.6 copy-start.27
  2080.4 20.6 copy-start.15
  2080.4 20.6 copy-start.16
  2083.9 17.2 copy-start.26
  2089.6 16.7 copy-start.10
  2089.6 16.7 copy-start.11
  2096.1 10.3 copy-start.21
  2148.8 1.4 copy-start.19
  2184.5 1.3 copy-start.7
  2184.5 1.6 copy-start.9
  2186.1 0.8 copy-start.30
  2300.7 2.5 copy-start.1
  2361.6 4.0 copy-start.6
  2376.9 3.6 copy-start.3
  2383.4 11.1 collective-permute-start.1
  2414.1 361.2 %reduce-scatter.10.cloned.1.call-start = ((), (), s32[]{:S(2)}) async-start(), calls=%async_computation.13 | async-start | bytes 18579456
  2481.4 0.7 copy-start.34
  2481.5 574.1 %reduce-scatter.12.cloned.1.call-start = ((), (), s32[]{:S(2)}) async-start(), calls=%async_computation.14 | async-start | bytes 18579456
Sparse Core Ops, SparseCore 0:
  9.6 40.1 all-gather.5
  52.0 130.8 all-gather.3
  185.1 129.0 all-gather.7
  2414.2 78.9 reduce-scatter.7
  2497.0 278.2 reduce-scatter.9
  2779.1 276.4 reduce-scatter.11
where the time goes:
time: 3090 us; the launch traced here: 3070 us
  local copies, waits for them, and re-layouts  1850 us (60%)
  waiting for transfers between devices  746 us (24%)
  blocking collectives  212 us (7%)
  other arithmetic  138 us (4%)
  matrix products  89.5 us (3%)
    slice x76, local copies, waits for them, and re-layouts, on_device(): lax.associative_scan(combine, (long_decay, long_source), axis=1)  646 us
    slice x78, local copies, waits for them, and re-layouts, on_device(): lax.associative_scan(combine, (long_decay, long_decay * long_direct), rev...  606 us
    unnamed x8, waiting for transfers between devices  462 us
    pad x24, local copies, waits for them, and re-layouts, on_device(): lax.associative_scan(combine, (long_decay, long_source), axis=1)  226 us
    unnamed x85, local copies, waits for them, and re-layouts  213 us
    all_gather x1, waiting for transfers between devices, on_device(): lax.all_gather(w_now, 'seq', axis=1, tiled=True)  126 us
    all_gather x1, waiting for transfers between devices, on_device(): lax.all_gather(w_prev, 'seq', axis=1, tiled=True)  117 us
    pad x22, local copies, waits for them, and re-layouts, on_device(): lax.associative_scan(combine, (long_decay, long_decay * long_direct), rev...  84.7 us
  transfers between devices with their start and end apart: 11, of which 6 were waited for; matrix products, arithmetic and copies ran while one was open for 38% of the time, Pallas kernels for 0%

commit v1 on v0

v1 whole, which is shorter than its diff:
```python
import jax, jax.numpy as jnp
from jax import lax
from jax.experimental import pallas as pl
from jax.experimental.pallas import tpu as pltpu
from jax.sharding import PartitionSpec as P
F32=jnp.float32; BF=jnp.bfloat16
SEGS=8; LANES=128; TM=64

def both(g):
    e=jnp.exp(-jnp.abs(g)); r=1.0/(1.0+e); er=e*r
    up=g>=0
    return jnp.where(up,r,er), jnp.where(up,er,r)

def cuts(c):
    return [(l, l*LANES, min(LANES, c-l*LANES)) for l in range(-(-c//LANES))]

def tot_kernel(g_ref, up_ref, keep_ref, seg_ref, tot_ref, d_s, s_s, q_s, seg_s):
    _,t,c=g_ref.shape
    span=t//SEGS
    lanes=cuts(c)
    def act(r,_):
        rows=pl.ds(pl.multiple_of(r*TM,TM),TM)
        for l,lo,w in lanes:
            ch=slice(lo,lo+w)
            f,i=both(g_ref[1,rows,ch])
            o,_=both(g_ref[2,rows,ch])
            d=keep_ref[rows,:w]*f
            d_s[l,rows,:w]=d
            s_s[l,rows,:w]=i*jnp.tanh(g_ref[0,rows,ch])
            q_s[l,rows,:w]=d*(up_ref[rows,ch].astype(F32)*o)
        return 0
    lax.fori_loop(0,t//TM,act,0)
    one=jnp.ones((SEGS,LANES),F32); zero=jnp.zeros((SEGS,LANES),F32)
    def step(j,carry):
        at=pl.ds(j,SEGS,stride=span); back=pl.ds(span-1-j,SEGS,stride=span)
        new=[]
        for l,_,_ in lanes:
            a,s,r=carry[l]
            d=d_s[l,at,:]
            new.append((a*d, d*s+s_s[l,at,:], d_s[l,back,:]*r+q_s[l,back,:]))
        return tuple(new)
    res=lax.fori_loop(0,span,step,tuple((one,zero,zero) for _ in lanes),unroll=4)
    for l,lo,w in lanes:
        for k in range(3):
            seg_s[k]=res[l][k]
            seg_ref[k,:,lo:lo+w]=res[l][k][:,:w]
        a=jnp.ones((1,LANES),F32); s=jnp.zeros((1,LANES),F32); r=jnp.zeros((1,LANES),F32)
        for k in range(SEGS):
            m=seg_s[0,k:k+1,:]
            s=m*s+seg_s[1,k:k+1,:]
            a=a*m
            b=SEGS-1-k
            r=seg_s[0,b:b+1,:]*r+seg_s[2,b:b+1,:]
        for k,v in enumerate((a,s,r)): tot_ref[k:k+1,lo:lo+w]=v[:,:w]

def totals(gates, up, keep):
    _,t,c=gates.shape
    lt=len(cuts(c))
    return pl.pallas_call(tot_kernel,
        out_shape=(jax.ShapeDtypeStruct((3,SEGS,c),F32),jax.ShapeDtypeStruct((3,c),F32)),
        scratch_shapes=[pltpu.VMEM((lt,t,LANES),F32)]*3+[pltpu.VMEM((3,SEGS,LANES),F32)],
        compiler_params=pltpu.CompilerParams(vmem_limit_bytes=60<<20),
        name="pool_totals")(gates,up,keep)

def fin_kernel(me_ref, g_ref, up_ref, keep_ref, seg_ref, all_ref, hid_ref, gg_ref, gb_ref, d_s, s_s, q_s, p_s, c_s):
    _,t,c=g_ref.shape
    n=all_ref.shape[0]
    span=t//SEGS
    lanes=cuts(c)
    me=me_ref[0]
    def act(r,_):
        rows=pl.ds(pl.multiple_of(r*TM,TM),TM)
        for l,lo,w in lanes:
            ch=slice(lo,lo+w)
            f,i=both(g_ref[1,rows,ch])
            o,_=both(g_ref[2,rows,ch])
            d_s[l,rows,:w]=keep_ref[rows,:w]*f
            s_s[l,rows,:w]=i*jnp.tanh(g_ref[0,rows,ch])
            q_s[l,rows,:w]=up_ref[rows,ch].astype(F32)*o
        return 0
    lax.fori_loop(0,t//TM,act,0)
    h=jnp.zeros((1,c),F32); r=jnp.zeros((1,c),F32)
    for k in range(n):
        h=jnp.where(k<me, all_ref[k,0:1,:]*h+all_ref[k,1:2,:], h)
        b=n-1-k
        r=jnp.where(b>me, all_ref[b,0:1,:]*r+all_ref[b,2:3,:], r)
    for k in range(SEGS):
        b=SEGS-1-k
        for l,lo,w in lanes:
            c_s[0,l,k:k+1,:w]=h[:,lo:lo+w]
            c_s[1,l,b:b+1,:w]=r[:,lo:lo+w]
        h=seg_ref[0,k:k+1,:]*h+seg_ref[1,k:k+1,:]
        r=seg_ref[0,b:b+1,:]*r+seg_ref[2,b:b+1,:]
    def step(j,carry):
        at=pl.ds(j,SEGS,stride=span); back=pl.ds(span-1-j,SEGS,stride=span)
        new=[]
        for l,_,_ in lanes:
            h,r=carry[l]
            dh=d_s[l,at,:]*h
            h=dh+s_s[l,at,:]
            p_s[l,at,:]=dh
            s_s[l,at,:]=h
            g=q_s[l,back,:]+r
            q_s[l,back,:]=g
            new.append((h, d_s[l,back,:]*g))
        return tuple(new)
    lax.fori_loop(0,span,step,tuple((c_s[0,l],c_s[1,l]) for l,_,_ in lanes),unroll=4)
    def out(r,acc):
        rows=pl.ds(pl.multiple_of(r*TM,TM),TM)
        new=[]
        for l,lo,w in lanes:
            ch=slice(lo,lo+w)
            f,i=both(g_ref[1,rows,ch])
            o,cl=both(g_ref[2,rows,ch])
            z=jnp.tanh(g_ref[0,rows,ch])
            gs=q_s[l,rows,:w]; oh=o*s_s[l,rows,:w]
            hid_ref[rows,ch]=oh.astype(BF)
            gi=gs*i
            for k,v in enumerate((gi*(1.0-z*z), gi*(p_s[l,rows,:w]-f*z), up_ref[rows,ch].astype(F32)*oh*cl)):
                gg_ref[k,rows,ch]=v.astype(BF)
                new.append(acc[len(new)]+jnp.sum(v.reshape(TM//8,8,w),axis=0))
        return tuple(new)
    acc=lax.fori_loop(0,t//TM,out,tuple(jnp.zeros((8,w),F32) for _,_,w in lanes for _ in range(3)))
    for l,lo,w in lanes:
        for k in range(3): gb_ref[k:k+1,lo:lo+w]=jnp.sum(acc[3*l+k],axis=0,keepdims=True)

def finish(me, gates, up, keep, seg, every):
    _,t,c=gates.shape
    lt=len(cuts(c))
    V=pl.BlockSpec(memory_space=pltpu.VMEM)
    return pl.pallas_call(fin_kernel,
        in_specs=[pl.BlockSpec(memory_space=pltpu.SMEM)]+[V]*5,
        out_shape=(jax.ShapeDtypeStruct((t,c),BF),jax.ShapeDtypeStruct((3,t,c),BF),jax.ShapeDtypeStruct((3,c),F32)),
        scratch_shapes=[pltpu.VMEM((lt,t,LANES),F32)]*4+[pltpu.VMEM((2,lt,SEGS,LANES),F32)],
        compiler_params=pltpu.CompilerParams(vmem_limit_bytes=60<<20),
        name="pool_finish")(me,gates,up,keep,seg,every)


def on_device(layer_input, keep, w_now, w_prev, bias, grad_out):
    me = lax.axis_index("seq")
    n = lax.axis_size("seq")
    x = lax.all_gather(layer_input, "gate", axis=1, tiled=True)
    ahead = [(i, i + 1) for i in range(n - 1)]
    back = [(i + 1, i) for i in range(n - 1)]
    halo = lax.ppermute(x[-1:], "seq", ahead)
    xp = jnp.concatenate([halo, x[:-1]], axis=0)
    xp = jnp.where(keep[:, None] > 0, xp, jnp.zeros_like(xp))
    wn = lax.all_gather(w_now, "seq", axis=1, tiled=True)
    wp = lax.all_gather(w_prev, "seq", axis=1, tiled=True)
    gates = jnp.einsum("td,kdc->ktc", x, wn, preferred_element_type=F32)
    gates = gates + jnp.einsum("td,kdc->ktc", xp, wp, preferred_element_type=F32)
    gates = gates + bias[:, None, :]
    keep_f = keep.astype(F32)
    keep_w = jnp.broadcast_to(keep_f[:, None], (keep.shape[0], LANES))
    seg, tot = totals(gates, grad_out, keep_w)
    every = lax.all_gather(tot, "seq", axis=0)
    hidden, g, gb = finish(me[None].astype(jnp.int32), gates, grad_out, keep_w, seg, every)
    kb = keep.astype(BF)
    follow = lax.ppermute(g[:, :1] * kb[0], "seq", back)
    gs = jnp.concatenate([g[:, 1:] * kb[None, 1:, None], follow], axis=1)
    part_now = jnp.einsum("td,ktc->kdc", x, g, preferred_element_type=F32).astype(BF)
    grad_now = lax.psum_scatter(part_now, "seq", scatter_dimension=1, tiled=True).astype(F32)
    part_prev = jnp.einsum("td,ktc->kdc", x, gs, preferred_element_type=F32).astype(BF)
    grad_prev = lax.psum_scatter(part_prev, "seq", scatter_dimension=1, tiled=True).astype(F32)
    grad_bias = lax.psum(gb, "seq")
    dx = jnp.einsum("ktc,kdc->td", g, wn, preferred_element_type=F32)
    dx = dx + jnp.einsum("ktc,kdc->td", gs, wp, preferred_element_type=F32)
    grad_x = lax.psum_scatter(dx.astype(BF), "gate", scatter_dimension=1, tiled=True)
    return hidden, grad_x, grad_now, grad_prev, grad_bias


def solution(mesh):
    return jax.shard_map(
        on_device,
        mesh=mesh,
        in_specs=(P("seq", "gate"), P("seq"), P(None, "seq", "gate"), P(None, "seq", "gate"), P(None, "gate"), P("seq", "gate")),
        out_specs=(P("seq", "gate"), P("seq", "gate"), P(None, "seq", "gate"), P(None, "seq", "gate"), P(None, "gate")),
        check_vma=False,
    )
```

time: 3090 us -> 816 us (0.26)
  local copies, waits for them, and re-layouts: 1850 us -> 108 us
  waiting for transfers between devices: 746 us -> 480 us
  blocking collectives: 212 us -> 70.6 us
  other arithmetic: 138 us -> 5.85 us
  Pallas kernels: 0 us -> 37.5 us
    slice x160 -> x4, local copies, waits for them, and re-layouts: 1310 us -> 2.12 us  [the longest x2 1.54 us: on_device(): halo = lax.ppermute(x[-1:], 'seq', ahead)]
    pad x46 -> x0, local copies, waits for them, and re-layouts: 311 us -> none  [the longest x24 226 us: on_device(): lax.associative_scan(combine, (long_decay, long_source), axis=1)]
    unnamed x8, waiting for transfers between devices: 462 us -> 156 us
    all_to_all x3 -> x0, blocking collectives: 173 us -> none  [the longest x1 58.3 us: on_device(): lax.all_to_all(long_state, 'seq', split_axis=1, concat_axis=0, tiled=True)]
    unnamed x85 -> x26, local copies, waits for them, and re-layouts: 213 us -> 104 us
    add x54 -> x0, other arithmetic: 49.7 us -> none  [the longest x14 24.4 us: on_device(): lax.associative_scan(combine, (long_decay, long_source), axis=1)]
    reduce_scatter x1, waiting for transfers between devices: 0.01 us -> 43 us  [on_device(): lax.psum_scatter(dx.astype(BF), 'gate', scatter_dimension=1, tiled=True)]
    mul x24 -> x2, other arithmetic: 43.7 us -> 5.08 us  [the longest x1 3.67 us: on_device(): gs = jnp.concatenate([g[:, 1:] * kb[None, 1:, None], follow], axis=1)]
  transfers between devices with their start and end apart: 11 -> 8, of which waited for: 6 -> 7; matrix products, arithmetic and copies ran while one was open for 38% -> 16% of each run, Pallas kernels for 0% -> 0%
where the time goes in v1:
time: 816 us; the launch traced here: 813 us
  waiting for transfers between devices  480 us (59%)
  local copies, waits for them, and re-layouts  108 us (13%)
  matrix products  92.1 us (11%)
  blocking collectives  70.6 us (9%)
  Pallas kernels  37.5 us (5%)
  between operations  14.3 us (2%)
    unnamed x8, waiting for transfers between devices  156 us
    all_gather x1, waiting for transfers between devices, on_device(): wn = lax.all_gather(w_now, 'seq', axis=1, tiled=True)  126 us
    all_gather x1, waiting for transfers between devices, on_device(): wp = lax.all_gather(w_prev, 'seq', axis=1, tiled=True)  115 us
    unnamed x26, local copies, waits for them, and re-layouts  104 us
    reduce_scatter x1, waiting for transfers between devices, on_device(): lax.psum_scatter(dx.astype(BF), 'gate', scatter_dimension=1, tiled=True)  43 us
    all_gather x1, waiting for transfers between devices, on_device(): x = lax.all_gather(layer_input, 'gate', axis=1, tiled=True)  39.6 us
    psum x1, blocking collectives, on_device(): grad_bias = lax.psum(gb, 'seq')  37.7 us
    all_gather x1, blocking collectives, on_device(): every = lax.all_gather(tot, 'seq', axis=0)  32.9 us
  transfers between devices with their start and end apart: 8, of which 7 were waited for; matrix products, arithmetic and copies ran while one was open for 16% of the time, Pallas kernels for 0%

profile of v1, /device:TPU:0, one launch (start us, length us, event | category | flops | bytes accessed | tf_op | source)
XLA Modules:
  0.0 813.3 jit_solution(8877244899339609500)
XLA Ops:
  7.2 0.7 all-gather.8.cloned.1.call-update
  8.0 0.7 all-gather.6.cloned.1.call-update
  8.7 0.7 all-gather.10.cloned.1.call-update
  9.4 0.0 reduce-scatter.10.cloned.1.call-start
  9.5 0.8 fusion.19
  10.2 39.6 %all-gather.8.cloned.1.call-done = bf16[1024,2304]{0,1:T(8,128)(2,1)} async-done(((bf16[1024,576]{0,1:T(8,128)(2,1)}), bf16[1024,2304]{0,1:T(8,128)(2,1)}) %all-gather.8.cloned.1.call-update) | async-done | bytes 4718608 | tf_op jit(solution)/shard_map/all_gather | solution.py:142
  49.8 1.3 slice.24
  51.1 0.3 copy.24
  51.3 3.4 collective-permute-start
  54.7 1.4 copy.29.up_ref
  56.2 0.4 copy.25
  56.6 126.3 %all-gather.6.cloned.1.call-done = bf16[3,2304,576]{2,1,0:T(8,128)(2,1)} async-done(((bf16[3,288,576]{2,1,0:T(8,128)(2,1)}), bf16[3,2304,576]{2,1,0:T(8,128)(2,1)}) %all-gather.6.cloned.1.call-update) | async-done | bytes 7962640 | tf_op jit(solution)/shard_map/all_gather | solution.py:148
  182.9 16.4 %fusion.9 = f32[3,576,1024]{1,2,0:T(8,128)} fusion(bf16[3,2304,576]{2,1,0:T(8,128)(2,1)} %all-gather.6.cloned.1.call-done, bf16[1024,2304]{0,1:T(8,128)(2,1)} %all-gather.8.cloned.1.call-done), kind=kOutput, calls=%fused_computation.13 | convolution fusion | flops 8153726976 | bytes 19759104 | tf_op jit(solution)/shard_map/td,kdc->ktc/dot_general | solution.py:150
  199.2 114.9 %all-gather.10.cloned.1.call-done = bf16[3,2304,576]{2,1,0:T(8,128)(2,1)} async-done(((bf16[3,288,576]{2,1,0:T(8,128)(2,1)}), bf16[3,2304,576]{2,1,0:T(8,128)(2,1)}) %all-gather.10.cloned.1.call-update) | async-done | bytes 7962640 | tf_op jit(solution)/shard_map/all_gather | solution.py:149
  314.1 17.9 %fusion.1.g_ref = f32[3,1024,576]{2,1,0:T(8,128)} fusion(f32[3,576,1024]{1,2,0:T(8,128)} %fusion.9, f32[3,576]{1,0:T(4,128)S(1)} %copy-done.6, bf16[3,2304,576]{2,1,0:T(8,128)(2,1)} %all-gather.10.cloned.1.call-done, bf16[1023,2304]{0,1:T(8,128)(2,1)} %bitcast.48, bf16[1,2304]{0,1:T(8,128)(2,1)S(1)} %copy.25, pred[1024]{0:T(1024)(128)(4,1)S(1)} %broadcast_compare_fusion), kind=kOutput, calls=%fused_computation.5 | convolution fusion | flops 8169062400 | bytes 26844928 | tf_op jit(solution)/shard_map/td,kdc->ktc/dot_general | solution.py:151
  332.0 1.0 broadcast_in_dim.26.keep_ref
  333.0 13.8 %pool_totals.1 = (f32[3,8,576]{2,1,0:T(8,128)}, f32[3,576]{1,0:T(4,128)}) custom-call(f32[3,1024,576]{2,1,0:T(8,128)} %fusion.1.g_ref, bf16[1024,576]{1,0:T(8,128)(2,1)} %copy.29.up_ref, f32[1024,128]{1,0:T(8,128)} %broadcast_in_dim.26.keep_ref), custom_call_target="tpu_custom_call" | custom-call | tf_op jit(solution)/shard_map/pool_totals/pallas_call | solution.py:59
  346.8 32.9 %all-gather.1.all_ref = f32[8,3,576]{2,1,0:T(4,128)} all-gather(f32[1,3,576]{2,1,0:T(4,128)} %bitcast.49), channel_id=2, replica_groups=mesh['seq'=8,'gate'=4] {'seq'}, dimensions={0}, use_global_device_ids=true | all-gather | bytes 62208 | tf_op jit(solution)/shard_map/all_gather | solution.py:156
  379.7 23.7 %pool_finish.1 = (bf16[1024,576]{1,0:T(8,128)(2,1)}, bf16[3,1024,576]{2,1,0:T(8,128)(2,1)}, f32[3,576]{1,0:T(4,128)}) custom-call(s32[1]{0:T(128)} %bitcast.me_ref, f32[3,1024,576]{2,1,0:T(8,128)} %fusion.1.g_ref, bf16[1024,576]{1,0:T(8,128)(2,1)} %copy.29.up_ref, f32[1024,128]{1,0:T(8,128)} %broadcast_in_dim.26.keep_ref, ...), custom_call_target="tpu_custom_call" | custom-call | tf_op jit(solution)/shard_map/pool_finish/pallas_call | solution.py:131
  403.4 15.5 %convert_bitcast_fusion.1 = bf16[3,2304,576]{1,2,0:T(8,128)(2,1)} fusion(bf16[3,1024,576]{2,1,0:T(8,128)(2,1)} %get-tuple-element.13, bf16[1024,2304]{0,1:T(8,128)(2,1)} %all-gather.8.cloned.1.call-done), kind=kOutput, calls=%fused_computation.3 | convolution fusion | flops 8157708288 | bytes 16220160 | tf_op jit(solution)/shard_map/td,ktc->kdc/dot_general | solution.py:161
  418.9 19.5 %copy.45 = bf16[3,2304,576]{2,0,1:T(4,128)(2,1)} copy(bf16[3,2304,576]{1,2,0:T(8,128)(2,1)} %convert_bitcast_fusion.1) | data formatting | bytes 15925248
  438.4 23.1 %reshape.23 = bf16[2304,1728]{1,0:T(8,128)(2,1)} reshape(bf16[2304,3,576]{2,1,0:T(4,128)(2,1)} %bitcast.44) | data formatting | bytes 15925248
  461.5 0.0 reduce-scatter.12.cloned.1.call-start
  461.6 0.5 slice.23
  462.1 0.1 slice.21
  462.1 1.4 slice_multiply_fusion.1
  463.6 1.3 collective-permute-start.1
  464.8 3.7 slice_multiply_fusion
  468.5 0.6 collective-permute-done.1
  469.1 1.3 copy-done
  470.4 14.0 %convert_bitcast_fusion = bf16[3,2304,576]{1,2,0:T(8,128)(2,1)} fusion(bf16[1024,2304]{0,1:T(8,128)(2,1)} %all-gather.8.cloned.1.call-done, bf16[3,1,576]{2,1,0:T(2,128)(2,1)S(1)} %collective-permute-done.1, bf16[3,1023,576]{2,1,0:T(8,128)(2,1)S(1)} %slice_multiply_fusion), kind=kOutput, calls=%fused_computation.2 | convolution fusion | flops 8164786176 | bytes 16220160 | tf_op jit(solution)/shard_map/td,ktc->kdc/dot_general | solution.py:163
  484.4 19.6 %copy.47 = bf16[3,2304,576]{2,0,1:T(4,128)(2,1)} copy(bf16[3,2304,576]{1,2,0:T(8,128)(2,1)} %convert_bitcast_fusion) | data formatting | bytes 15925248
  504.0 23.1 %reshape.25 = bf16[2304,1728]{1,0:T(8,128)(2,1)} reshape(bf16[2304,3,576]{2,1,0:T(4,128)(2,1)} %bitcast.45) | data formatting | bytes 15925248
  527.1 0.3 reduce-scatter.8.cloned.1.call-start
  527.4 14.0 %fusion.20 = f32[1024,2304,1]{0,1,2:T(8,128)S(1)} fusion(bf16[3,1024,576]{2,1,0:T(8,128)(2,1)} %get-tuple-element.13, bf16[3,2304,576]{2,1,0:T(8,128)(2,1)} %all-gather.6.cloned.1.call-done), kind=kOutput, calls=%fused_computation.26 | convolution fusion | flops 8153726976 | bytes 20938752 | tf_op jit(solution)/shard_map/ktc,kdc->td/dot_general | solution.py:166
  541.4 14.3 %fusion = bf16[1024,2304]{0,1:T(8,128)(2,1)} fusion(f32[1024,2304,1]{0,1,2:T(8,128)S(1)} %fusion.20, bf16[3,2304,576]{2,1,0:T(8,128)(2,1)} %all-gather.10.cloned.1.call-done, bf16[3,1,576]{2,1,0:T(2,128)(2,1)S(1)} %collective-permute-done.1, bf16[3,1023,576]{2,1,0:T(8,128)(2,1)S(1)} %copy-done.1), kind=kOutput, calls=%fused_computation.1 | convolution fusion | flops 8165523456 | bytes 25657344 | tf_op jit(solution)/shard_map/ktc,kdc->td/dot_general | solution.py:167
  555.7 1.3 copy-done.2
  557.0 1.4 copy.34
  558.5 37.7 %psum.7 = f32[3,576]{1,0:T(4,128)} all-reduce(f32[3,576]{1,0:T(4,128)S(1)} %copy-done.5), channel_id=1, replica_groups=mesh['seq'=8,'gate'=4] {'seq'}, use_global_device_ids=true, to_apply=%region_3.4 | all-reduce | flops 1728 | bytes 13824 | tf_op jit(solution)/shard_map/psum | solution.py:165
  596.2 10.9 %reduce-scatter.10.cloned.1.call-done = bf16[288,1728]{1,0:T(8,128)(2,1)} async-done(((bf16[2304,1728]{1,0:T(8,128)(2,1)}), bf16[288,1728]{1,0:T(8,128)(2,1)}) %reduce-scatter.10.cloned.1.call-update) | async-done | bytes 995344
  607.1 3.0 reshape.24
  610.1 1.9 copy.46
  611.9 1.9 copy.35
  613.9 142.8 %reduce-scatter.12.cloned.1.call-done = bf16[288,1728]{1,0:T(8,128)(2,1)} async-done(((bf16[2304,1728]{1,0:T(8,128)(2,1)}), bf16[288,1728]{1,0:T(8,128)(2,1)}) %reduce-scatter.12.cloned.1.call-update) | async-done | bytes 995344
  756.6 3.0 reshape.26
  759.6 1.9 copy.48
  761.5 1.9 copy.36
  763.4 43.0 %reduce-scatter.8.cloned.1.call-done = bf16[1024,576]{0,1:T(8,128)(2,1)} async-done(((bf16[1024,2304]{0,1:T(8,128)(2,1)}), bf16[1024,576]{0,1:T(8,128)(2,1)}) %reduce-scatter.8.cloned.1.call-update) | async-done | bytes 1179664 | tf_op jit(solution)/shard_map/reduce_scatter | solution.py:168
  (20 shorter events, 0.2 us)
Async XLA Ops:
  7.2 47.5 %copy-start.4 = (s32[1024]{0:T(1024)S(1)}, s32[1024]{0:T(1024)}, u32[]{:S(2)}) copy-start(s32[1024]{0:T(1024)} %param.7) | copy-start | bytes 12292
  7.2 47.5 %copy-start.3 = (bf16[1024,576]{0,1:T(8,128)(2,1)S(1)}, bf16[1024,576]{0,1:T(8,128)(2,1)}, u32[]{:S(2)}) copy-start(bf16[1024,576]{0,1:T(8,128)(2,1)} %param.11) | copy-start | bytes 3538948
  7.2 42.6 %all-gather.8.cloned.1.call-start = ((), (), s32[]{:S(2)}) async-start(), calls=%async_computation.4 | async-start | bytes 5898240 | tf_op jit(solution)/shard_map/all_gather | solution.py:142
  7.9 174.9 %all-gather.6.cloned.1.call-start = ((), (), s32[]{:S(2)}) async-start(), calls=%async_computation.3 | async-start | bytes 9953280 | tf_op jit(solution)/shard_map/all_gather | solution.py:148
  8.7 305.5 %all-gather.10.cloned.1.call-start = ((), (), s32[]{:S(2)}) async-start(), calls=%async_computation.5 | async-start | bytes 9953280 | tf_op jit(solution)/shard_map/all_gather | solution.py:149
  9.4 597.7 %reduce-scatter.10.cloned.1.call-start = ((), (), s32[]{:S(2)}) async-start(), calls=%async_computation.7 | async-start | bytes 9289728
  51.3 4.9 collective-permute-start
  56.5 257.6 %copy-start.6 = (f32[3,576]{1,0:T(4,128)S(1)}, f32[3,576]{1,0:T(4,128)}, u32[]{:S(2)}) copy-start(f32[3,576]{1,0:T(4,128)} %param.10) | copy-start | bytes 20740
  461.5 295.1 %reduce-scatter.12.cloned.1.call-start = ((), (), s32[]{:S(2)}) async-start(), calls=%async_computation.8 | async-start | bytes 9289728
  463.6 5.5 collective-permute-start.1
  468.5 1.9 copy-start
  527.1 279.3 %reduce-scatter.8.cloned.1.call-start = ((), (), s32[]{:S(2)}) async-start(), calls=%async_computation.6 | async-start | bytes 5898240 | tf_op jit(solution)/shard_map/reduce_scatter | solution.py:168
  527.4 14.0 %copy-start.1 = (bf16[3,1023,576]{2,1,0:T(8,128)(2,1)S(1)}, bf16[3,1023,576]{2,1,0:T(8,128)(2,1)}, u32[]{:S(2)}) copy-start(bf16[3,1023,576]{2,1,0:T(8,128)(2,1)} %copy-done) | copy-start | bytes 10606468
  555.7 1.3 copy-start.2
  555.7 2.7 copy-start.5
Sparse Core Ops, SparseCore 0:
  9.6 40.1 all-gather.7
  52.0 130.8 all-gather.5
  185.1 129.0 all-gather.9
  461.6 145.4 reduce-scatter.9
  610.6 145.9 reduce-scatter.11
  759.6 46.8 reduce-scatter.7

commit v2 on v0

v2 whole, which is shorter than its diff:
```python
import functools

import jax
import jax.numpy as jnp
from jax import lax
from jax.experimental import pallas as pl
from jax.experimental.pallas import tpu as pltpu
from jax.sharding import PartitionSpec as P

F32 = jnp.float32
BF = jnp.bfloat16
SEGS = 8
LANES = 128
TM = 64
ROWS = 256
EDGE = 16
VMEM = 62 << 20
WIDTHS = (128, 160)


def ceil_to(value, unit):
    return -(-value // unit) * unit


def both(g):
    e = jnp.exp(-jnp.abs(g))
    r = 1.0 / (1.0 + e)
    er = e * r
    pos = g >= 0
    return jnp.where(pos, r, er), jnp.where(pos, er, r)


def load_up(ref, rows, lo, w):
    return ref[rows, lo : lo + w].astype(F32)


def cuts(c):
    return [(i, i * LANES, min(LANES, c - i * LANES)) for i in range(-(-c // LANES))]


def params():
    return pltpu.CompilerParams(vmem_limit_bytes=VMEM)


URGENT, LATER = 100, 50
TINY = pl.CostEstimate(flops=1 << 10, bytes_accessed=1 << 10, transcendentals=0)
SMEM_SPEC = pl.BlockSpec(memory_space=pltpu.SMEM)
VMEM_SPEC = pl.BlockSpec(memory_space=pltpu.VMEM)
ANY_SPEC = pl.BlockSpec(memory_space=pl.ANY)


def offsets(widths):
    at = 0
    for w in widths:
        yield at, w
        at += w


def pack_w_kernel(widths, share, place, now_ref, prev_ref, *outs):
    half = now_ref.shape[2] // 2
    low = place[1] == 0
    for tap, ref in enumerate((now_ref, prev_ref)):
        for k in range(3):
            v = ref[k].astype(F32)
            mine = jnp.where(low, v[:, :half], v[:, half:])
            other = jnp.where(low, v[:, half:], v[:, :half])
            at, w = list(offsets(widths))[share]
            lo = (tap * 3 + k) * w
            outs[0][:, lo : lo + w] = mine[:, at : at + w].astype(BF)
            outs[1][:, lo : lo + w] = other[:, at : at + w].astype(BF)


def pack_weights(widths, share, place, w_now, w_prev):
    rows, w = w_now.shape[1], widths[share]
    return pl.pallas_call(
        functools.partial(pack_w_kernel, widths, share),
        in_specs=[SMEM_SPEC, VMEM_SPEC, VMEM_SPEC],
        out_shape=[jax.ShapeDtypeStruct((rows, 6 * w), BF)] * 2,
        compiler_params=params(),
        cost_estimate=TINY,
        name="pack_weights",
    )(place, w_now, w_prev)


def pack_up_kernel(widths, place, up_ref, *outs):
    half = up_ref.shape[1] // 2
    low = place[1] == 0

    def body(r, _):
        rows = pl.ds(pl.multiple_of(r * TM, TM), TM)
        v = up_ref[rows, :].astype(F32)
        mine = jnp.where(low, v[:, :half], v[:, half:])
        other = jnp.where(low, v[:, half:], v[:, :half])
        for i, (at, w) in enumerate(offsets(widths)):
            outs[2 * i][rows, :] = mine[:, at : at + w].astype(BF)
            outs[2 * i + 1][rows, :w] = other[:, at : at + w].astype(BF)
        return 0

    lax.fori_loop(0, up_ref.shape[0] // TM, body, 0)


def pack_up(widths, place, grad_out):
    t = grad_out.shape[0]
    return pl.pallas_call(
        functools.partial(pack_up_kernel, widths),
        in_specs=[SMEM_SPEC, VMEM_SPEC],
        out_shape=[jax.ShapeDtypeStruct((t, w), BF) for v in widths for w in (v, ceil_to(v, LANES))],
        compiler_params=params(),
        cost_estimate=TINY,
        name="pack_up",
    )(place, grad_out)


def gates_kernel(plan, place, *refs):
    n, m, dw, dl, t, c, up_at, wrel, xrel = plan
    n_w, n_x = len(wrel) or 1, len(xrel) or 1
    w_in, refs = refs[:n_w], refs[n_w:]
    x_in, refs = refs[:n_x], refs[n_x:]
    if not xrel:
        halo_in, refs = refs[0], refs[1:]
    bias_ref, up0, up1 = refs[:3]
    refs = refs[3:]
    if not xrel:
        keep_w, refs = refs[0], refs[1:]
    g_ref, seg_ref, tot_ref, refs = refs[0], refs[1], refs[2], refs[3:]
    if xrel:
        x_out, halo_out, keep_w, refs = refs[0], refs[1], refs[2], refs[3:]
    w_out, refs = refs[0], refs[1:]
    xs, halo, ws, p_s, d_s, s_s, q_s, seg_s, xsem, hsem, wsem, osem = refs
    pad = ws.shape[1]
    width = ws.shape[2]
    wide = n // m
    h, l, p, a, b = (place[i] for i in range(5))
    heads = n // 4
    copies = []
    if wrel:
        for i, (kh, d_p) in enumerate(wrel):
            for d_l in range(2):
                block = (lax.rem(h - kh + heads, heads) * 2 + (l ^ d_l)) * 2 + (p ^ d_p)
                at = pl.multiple_of(lax.rem(block, wide) * dw, 16)
                copies.append(
                    pltpu.make_async_copy(
                        w_in[i].at[d_l], ws.at[block // wide, pl.ds(at, dw), :], wsem.at[2 * i + d_l]
                    )
                )
        if pad > dl:
            for g in range(m):
                ws[g, dl:, :] = jnp.zeros((pad - dl, width), BF)
    else:
        copies.append(pltpu.make_async_copy(w_in[0], ws, wsem.at[0]))
    xcopies = [[], []]
    if xrel:
        for i, (slot, d_a, d_b) in enumerate(xrel):
            at = pl.multiple_of(((a ^ d_a) * 2 + (b ^ d_b)) * pad, LANES)
            xcopies[slot].append(
                pltpu.make_async_copy(
                    x_in[i].at[pl.ds(0, t)], xs.at[pl.ds(slot * t, t), pl.ds(at, pad)], xsem.at[i]
                )
            )
            copies.append(
                pltpu.make_async_copy(
                    x_in[i].at[pl.ds(t, EDGE)], halo.at[pl.ds(slot * EDGE, EDGE), pl.ds(at, pad)], hsem.at[i]
                )
            )
    else:
        for slot in range(2):
            rows = pl.ds(slot * t, t)
            xcopies[slot].append(pltpu.make_async_copy(x_in[0].at[rows], xs.at[rows], xsem.at[slot]))
        copies.append(pltpu.make_async_copy(halo_in, halo, hsem.at[0]))
    for copy in copies + xcopies[0] + xcopies[1]:
        copy.start()
    for copy in copies:
        copy.wait()
    outs = []
    for g in range(m):
        outs.append(pltpu.make_async_copy(ws.at[g], w_out.at[(a * 2 + b) ^ g], osem.at[g]))
    for copy in outs:
        copy.start()
    lanes = cuts(c)
    weights = ws[...].reshape(m * pad, width)
    if xrel:
        out = pltpu.make_async_copy(halo, halo_out, osem.at[m + 2])
        out.start()
        outs.append(out)
    edge = jnp.dot(halo[...], weights, preferred_element_type=F32)
    for slot, up_ref in enumerate((up0, up1)):
        for copy in xcopies[slot]:
            copy.wait()
        if xrel:
            rows = pl.ds(slot * t, t)
            out = pltpu.make_async_copy(xs.at[rows], x_out.at[rows], osem.at[m + slot])
            out.start()
            outs.append(out)
        p_s[7:8, :] = edge[slot * EDGE : slot * EDGE + 1, :]

        def tile(i, _, slot=slot, up_ref=up_ref):
            base = pl.multiple_of(i * ROWS, ROWS)
            x = xs[pl.ds(pl.multiple_of(slot * t + base, ROWS), ROWS), :]
            p_s[8:, :] = jnp.dot(x, ws[...].reshape(m * pad, width), preferred_element_type=F32)
            for r in range(ROWS // TM):
                rows = pl.ds(pl.multiple_of(base + r * TM, TM), TM)
                full = pl.ds(pl.multiple_of(slot * t + base + r * TM, TM), TM)
                if xrel:
                    flags = xs[full, dl:pad].astype(F32)
                    keep = jnp.concatenate([flags] * (LANES // (pad - dl)), axis=1)
                    keep_w[full, :] = keep
                else:
                    keep = keep_w[full, :]
                for k_l, lo, w in lanes:
                    g = []
                    for k in range(3):
                        now = p_s[8 + r * TM : 8 + (r + 1) * TM, k * c + lo : k * c + lo + w]
                        before = p_s[7 + r * TM : 7 + (r + 1) * TM, (3 + k) * c + lo : (3 + k) * c + lo + w]
                        v = now + keep[:, :w] * before + bias_ref[k : k + 1, lo : lo + w]
                        g_ref[k, full, lo : lo + w] = v
                        g.append(v)
                    f, intake = both(g[1])
                    o, _ = both(g[2])
                    d = keep[:, :w] * f
                    d_s[slot, k_l, rows, :w] = d
                    s_s[slot, k_l, rows, :w] = intake * jnp.tanh(g[0])
                    q_s[slot, k_l, rows, :w] = d * (load_up(up_ref, rows, slot * up_at + lo, w) * o)
            p_s[7:8, :] = p_s[ROWS + 7 : ROWS + 8, :]
            return 0

        lax.fori_loop(0, t // ROWS, tile, 0)
    span = t // SEGS
    chains = [(slot, k_l) for slot in range(2) for k_l, _, _ in lanes]
    one, zero = jnp.ones((SEGS, LANES), F32), jnp.zeros((SEGS, LANES), F32)

    def step(j, carry):
        at, back = pl.ds(j, SEGS, stride=span), pl.ds(span - 1 - j, SEGS, stride=span)
        new = []
        for (slot, k_l), (pa, ps, pr) in zip(chains, carry):
            d = d_s[slot, k_l, at, :]
            new.append(
                (
                    pa * d,
                    d * ps + s_s[slot, k_l, at, :],
                    d_s[slot, k_l, back, :] * pr + q_s[slot, k_l, back, :],
                )
            )
        return tuple(new)

    res = lax.fori_loop(0, span, step, tuple((one, zero, zero) for _ in chains), unroll=4)
    for (slot, k_l), triple in zip(chains, res):
        _, lo, w = lanes[k_l]
        for k in range(3):
            seg_s[k] = triple[k]
            seg_ref[slot, k, :, lo : lo + w] = triple[k][:, :w]
        pa, ps, pr = one[:1], zero[:1], zero[:1]
        for k in range(SEGS):
            d = seg_s[0, k : k + 1, :]
            ps = d * ps + seg_s[1, k : k + 1, :]
            pa = pa * d
            r = SEGS - 1 - k
            pr = seg_s[0, r : r + 1, :] * pr + seg_s[2, r : r + 1, :]
        for k, v in enumerate((pa, ps, pr)):
            tot_ref[slot, k : k + 1, lo : lo + w] = v[:, :w]
    for copy in outs:
        copy.wait()


def after(v, *needs):
    return lax.optimization_barrier((v, *needs))[0]


def gates_and_totals(dims, up_at, place, w, wrel, x, xrel, bias, ups, keep_w=None):
    n, m, dw, dl, t, c = dims
    pad = ceil_to(dl, LANES)
    lt = len(cuts(c))
    width = 6 * c
    plan = (n, m, dw, dl, t, c, up_at, tuple(wrel), tuple(xrel))
    shape = jax.ShapeDtypeStruct
    outs = [shape((3, 2 * t, c), F32), shape((2, 3, SEGS, c), F32), shape((2, 3, c), F32)]
    specs = [VMEM_SPEC] * 3
    if xrel:
        outs += [shape((2 * t, m * pad), BF), shape((2 * EDGE, m * pad), BF), shape((2 * t, LANES), F32)]
        specs += [ANY_SPEC, ANY_SPEC, VMEM_SPEC]
    outs.append(shape((m, pad, width), BF))
    specs.append(ANY_SPEC)
    return pl.pallas_call(
        functools.partial(gates_kernel, plan),
        in_specs=[SMEM_SPEC] + [ANY_SPEC] * (len(w) + len(x)) + [VMEM_SPEC] * (3 if xrel else 4),
        out_specs=specs,
        out_shape=outs,
        scratch_shapes=[
            pltpu.VMEM((2 * t, m * pad), BF),
            pltpu.VMEM((2 * EDGE, m * pad), BF),
            pltpu.VMEM((m, pad, width), BF),
            pltpu.VMEM((ROWS + 8, width), F32),
            pltpu.VMEM((2, lt, t, LANES), F32),
            pltpu.VMEM((2, lt, t, LANES), F32),
            pltpu.VMEM((2, lt, t, LANES), F32),
            pltpu.VMEM((3, SEGS, LANES), F32),
            pltpu.SemaphoreType.DMA((max(2, len(x)),)),
            pltpu.SemaphoreType.DMA((max(1, len(x)),)),
            pltpu.SemaphoreType.DMA((2 * len(w),)),
            pltpu.SemaphoreType.DMA((m + 3,)),
        ],
        compiler_params=params(),
        cost_estimate=TINY,
        name="gates_and_totals",
    )(place, *w, *x, bias, *ups, *([] if xrel else [keep_w]))


def finish_kernel(n, up_at, place, g_ref, up0, up1, keep_ref, seg_ref, all_ref, h0, h1, gg_ref, gf_ref, gp_ref, gb_ref, d_s, s_s, q_s, p_s, c_s):
    t, c = up0.shape
    span = t // SEGS
    lanes = cuts(c)
    heads = n // 4
    hh, ll, pp = place[0], place[1], place[2]
    ups, hids = (up0, up1), (h0, h1)
    for slot in range(2):

        def act(r, _, slot=slot):
            rows = pl.ds(pl.multiple_of(r * TM, TM), TM)
            full = pl.ds(pl.multiple_of(slot * t + r * TM, TM), TM)
            for k_l, lo, w in lanes:
                ch = slice(lo, lo + w)
                f, i = both(g_ref[1, full, ch])
                o, _ = both(g_ref[2, full, ch])
                d_s[slot, k_l, rows, :w] = keep_ref[full, :w] * f
                s_s[slot, k_l, rows, :w] = i * jnp.tanh(g_ref[0, full, ch])
                q_s[slot, k_l, rows, :w] = load_up(ups[slot], rows, slot * up_at + lo, w) * o
            return 0

        lax.fori_loop(0, t // TM, act, 0)
    zrow = jnp.zeros((1, c), F32)
    mine = [(hh * 2 + (ll ^ slot)) * 2 + pp for slot in range(2)]

    def total(block, k):
        p_b, l_b, h_b = block % 2, block // 2 % 2, block // 4
        member = lax.rem(hh - h_b + heads, heads) * 2 + (pp ^ p_b)
        return all_ref[member, ll ^ l_b, k : k + 1, :]

    h, r = zrow, zrow
    h_in, r_in = [zrow, zrow], [zrow, zrow]
    for k in range(n):
        b = n - 1 - k
        h_in = [jnp.where(mine[s] == k, h, h_in[s]) for s in range(2)]
        r_in = [jnp.where(mine[s] == b, r, r_in[s]) for s in range(2)]
        h = total(k, 0) * h + total(k, 1)
        r = total(b, 0) * r + total(b, 2)
    for slot in range(2):
        h, r = h_in[slot], r_in[slot]
        for k in range(SEGS):
            b = SEGS - 1 - k
            for k_l, lo, w in lanes:
                c_s[0, slot, k_l, k : k + 1, :w] = h[:, lo : lo + w]
                c_s[1, slot, k_l, b : b + 1, :w] = r[:, lo : lo + w]
            h = seg_ref[slot, 0, k : k + 1, :] * h + seg_ref[slot, 1, k : k + 1, :]
            r = seg_ref[slot, 0, b : b + 1, :] * r + seg_ref[slot, 2, b : b + 1, :]
    chains = [(slot, k_l) for slot in range(2) for k_l, _, _ in lanes]

    def step(j, carry):
        at, back = pl.ds(j, SEGS, stride=span), pl.ds(span - 1 - j, SEGS, stride=span)
        new = []
        for (slot, k_l), (h, r) in zip(chains, carry):
            dh = d_s[slot, k_l, at, :] * h
            h = dh + s_s[slot, k_l, at, :]
            p_s[slot, k_l, at, :] = dh
            s_s[slot, k_l, at, :] = h
            g = q_s[slot, k_l, back, :] + r
            q_s[slot, k_l, back, :] = g
            new.append((h, d_s[slot, k_l, back, :] * g))
        return tuple(new)

    lax.fori_loop(0, span, step, tuple((c_s[0, s, k_l], c_s[1, s, k_l]) for s, k_l in chains), unroll=4)
    sums = [jnp.zeros((8, w), F32) for _, _, w in lanes for _ in range(3)]
    top = lax.broadcasted_iota(jnp.int32, (EDGE, LANES), 0) == 0
    gp_ref[...] = jnp.zeros(gp_ref.shape, BF)
    for slot in range(2):

        def out(i, state, slot=slot):
            acc, nxt = state
            r = t // TM - 1 - i
            rows = pl.ds(pl.multiple_of(r * TM, TM), TM)
            full = pl.ds(pl.multiple_of(slot * t + r * TM, TM), TM)
            last = lax.broadcasted_iota(jnp.int32, (TM, LANES), 0) == TM - 1
            new, first = [], []
            for k_l, lo, w in lanes:
                ch = slice(lo, lo + w)
                f, intake = both(g_ref[1, full, ch])
                o, cl = both(g_ref[2, full, ch])
                z = jnp.tanh(g_ref[0, full, ch])
                keep = keep_ref[full, :w]
                gs = q_s[slot, k_l, rows, :w]
                oh = o * s_s[slot, k_l, rows, :w]
                hids[slot][rows, ch] = oh.astype(BF)
                gi = gs * intake
                grads = (
                    gi * (1.0 - z * z),
                    gi * (p_s[slot, k_l, rows, :w] - f * z),
                    load_up(ups[slot], rows, slot * up_at + lo, w) * oh * cl,
                )
                for k, v in enumerate(grads):
                    gg_ref[full, k * c + lo : k * c + lo + w] = v.astype(BF)
                    kept = keep * v
                    moved = jnp.where(last[:, :w], nxt[len(new)], pltpu.roll(kept, TM - 1, 0))
                    gg_ref[full, (3 + k) * c + lo : (3 + k) * c + lo + w] = moved.astype(BF)
                    first.append(kept[:1])
                    new.append(acc[len(new)] + jnp.sum(v.reshape(TM // 8, 8, w), axis=0))
            return tuple(new), tuple(first)

        zeros = tuple(jnp.zeros((1, w), F32) for _, _, w in lanes for _ in range(3))
        sums, firsts = lax.fori_loop(0, t // TM, out, (tuple(sums), zeros))
        for k_l, lo, w in lanes:
            for k in range(3):
                gf_ref[slot : slot + 1, k * c + lo : k * c + lo + w] = firsts[3 * k_l + k]
                gp_ref[slot * EDGE : slot * EDGE + EDGE, (3 + k) * c + lo : (3 + k) * c + lo + w] = jnp.where(
                    top[:, :w], firsts[3 * k_l + k], 0.0
                ).astype(BF)
    for k_l, lo, w in lanes:
        for k in range(3):
            gb_ref[0:1, k * c + lo : k * c + lo + w] = jnp.sum(sums[3 * k_l + k], axis=0, keepdims=True)


def finish(n, up_at, place, gates, ups, keep_w, seg, every):
    t, c = ups[0].shape
    lt = len(cuts(c))
    shape = jax.ShapeDtypeStruct
    return pl.pallas_call(
        functools.partial(finish_kernel, n, up_at),
        in_specs=[SMEM_SPEC] + [VMEM_SPEC] * 6,
        out_shape=[
            shape((t, c), BF),
            shape((t, c), BF),
            shape((2 * t, 6 * c), BF),
            shape((2, 3 * c), F32),
            shape((2 * EDGE, 6 * c), BF),
            shape((1, 3 * c), F32),
        ],
        scratch_shapes=[pltpu.VMEM((2, lt, t, LANES), F32)] * 4 + [pltpu.VMEM((2, 2, lt, SEGS, LANES), F32)],
        compiler_params=params(),
        cost_estimate=TINY,
        name="finish",
    )(place, gates, *ups, keep_w, seg, every)


def wgrad_kernel(dw, place, x_ref, halo_ref, gg_ref, gp_ref, here_ref, away_ref, acc):
    over_tokens = (((0,), (0,)), ((), ()))
    v = lax.dot_general(x_ref[...], gg_ref[...], over_tokens, preferred_element_type=F32)
    acc[...] = v + lax.dot_general(halo_ref[...], gp_ref[...], over_tokens, preferred_element_type=F32)
    p = place[2]
    here_ref[0] = acc[pl.ds(pl.multiple_of(p * dw, 16), dw), :].astype(BF)
    away_ref[0] = acc[pl.ds(pl.multiple_of((1 - p) * dw, 16), dw), :].astype(BF)


def weight_grads(heads, kh, dw, pad, place, x_all, halo, gg, gp):
    width = gg.shape[1]

    def lanes(i, at):
        return (0, lax.rem(at[0] + kh, heads) * 2 + (at[1] ^ (1 - i)))

    whole = lambda i, at: (0, 0)
    return pl.pallas_call(
        functools.partial(wgrad_kernel, dw),
        grid_spec=pltpu.PrefetchScalarGridSpec(
            num_scalar_prefetch=1,
            grid=(2,),
            in_specs=[
                pl.BlockSpec((x_all.shape[0], pad), lanes),
                pl.BlockSpec((halo.shape[0], pad), lanes),
                pl.BlockSpec(gg.shape, whole),
                pl.BlockSpec(gp.shape, whole),
            ],
            out_specs=[pl.BlockSpec((1, dw, width), lambda i, at: (i, 0, 0))] * 2,
            scratch_shapes=[pltpu.VMEM((pad, width), F32)],
        ),
        out_shape=[jax.ShapeDtypeStruct((2, dw, width), BF)] * 2,
        compiler_params=params(),
        cost_estimate=TINY,
        name="weight_grads",
    )(place, x_all, halo, gg, gp)


def xgrad_kernel(slot, place, *refs):
    count = (len(refs) - 3) // 4
    gg_in, nx, w_in = refs[:count], refs[count : 2 * count], refs[2 * count : 3 * count]
    send_ref, keep_ref = refs[3 * count : 3 * count + 2]
    gg_s, sem = refs[3 * count + 2 : 4 * count + 2], refs[4 * count + 2]
    i = pl.program_id(0)
    t = gg_s[0].shape[0]

    @pl.when(i == 0)
    def _():
        copies = [
            pltpu.make_async_copy(gg_in[k].at[pl.ds(slot * t, t)], gg_s[k], sem.at[k]) for k in range(count)
        ]
        for copy in copies:
            copy.start()
        for k, copy in enumerate(copies):
            copy.wait()
            c3 = nx[k].shape[1]
            old = gg_s[k][t - EDGE :, c3:].astype(F32)
            last = lax.broadcasted_iota(jnp.int32, (EDGE, c3), 0) == EDGE - 1
            gg_s[k][t - EDGE :, c3:] = jnp.where(last, nx[k][slot : slot + 1, :], old).astype(BF)

    v = 0.0
    for k in range(count):
        v = v + lax.dot_general(gg_s[k][...], w_in[k][0], (((1,), (1,)), ((), ())), preferred_element_type=F32)

    @pl.when(i < 2)
    def _():
        send_ref[0] = v.astype(BF)

    @pl.when(i >= 2)
    def _():
        keep_ref[0] = v.astype(BF)


def input_grads(slot, place, ggs, nexts, ws):
    count = len(ggs)
    t = ggs[0].shape[0] // 2
    m, pad, _ = ws[0].shape
    order = lambda i: jnp.where(i < 2, 2 * i + 1, 2 * i - 4)
    return pl.pallas_call(
        functools.partial(xgrad_kernel, slot),
        grid_spec=pltpu.PrefetchScalarGridSpec(
            num_scalar_prefetch=1,
            grid=(m,),
            in_specs=[ANY_SPEC] * count
            + [pl.BlockSpec(v.shape, lambda i, at: (0, 0)) for v in nexts]
            + [pl.BlockSpec((1, pad, w.shape[2]), lambda i, at: (order(i), 0, 0)) for w in ws],
            out_specs=[
                pl.BlockSpec((1, t, pad), lambda i, at: (jnp.minimum(i, 1), 0, 0)),
                pl.BlockSpec((1, t, pad), lambda i, at: (jnp.maximum(i - 2, 0), 0, 0)),
            ],
            scratch_shapes=[pltpu.VMEM((t, gg.shape[1]), BF) for gg in ggs]
            + [pltpu.SemaphoreType.DMA((count,))],
        ),
        out_shape=[jax.ShapeDtypeStruct((2, t, pad), BF)] * 2,
        compiler_params=params(),
        cost_estimate=TINY,
        name="input_grads",
    )(place, *ggs, *nexts, *ws)


def join_kernel(*refs):
    *terms, out = refs
    v = terms[0][...].astype(F32)
    for ref in terms[1:]:
        v = v + ref[...].astype(F32)
    out[...] = v.astype(BF)


def join(terms, urgency):
    arrays = [v for v, _ in terms]
    shape = arrays[0].shape[-2:]
    steps = 2 if shape[0] % 32 == 0 else 1
    blocks = shape[0] // steps

    def spec(v, at):
        if at is None:
            return pl.BlockSpec((blocks, shape[1]), lambda i: (i, 0))
        return pl.BlockSpec((None, blocks, shape[1]), lambda i, at=at: (at, i, 0))

    return pl.pallas_call(
        join_kernel,
        grid=(steps,),
        in_specs=[spec(v, at) for v, at in terms],
        out_specs=pl.BlockSpec((blocks, shape[1]), lambda i: (i, 0)),
        out_shape=jax.ShapeDtypeStruct(shape, BF),
        compiler_params=params(),
        cost_estimate=pl.CostEstimate(flops=0, bytes_accessed=urgency * 3690000, transcendentals=0),
        name="join",
    )(*arrays)


def unpack_w_kernel(widths, place, *refs):
    count = len(widths)
    outs = refs[2 * count :]
    low = place[1] == 0
    for tap in range(2):
        for k in range(3):
            mine, other = [], []
            for i, w in enumerate(widths):
                lo = (tap * 3 + k) * w
                mine.append(refs[2 * i][:, lo : lo + w].astype(F32))
                other.append(refs[2 * i + 1][:, lo : lo + w].astype(F32))
            mine, other = jnp.concatenate(mine, axis=1), jnp.concatenate(other, axis=1)
            outs[tap][k] = jnp.concatenate([jnp.where(low, mine, other), jnp.where(low, other, mine)], axis=1)


def unpack_weights(widths, place, pairs):
    rows = pairs[0].shape[0]
    shape = jax.ShapeDtypeStruct((3, rows, 2 * sum(widths)), F32)
    return pl.pallas_call(
        functools.partial(unpack_w_kernel, widths),
        in_specs=[SMEM_SPEC] + [VMEM_SPEC] * len(pairs),
        out_shape=[shape, shape],
        compiler_params=params(),
        cost_estimate=TINY,
        name="unpack_weights",
    )(place, *pairs)


def unpack_h_kernel(widths, place, *refs):
    out_ref = refs[-1]
    low = place[1] == 0

    def body(r, _):
        rows = pl.ds(pl.multiple_of(r * TM, TM), TM)
        mine = jnp.concatenate([refs[i][rows, :].astype(F32) for i in range(len(widths))], axis=1)
        other = refs[len(widths)][rows, :].astype(F32)
        both_halves = jnp.concatenate([jnp.where(low, mine, other), jnp.where(low, other, mine)], axis=1)
        out_ref[rows, :] = both_halves.astype(BF)
        return 0

    lax.fori_loop(0, out_ref.shape[0] // TM, body, 0)


def unpack_hidden(widths, place, mine, other):
    t = other.shape[0]
    return pl.pallas_call(
        functools.partial(unpack_h_kernel, widths),
        in_specs=[SMEM_SPEC] + [VMEM_SPEC] * (len(mine) + 1),
        out_shape=jax.ShapeDtypeStruct((t, 2 * sum(widths)), BF),
        compiler_params=params(),
        cost_estimate=TINY,
        name="unpack_hidden",
    )(place, *mine, other)


def on_device(layer_input, keep, w_now, w_prev, bias, grad_out):
    n, m = lax.axis_size("seq"), lax.axis_size("gate")
    heads = n // 4
    s, g = lax.axis_index("seq"), lax.axis_index("gate")
    h, l, p, a, b = s // 4, s // 2 % 2, s % 2, g // 2, g % 2
    place = jnp.stack([h, l, p, a, b]).astype(jnp.int32)
    t, dl = layer_input.shape
    dw = w_now.shape[1]
    half = dl // 2
    pad = ceil_to(dl, LANES)
    widths = tuple(w for w in WIDTHS) if sum(WIDTHS) == half else (half,)
    low = l == 0

    def seq_to(v, kh, d_l, d_p):
        route = []
        for i in range(n):
            i_h, i_l, i_p = i // 4, i // 2 % 2, i % 2
            route.append((i, ((i_h + kh) % heads * 2 + (i_l ^ d_l)) * 2 + (i_p ^ d_p)))
        return lax.ppermute(v, "seq", route)

    def gate_to(v, d_a, d_b):
        return lax.ppermute(v, "gate", [(i, i ^ (d_a * 2 + d_b)) for i in range(m)])

    group = [(kh, d_p) for kh in range(heads) for d_p in range(2)]

    packed = pack_weights(widths, 0, place, w_now, w_prev)
    behind = lax.ppermute(layer_input[-1:], "seq", [(i, i + 1) for i in range(n - 1)])
    flags = jnp.broadcast_to(jnp.pad(keep, (0, EDGE)).astype(BF)[:, None], (t + EDGE, pad - dl))
    rows = jnp.concatenate([layer_input, jnp.pad(behind, ((0, EDGE - 1), (0, 0)))], axis=0)
    x0 = after(jnp.concatenate([rows, flags], axis=1), packed[0])
    def share_w(pair, *needs):
        got = {(0, 0): pair, (0, 1): seq_to(pair, 0, 0, 1)}
        for kh in range(1, heads):
            got[kh, 0] = seq_to(after(pair, *needs) if needs else pair, kh, 0, 0)
        return got

    def finish_share(got, *needs):
        for kh in range(1, heads):
            got[kh, 1] = seq_to(after(got[kh, 0], *needs) if needs else got[kh, 0], 0, 0, 1)

    def weights_in(got, c):
        if dw % 16 == 0:
            return [got[r] for r in got], list(got)
        stacked = jnp.stack([got[kh, d_p][d_l] for kh in range(heads) for d_l in range(2) for d_p in range(2)])
        blocks = jnp.arange(n)
        rel = (((h - blocks // 4) % heads) * 2 + (l ^ (blocks // 2 % 2))) * 2 + (p ^ (blocks % 2))
        whole = jnp.take(stacked, rel, axis=0).reshape(m, dl, 6 * c)
        return [jnp.pad(whole, ((0, 0), (0, pad - dl), (0, 0)))], []

    half_bias = jnp.where(low, bias[:, :half], bias[:, half:])
    count = len(widths)
    spans = list(offsets(widths))
    near = seq_to(packed[1], 0, 1, 0)
    got = [share_w(jnp.stack([packed[0], near]))]
    y0 = gate_to(x0, 1, 0)
    x1 = seq_to(after(x0, near), 0, 1, 0)
    first_p = got[0][0, 1]
    c0, cy0 = gate_to(after(x0, y0, first_p), 0, 1), gate_to(after(y0, first_p), 0, 1)
    up_packed = pack_up(widths, place, after(grad_out, x0))
    ups = [[up_packed[0], seq_to(after(up_packed[1], first_p), 0, 1, 0)]]
    x1_here = after(x1, c0, cy0)
    y1, c1 = gate_to(x1_here, 1, 0), gate_to(x1_here, 0, 1)
    finish_share(got[0], c1)
    for i in range(1, count):
        packed = pack_weights(widths, i, place, after(w_now, near), w_prev)
        near = seq_to(after(packed[1], c0, cy0, x1), 0, 1, 0)
        got.append(share_w(jnp.stack([packed[0], near]), c1, *[got[i - 1][kh, 0] for kh in range(1, heads)]))
        ups.append([up_packed[2 * i], seq_to(after(up_packed[2 * i + 1], near), 0, 1, 0)])
    cy1 = gate_to(after(y1, ups[0][1]), 0, 1)
    xs = {(0, 0, 0): x0, (0, 1, 0): y0, (0, 0, 1): c0, (0, 1, 1): cy0}
    xs |= {(1, 0, 0): x1, (1, 1, 0): y1, (1, 0, 1): c1, (1, 1, 1): cy1}
    hidden_mine, hidden_other, grads, wide_w, g_first, g_bias, w_pairs = [], [], [], [], [], [], []

    def spread_totals(tot):
        return jnp.stack([tot if r == (0, 0) else seq_to(tot, r[0], 0, r[1]) for r in group])

    def weight_parts(gg, gp, *needs):
        if dw % 16 == 0 and n == 2 * m:
            parts = [
                (kh, *weight_grads(heads, kh, dw, pad, place, x_all, halo, gg, gp)) for kh in range(1, heads)
            ]
            gp = after(gp, parts[-1][1], *needs)
            return parts + [(0, *weight_grads(heads, 0, dw, pad, place, x_all, halo, gg, gp))]
        dots = jnp.einsum("td,tn->dn", x_all, gg, preferred_element_type=F32)
        dots = dots + jnp.einsum("td,tn->dn", halo, gp, preferred_element_type=F32)
        v = dots.astype(BF).reshape(m, pad, -1)[:, :dl].reshape(heads, 2, 2, dw, gg.shape[1])
        away = jnp.where(p == 0, v[:, :, 1], v[:, :, 0])
        here = jnp.where(p == 0, v[:, :, 0], v[:, :, 1])

        def block(v, kh):
            row = lax.dynamic_index_in_dim(v, (h + kh) % heads, 0, keepdims=False)
            return jnp.where(low, row[::-1], row)

        return [(kh, block(here, kh), block(away, kh)) for kh in list(range(1, heads)) + [0]]

    def over_p(parts, *needs):
        came = []
        for _, _, away in parts:
            came.append(after(seq_to(away, 0, 0, 1), *came[-1:], *needs))
        return [here.astype(F32) + v.astype(F32) for (_, here, _), v in zip(parts, came)]

    def over_h(parts, sums, *needs):
        total = sums[-1]
        for (kh, _, _), v in zip(parts[:-1], sums[:-1]):
            total = total + after(seq_to(v.astype(BF), kh, 0, 0), *needs).astype(F32)
        return total.astype(BF)

    waiting = None
    for i, (at, c) in enumerate(spans):
        dims = (n, m, dw, dl, t, c)
        bias_i = half_bias[:, at : at + c]
        if i > 0:
            finish_share(got[i], every)
        w_in, wrel = weights_in(got[i], c)
        if i == 0:
            xrel = list(xs)
            gates, seg, tot, x_all, halo, keep_w, w_rel = gates_and_totals(
                dims, 0, place, w_in, wrel, [xs[r] for r in xrel], xrel, bias_i, ups[i]
            )
        else:
            w_in[0] = after(w_in[0], *[v[2] for v in waiting])
            gates, seg, tot, w_rel = gates_and_totals(
                dims, 0, place, w_in, wrel, [x_all, halo], [], bias_i, ups[i], keep_w
            )
        every = spread_totals(tot)
        wide_w.append(w_rel)
        if i > 0:
            sums = over_p(waiting, tot)
            h_sums = [after(v, every) for v in sums]
            every = after(every, *sums)
        h0, h1, gg, gf, gp, gb = finish(n, 0, place, gates, ups[i], keep_w, seg, every)
        hidden_mine.append(h0)
        hidden_other.append(h1)
        g_first.append(gf)
        g_bias.append(gb)
        needs = []
        if i == count - 1:
            parts = jnp.concatenate([jnp.concatenate(g_first, axis=1), jnp.concatenate(g_bias, axis=1)], axis=0)
            came = [parts if r == (0, 0) else seq_to(parts, r[0], 0, r[1]) for r in group]
            hidden_came = seq_to(after(jnp.concatenate(hidden_other, axis=1), parts), 0, 1, 0)
        if i > 0:
            total = over_h(waiting, h_sums, gg)
            needs.append(total)
        if i == count - 1:
            came = [after(v, *needs) for v in came]
            around = jnp.stack(came)
            needs += [around, hidden_came]
        waiting_next = weight_parts(gg, gp, *needs)
        if i > 0:
            w_pairs += [total[1], seq_to(after(total[0], waiting_next[-1][1]), 0, 1, 0)]
        waiting = waiting_next
        grads.append(gg)
    full_bias = jnp.sum(around[:, 2], axis=0)
    nexts = []
    for slot in range(2):
        block_id = (h * 2 + (l ^ slot)) * 2 + p + 1
        n_h, n_l, n_p = block_id // 4, block_id // 2 % 2, block_id % 2
        member = ((h - n_h) % heads) * 2 + (p ^ n_p)
        row = lax.dynamic_index_in_dim(around, member, 0, keepdims=False)
        row = lax.dynamic_index_in_dim(row, l ^ n_l, 0, keepdims=False)
        nexts.append(jnp.where(block_id < n, row, jnp.zeros_like(row)))
    nexts = jnp.stack(nexts)
    nexts = [nexts[:, 3 * at : 3 * (at + c)] for at, c in spans]
    bias_half = []
    at = 0
    for c in widths:
        bias_half.append(full_bias[at : at + 3 * c].reshape(3, c))
        at += 3 * c
    bias_half = jnp.concatenate(bias_half, axis=1)
    bias_other = seq_to(bias_half, 0, 1, 0)
    nexts[0] = after(nexts[0], bias_other, *[v[2] for v in waiting])
    sent1, kept1 = input_grads(1, place, grads, nexts, wide_w)

    p_came = []
    for v in waiting:
        p_came.append(after(seq_to(v[2], 0, 0, 1), *p_came[-1:]))
    c_came1 = gate_to(after(sent1, p_came[0]), 0, 1)
    nexts[0] = after(nexts[0], c_came1, *w_pairs)
    h_came = []
    for k, (kh, here, _) in enumerate(waiting[:-1]):
        both_l = jnp.stack([join([(here, d), (p_came[k], d)], URGENT) for d in range(2)])
        h_came.append(seq_to(both_l, kh, 0, 0))
    y_came1 = gate_to(join([(kept1, 1), (c_came1, 1)], URGENT), 1, 0)
    sent0, kept0 = input_grads(0, place, grads, nexts, wide_w)
    c_came0 = gate_to(sent0, 0, 1)
    l_came = seq_to(join([(kept1, 0), (c_came1, 0), (y_came1, None)], URGENT), 0, 1, 0)
    total = [
        join([(waiting[-1][1], d), (p_came[-1], d)] + [(v, d) for v in h_came], LATER) for d in range(2)
    ]
    w_pairs += [total[1], seq_to(total[0], 0, 1, 0)]
    y_came0 = gate_to(join([(kept0, 1), (c_came0, 1)], 1), 1, 0)
    grad_x = kept0[0].astype(F32) + c_came0[0].astype(F32) + y_came0.astype(F32) + l_came.astype(F32)
    grad_x = grad_x[:, :dl].astype(BF)

    grad_bias = jnp.concatenate(
        [jnp.where(low, bias_half, bias_other), jnp.where(low, bias_other, bias_half)], axis=1
    )
    hidden = unpack_hidden(widths, place, hidden_mine, hidden_came)
    grad_now, grad_prev = unpack_weights(widths, place, w_pairs)
    return hidden, grad_x, grad_now, grad_prev, grad_bias


def solution(mesh):
    tokens, matrix = P("seq", "gate"), P(None, "seq", "gate")
    return jax.shard_map(
        on_device,
        mesh=mesh,
        in_specs=(tokens, P("seq"), matrix, matrix, P(None, "gate"), tokens),
        out_specs=(tokens, tokens, matrix, matrix, P(None, "gate")),
        check_vma=False,
    )
```

time: 3090 us -> 499 us (0.16)
  local copies, waits for them, and re-layouts: 1850 us -> 19 us
  waiting for transfers between devices: 746 us -> 195 us
  blocking collectives: 212 us -> 0 us
  Pallas kernels: 0 us -> 210 us
  other arithmetic: 138 us -> 23.3 us
  matrix products: 89.5 us -> 0 us
    slice x160 -> x4, local copies, waits for them, and re-layouts: 1310 us -> 1.2 us  [the longest x2 1.19 us: on_device(): bias_i = half_bias[:, at:at + c]]
    unnamed x8 -> x0, waiting for transfers between devices: 462 us -> none
    pad x46 -> x1, local copies, waits for them, and re-layouts: 311 us -> 0.01 us  [on_device(): jnp.pad(keep, (0, EDGE)).astype(BF)[:, None]]
    all_gather x3 -> x0, waiting for transfers between devices: 283 us -> none  [the longest x1 126 us: on_device(): lax.all_gather(w_now, 'seq', axis=1, tiled=True)]
    pallas_call x0 -> x22, Pallas kernels: none -> 210 us  [the longest x2 57.3 us: gates_and_totals(): pl.pallas_call(functools.partial(gates_kernel, plan), in_specs=[SMEM_SPEC...]
    unnamed x85 -> x53, local copies, waits for them, and re-layouts: 213 us -> 11.1 us
    ppermute x2 -> x42, waiting for transfers between devices: 1.31 us -> 195 us  [the longest x31 174 us: seq_to(): return lax.ppermute(v, 'seq', route)]
    all_to_all x3 -> x0, blocking collectives: 173 us -> none  [the longest x1 58.3 us: on_device(): lax.all_to_all(long_state, 'seq', split_axis=1, concat_axis=0, tiled=True)]
  transfers between devices with their start and end apart: 11 -> 42, of which waited for: 6 -> 14; matrix products, arithmetic and copies ran while one was open for 38% -> 6% of each run, Pallas kernels for 0% -> 38%
where the time goes in v2:
time: 499 us; the launch traced here: 498 us
  Pallas kernels  210 us (42%)
  waiting for transfers between devices  195 us (39%)
  starting transfers between devices  48.7 us (10%)
  other arithmetic  23.3 us (5%)
  local copies, waits for them, and re-layouts  19 us (4%)
    ppermute x31, waiting for transfers between devices, seq_to(): return lax.ppermute(v, 'seq', route)  174 us
    pallas_call x2, Pallas kernels, gates_and_totals(): pl.pallas_call(functools.partial(gates_kernel, plan), in_specs=[SMEM_SPEC...  57.3 us
    pallas_call x4, Pallas kernels, weight_grads(): pl.pallas_call(functools.partial(wgrad_kernel, dw), grid_spec=pltpu.Prefe...  41.9 us
    pallas_call x2, Pallas kernels, input_grads(): pl.pallas_call(functools.partial(xgrad_kernel, slot), grid_spec=pltpu.Pre...  38.8 us
    ppermute x31, starting transfers between devices, seq_to(): return lax.ppermute(v, 'seq', route)  37.9 us
    pallas_call x2, Pallas kernels, finish(): pl.pallas_call(functools.partial(finish_kernel, n, up_at), in_specs=[SMEM...  35.4 us
    ppermute x10, waiting for transfers between devices, gate_to(): return lax.ppermute(v, 'gate', [(i, i ^ d_a * 2 + d_b) for i in range(m)])  20.9 us
    pallas_call x7, Pallas kernels, join(): pl.pallas_call(join_kernel, grid=(steps,), in_specs=[spec(v, at) for v, a...  17.1 us
  transfers between devices with their start and end apart: 42, of which 14 were waited for; matrix products, arithmetic and copies ran while one was open for 6% of the time, Pallas kernels for 38%

profile of v2, /device:TPU:0, one launch (start us, length us, event | category | flops | bytes accessed | tf_op | source)
XLA Modules:
  0.0 497.8 jit_solution(11616404691921929970)
XLA Ops:
  3.4 4.8 collective-permute-start.3
  8.9 3.3 pack_weights.2
  17.2 6.9 %collective-permute-done = bf16[288,768]{1,0:T(8,128)(2,1)S(1)} collective-permute-done((bf16[288,768]{1,0:T(8,128)(2,1)}, bf16[288,768]{1,0:T(8,128)(2,1)S(1)}, u32[]{:S(2)}, u32[]{:S(2)}) %collective-permute-start) | collective-permute-done | bytes 442400 | tf_op jit(solution)/shard_map/ppermute | solution.py:644
  28.3 17.3 %collective-permute-done.1.refs_1_ = bf16[2,288,768]{2,1,0:T(8,128)(2,1)S(1)} collective-permute-done((bf16[2,288,768]{2,1,0:T(8,128)(2,1)}, bf16[2,288,768]{2,1,0:T(8,128)(2,1)S(1)}, u32[]{:S(2)}, u32[]{:S(2)}) %collective-permute-start.1) | collective-permute-done | bytes 884768 | tf_op jit(solution)/shard_map/ppermute | solution.py:644
  47.0 9.2 %collective-permute-done.4.refs_8_ = bf16[1040,640]{1,0:T(8,128)(2,1)} collective-permute-done((bf16[1040,640]{1,0:T(8,128)(2,1)S(1)}, bf16[1040,640]{1,0:T(8,128)(2,1)}, u32[]{:S(2)}, u32[]{:S(2)}) %collective-permute-start.4) | collective-permute-done | bytes 1331232 | tf_op jit(solution)/shard_map/ppermute | solution.py:644
  58.9 2.6 collective-permute-start.2
  61.5 3.6 pack_weights.3
  65.8 2.4 copy.18.up_ref
  68.2 5.0 %pack_up.1 = (bf16[1024,128]{1,0:T(8,128)(2,1)}, bf16[1024,128]{1,0:T(8,128)(2,1)}, bf16[1024,160]{1,0:T(8,128)(2,1)}, bf16[1024,256]{1,0:T(8,128)(2,1)}) custom-call(s32[5]{0:T(128)} %stack.100.place, bf16[1024,576]{1,0:T(8,128)(2,1)} %copy.18.up_ref), custom_call_target="tpu_custom_call" | custom-call | flops 1024 | bytes 1024 | tf_op jit(solution)/shard_map/pack_up/pallas_call | solution.py:104
  74.6 29.7 %collective-permute-done.11.refs_14_.up1 = bf16[1024,128]{1,0:T(8,128)(2,1)S(1)} collective-permute-done((bf16[1024,128]{1,0:T(8,128)(2,1)}, bf16[1024,128]{1,0:T(8,128)(2,1)S(1)}, u32[]{:S(2)}, u32[]{:S(2)}) %collective-permute-start.11) | collective-permute-done | bytes 262176 | tf_op jit(solution)/shard_map/ppermute | solution.py:644
  108.2 20.7 %collective-permute-done.9.refs_3_ = bf16[2,288,768]{2,1,0:T(8,128)(2,1)} collective-permute-done((bf16[2,288,768]{2,1,0:T(8,128)(2,1)}, bf16[2,288,768]{2,1,0:T(8,128)(2,1)}, u32[]{:S(2)}, u32[]{:S(2)}) %collective-permute-start.9) | collective-permute-done | bytes 884768 | tf_op jit(solution)/shard_map/ppermute | solution.py:644
  128.9 22.2 %gates_and_totals.2 = (f32[3,2048,128]{2,1,0:T(8,128)}, f32[2,3,8,128]{3,2,1,0:T(8,128)}, f32[2,3,128]{2,1,0:T(4,128)}, bf16[2048,2560]{1,0:T(8,128)(2,1)}, bf16...) custom-call(s32[5]{0:T(128)} %stack.100.place, ...), custom_call_target="tpu_custom_call" | custom-call | flops 1024 | bytes 1024 | tf_op jit(solution)/shard_map/gates_and_totals/pallas_call | solution.py:282
  151.1 2.5 collective-permute-start.15
  156.2 4.7 collective-permute-done.15
  163.2 12.0 %finish.2 = (bf16[1024,128]{1,0:T(8,128)(2,1)}, bf16[1024,128]{1,0:T(8,128)(2,1)}, bf16[2048,768]{1,0:T(8,128)(2,1)}, f32[2,384]{1,0:T(2,128)}, bf16[32,768]{1,0:T(8,128)(2,1)}, /*index=5*/f32[1,384]{1,0:T(1,128)}) custom-call(s32[5]{0:T(128)} %stack.100.place, f32[3,2048,128]{2,1,0:T(8,128)} %get-tuple-element.96.g_ref, ...), custom_call_target="tpu_custom_call" | custom-call | flops 1024 | bytes 1024 | tf_op jit(solution)/shard_map/finish/pallas_call | solution.py:423
  175.2 9.5 %weight_grads.4 = (bf16[2,288,768]{2,1,0:T(8,128)(2,1)}, bf16[2,288,768]{2,1,0:T(8,128)(2,1)}) custom-call(s32[5]{0:T(128)} %stack.100.place, bf16[2048,2560]{1,0:T(8,128)(2,1)} %get-tuple-element.105.x_ref.refs_4_, bf16[32,2560]{1,0:T(8,128)(2,1)} %get-tuple-element.106.halo_ref.refs_5_, bf16[2048,768]{1,0:T(8,128)(2,1)} %get-tuple-element.107.gg_ref.refs_0_, ...), custom_call_target="tpu_custom_call" | custom-call | flops 1024 | bytes 1024 | tf_op jit(solution)/shard_map/weight_grads/pallas_call | solution.py:457
  185.8 9.5 %weight_grads.5 = (bf16[2,288,768]{2,1,0:T(8,128)(2,1)}, bf16[2,288,768]{2,1,0:T(8,128)(2,1)}) custom-call(s32[5]{0:T(128)} %stack.100.place, bf16[2048,2560]{1,0:T(8,128)(2,1)} %get-tuple-element.105.x_ref.refs_4_, bf16[32,2560]{1,0:T(8,128)(2,1)} %get-tuple-element.106.halo_ref.refs_5_, bf16[2048,768]{1,0:T(8,128)(2,1)} %get-tuple-element.107.gg_ref.refs_0_, ...), custom_call_target="tpu_custom_call" | custom-call | flops 1024 | bytes 1024 | tf_op jit(solution)/shard_map/weight_grads/pallas_call | solution.py:457
  196.7 2.2 collective-permute-done.20.refs_8_.up1
  199.0 11.0 %collective-permute-done.19.refs_3_ = bf16[2,288,960]{2,1,0:T(8,128)(2,1)} collective-permute-done((bf16[2,288,960]{2,1,0:T(8,128)(2,1)}, bf16[2,288,960]{2,1,0:T(8,128)(2,1)}, u32[]{:S(2)}, u32[]{:S(2)}) %collective-permute-start.19) | collective-permute-done | bytes 1105952 | tf_op jit(solution)/shard_map/ppermute | solution.py:644
  209.9 35.1 %gates_and_totals.3 = (f32[3,2048,160]{2,1,0:T(8,128)}, f32[2,3,8,160]{3,2,1,0:T(8,128)}, f32[2,3,160]{2,1,0:T(4,128)}, bf16[4,640,960]{2,1,0:T(8,128)(2,1)}) custom-call(s32[5]{0:T(128)} %stack.100.place, bf16[2,288,960]{2,1,0:T(8,128)(2,1)} %copy-done.2, bf16[2,288,960]{2,1,0:T(8,128)(2,1)} %collective-permute-done.17.refs_1_, ...), custom_call_target="tpu_custom_call" | custom-call | flops 1024 | bytes 1024 | tf_op jit(solution)/shard_map/gates_and_totals/pallas_call | solution.py:282
  245.8 2.3 collective-permute-start.22
  249.6 2.3 convert_add_fusion.1
  251.9 10.4 %collective-permute-done.23 = f32[2,3,160]{2,1,0:T(4,128)S(1)} collective-permute-done((f32[2,3,160]{2,1,0:T(4,128)}, f32[2,3,160]{2,1,0:T(4,128)S(1)}, u32[]{:S(2)}, u32[]{:S(2)}) %collective-permute-start.23) | collective-permute-done | bytes 3872 | tf_op jit(solution)/shard_map/ppermute | solution.py:644
  264.2 23.4 %finish.3 = (bf16[1024,160]{1,0:T(8,128)(2,1)}, bf16[1024,160]{1,0:T(8,128)(2,1)}, bf16[2048,960]{1,0:T(8,128)(2,1)}, f32[2,480]{1,0:T(2,128)}, bf16[32,960]{1,0:T(8,128)(2,1)}, /*index=5*/f32[1,480]{1,0:T(1,128)}) custom-call(s32[5]{0:T(128)} %stack.100.place, f32[3,2048,160]{2,1,0:T(8,128)} %get-tuple-element.119.g_ref, ...), custom_call_target="tpu_custom_call" | custom-call | flops 1024 | bytes 1024 | tf_op jit(solution)/shard_map/finish/pallas_call | solution.py:423
  290.2 2.9 collective-permute-start.29
  293.3 11.5 %weight_grads.6 = (bf16[2,288,960]{2,1,0:T(8,128)(2,1)}, bf16[2,288,960]{2,1,0:T(8,128)(2,1)}) custom-call(s32[5]{0:T(128)} %stack.100.place, bf16[2048,2560]{1,0:T(8,128)(2,1)} %get-tuple-element.105.x_ref.refs_4_, bf16[32,2560]{1,0:T(8,128)(2,1)} %get-tuple-element.106.halo_ref.refs_5_, bf16[2048,960]{1,0:T(8,128)(2,1)} %get-tuple-element.134.gg_ref.refs_1_, ...), custom_call_target="tpu_custom_call" | custom-call | flops 1024 | bytes 1024 | tf_op jit(solution)/shard_map/weight_grads/pallas_call | solution.py:457
  307.5 2.3 collective-permute-start.26
  309.8 2.3 add_convert_fusion
  314.4 3.4 collective-permute-done.26
  317.8 11.4 %weight_grads.7 = (bf16[2,288,960]{2,1,0:T(8,128)(2,1)}, bf16[2,288,960]{2,1,0:T(8,128)(2,1)}) custom-call(s32[5]{0:T(128)} %stack.100.place, bf16[2048,2560]{1,0:T(8,128)(2,1)} %get-tuple-element.105.x_ref.refs_4_, bf16[32,2560]{1,0:T(8,128)(2,1)} %get-tuple-element.106.halo_ref.refs_5_, bf16[2048,960]{1,0:T(8,128)(2,1)} %get-tuple-element.134.gg_ref.refs_1_, ...), custom_call_target="tpu_custom_call" | custom-call | flops 1024 | bytes 1024 | tf_op jit(solution)/shard_map/weight_grads/pallas_call | solution.py:457
  329.2 19.6 %input_grads.2 = (bf16[2,1024,640]{2,1,0:T(8,128)(2,1)}, bf16[2,1024,640]{2,1,0:T(8,128)(2,1)}) custom-call(s32[5]{0:T(128)} %stack.100.place, bf16[2048,768]{1,0:T(8,128)(2,1)} %get-tuple-element.107.gg_ref.refs_0_, bf16[2048,960]{1,0:T(8,128)(2,1)} %get-tuple-element.134.gg_ref.refs_1_, f32[2,384]{1,0:T(2,128)} %pad_maximum_fusion.10.refs_2_, ...), custom_call_target="tpu_custom_call" | custom-call | flops 1024 | bytes 1024 | tf_op jit(solution)/shard_map/input_grads/pallas_call | solution.py:518
  351.8 10.8 %collective-permute-done.34.refs_1_ = bf16[288,768]{1,0:T(8,128)(2,1)S(1)} collective-permute-done((bf16[288,768]{1,0:T(8,128)(2,1)S(1)}, bf16[288,768]{1,0:T(8,128)(2,1)S(1)}, u32[]{:S(2)}, u32[]{:S(2)}) %collective-permute-start.34) | collective-permute-done | bytes 442400 | tf_op jit(solution)/shard_map/ppermute | solution.py:644
  363.4 19.1 %input_grads.3 = (bf16[2,1024,640]{2,1,0:T(8,128)(2,1)}, bf16[2,1024,640]{2,1,0:T(8,128)(2,1)}) custom-call(s32[5]{0:T(128)} %stack.100.place, bf16[2048,768]{1,0:T(8,128)(2,1)} %get-tuple-element.107.gg_ref.refs_0_, bf16[2048,960]{1,0:T(8,128)(2,1)} %get-tuple-element.134.gg_ref.refs_1_, f32[2,384]{1,0:T(2,128)} %pad_maximum_fusion.10.refs_2_, ...), custom_call_target="tpu_custom_call" | custom-call | flops 1024 | bytes 1024 | tf_op jit(solution)/shard_map/input_grads/pallas_call | solution.py:518
  382.6 2.7 join.8
  389.7 2.1 join.11
  391.8 2.2 pad_maximum_fusion.1
  395.9 20.9 %collective-permute-done.37.refs_2_ = bf16[1024,640]{1,0:T(8,128)(2,1)} collective-permute-done((bf16[1024,640]{1,0:T(8,128)(2,1)}, bf16[1024,640]{1,0:T(8,128)(2,1)}, u32[]{:S(2)}, u32[]{:S(2)}) %collective-permute-start.37) | collective-permute-done | bytes 1310752 | tf_op jit(solution)/shard_map/ppermute | solution.py:647
  416.8 3.2 join.9
  421.7 2.7 join.7
  425.4 23.0 %collective-permute-done.40.refs_2_ = bf16[2,288,960]{2,1,0:T(8,128)(2,1)} collective-permute-done((bf16[2,288,960]{2,1,0:T(8,128)(2,1)}, bf16[2,288,960]{2,1,0:T(8,128)(2,1)}, u32[]{:S(2)}, u32[]{:S(2)}) %collective-permute-start.40) | collective-permute-done | bytes 1105952 | tf_op jit(solution)/shard_map/ppermute | solution.py:644
  448.4 2.2 join.13
  450.6 2.2 copy.20.refs_2_
  452.9 3.8 unpack_hidden.1
  456.7 2.4 copy.21
  459.8 2.2 join.12.refs_2_
  462.0 25.2 %collective-permute-done.41.refs_3_ = bf16[288,960]{1,0:T(8,128)(2,1)S(1)} collective-permute-done((bf16[288,960]{1,0:T(8,128)(2,1)}, bf16[288,960]{1,0:T(8,128)(2,1)S(1)}, u32[]{:S(2)}, u32[]{:S(2)}) %collective-permute-start.41) | collective-permute-done | bytes 552992 | tf_op jit(solution)/shard_map/ppermute | solution.py:644
  488.0 4.1 unpack_weights.1
  494.1 2.3 fusion.4
  (147 shorter events, 59.5 us)
Async XLA Ops:
  3.4 10.5 %collective-permute-start.3 = (bf16[1,576]{1,0:T(2,128)(2,1)S(1)}, bf16[1,576]{1,0:T(2,128)(2,1)S(1)}, u32[]{:S(2)}, u32[]{:S(2)}) collective-permute-start(bf16[1,576]{1,0:T(2,128)(2,1)S(1)} %slice.61), channel_id=1, source_target_pairs={{0,4},{4,8},{8,12},{12,16},{16,20},{20,24},{24,28},{1,5},{5,9},{9,... | collective-permute-start | bytes 3464 | tf_op jit(solution)/shard_map/ppermute | solution.py:652
  12.2 11.8 %collective-permute-start = (bf16[288,768]{1,0:T(8,128)(2,1)}, bf16[288,768]{1,0:T(8,128)(2,1)S(1)}, u32[]{:S(2)}, u32[]{:S(2)}) collective-permute-start(bf16[288,768]{1,0:T(8,128)(2,1)} %get-tuple-element.84), channel_id=1, source_target_pairs={{0,8},{4,12},{8,0},{12,4},{16,24},{20,28},{24,16},{28,20},{1,9},{5... | collective-permute-start | bytes 1327112 | tf_op jit(solution)/shard_map/ppermute | solution.py:644
  15.6 49.5 %copy-start = (bf16[1040,640]{1,0:T(8,128)(2,1)}, bf16[1040,640]{1,0:T(8,128)(2,1)S(1)}, u32[]{:S(2)}) copy-start(bf16[1040,640]{1,0:T(8,128)(2,1)S(1)} %fusion.6.refs_4_) | copy-start | bytes 3993604
  15.6 30.9 %collective-permute-start.5 = (bf16[1040,640]{1,0:T(8,128)(2,1)S(1)}, bf16[1040,640]{1,0:T(8,128)(2,1)S(1)}, u32[]{:S(2)}, u32[]{:S(2)}) collective-permute-start(bf16[1040,640]{1,0:T(8,128)(2,1)S(1)} %fusion.6.refs_4_), channel_id=1, source_target_pairs={{0,2},{1,3},{2,0},{3,1},{4,6},{5,7},{6,4},{7,5},{8,10},{9,11},{10,... | collective-permute-start | bytes 3993608 | tf_op jit(solution)/shard_map/ppermute | solution.py:647
  25.1 20.4 %collective-permute-start.1 = (bf16[2,288,768]{2,1,0:T(8,128)(2,1)}, bf16[2,288,768]{2,1,0:T(8,128)(2,1)S(1)}, u32[]{:S(2)}, u32[]{:S(2)}) collective-permute-start(bf16[2,288,768]{2,1,0:T(8,128)(2,1)} %pad_maximum_fusion.2.refs_0_), channel_id=1, source_target_pairs={{0,4},{4,0},{8,12},{12,8},{16,20},{20,16},{24,28},{28,24},{1,5},{5... | collective-permute-start | bytes 2654216 | tf_op jit(solution)/shard_map/ppermute | solution.py:644
  26.7 29.6 %collective-permute-start.4 = (bf16[1040,640]{1,0:T(8,128)(2,1)S(1)}, bf16[1040,640]{1,0:T(8,128)(2,1)}, u32[]{:S(2)}, u32[]{:S(2)}) collective-permute-start(bf16[1040,640]{1,0:T(8,128)(2,1)S(1)} %fusion.6.refs_4_), channel_id=1, source_target_pairs={{0,8},{4,12},{8,0},{12,4},{16,24},{20,28},{24,16},{28,20},{1,9},{5... | collective-permute-start | bytes 3993608 | tf_op jit(solution)/shard_map/ppermute | solution.py:644
  46.5 9.7 %collective-permute-start.6 = (bf16[1040,640]{1,0:T(8,128)(2,1)S(1)}, bf16[1040,640]{1,0:T(8,128)(2,1)S(1)}, u32[]{:S(2)}, u32[]{:S(2)}) collective-permute-start(bf16[1040,640]{1,0:T(8,128)(2,1)S(1)} %fusion.6.refs_4_), channel_id=1, source_target_pairs={{0,1},{1,0},{2,3},{3,2},{4,5},{5,4},{6,7},{7,6},{8,9},{9,8},{10,11... | collective-permute-start | bytes 3993608 | tf_op jit(solution)/shard_map/ppermute | solution.py:647
  46.5 9.7 %collective-permute-start.7 = (bf16[1040,640]{1,0:T(8,128)(2,1)S(1)}, bf16[1040,640]{1,0:T(8,128)(2,1)S(1)}, u32[]{:S(2)}, u32[]{:S(2)}) collective-permute-start(bf16[1040,640]{1,0:T(8,128)(2,1)S(1)} %collective-permute-done.5.refs_5_), channel_id=1, source_target_pairs={{0,1},{1,0},{2,3},{3,2},{4,5},{5,4},{6,7},{7,6},{8,9},{9,8},{10,11... | collective-permute-start | bytes 3993608 | tf_op jit(solution)/shard_map/ppermute | solution.py:647
  57.4 47.0 %collective-permute-start.10 = (bf16[1040,640]{1,0:T(8,128)(2,1)}, bf16[1040,640]{1,0:T(8,128)(2,1)}, u32[]{:S(2)}, u32[]{:S(2)}) collective-permute-start(bf16[1040,640]{1,0:T(8,128)(2,1)} %collective-permute-done.4.refs_8_), channel_id=1, source_target_pairs={{0,2},{1,3},{2,0},{3,1},{4,6},{5,7},{6,4},{7,5},{8,10},{9,11},{10,... | collective-permute-start | bytes 3993608 | tf_op jit(solution)/shard_map/ppermute | solution.py:647
  58.9 47.5 %collective-permute-start.8 = (bf16[1040,640]{1,0:T(8,128)(2,1)}, bf16[1040,640]{1,0:T(8,128)(2,1)}, u32[]{:S(2)}, u32[]{:S(2)}) collective-permute-start(bf16[1040,640]{1,0:T(8,128)(2,1)} %collective-permute-done.4.refs_8_), channel_id=1, source_target_pairs={{0,1},{1,0},{2,3},{3,2},{4,5},{5,4},{6,7},{7,6},{8,9},{9,8},{10,11... | collective-permute-start | bytes 3993608 | tf_op jit(solution)/shard_map/ppermute | solution.py:647
  58.9 47.5 %collective-permute-start.2 = (bf16[2,288,768]{2,1,0:T(8,128)(2,1)}, bf16[2,288,768]{2,1,0:T(8,128)(2,1)}, u32[]{:S(2)}, u32[]{:S(2)}) collective-permute-start(bf16[2,288,768]{2,1,0:T(8,128)(2,1)} %pad_maximum_fusion.2.refs_0_), channel_id=1, source_target_pairs={{0,16},{4,20},{8,24},{12,28},{16,0},{20,4},{24,8},{28,12},{1,17},{... | collective-permute-start | bytes 2654216 | tf_op jit(solution)/shard_map/ppermute | solution.py:644
  65.1 40.1 %copy-start.15 = (bf16[288,960]{1,0:T(8,128)(2,1)S(1)}, bf16[288,960]{1,0:T(8,128)(2,1)}, u32[]{:S(2)}) copy-start(bf16[288,960]{1,0:T(8,128)(2,1)} %get-tuple-element.102) | copy-start | bytes 1658884
  65.1 39.2 %collective-permute-start.16 = (bf16[288,960]{1,0:T(8,128)(2,1)}, bf16[288,960]{1,0:T(8,128)(2,1)S(1)}, u32[]{:S(2)}, u32[]{:S(2)}) collective-permute-start(bf16[288,960]{1,0:T(8,128)(2,1)} %get-tuple-element.104), channel_id=1, source_target_pairs={{0,8},{4,12},{8,0},{12,4},{16,24},{20,28},{24,16},{28,20},{1,9},{5... | collective-permute-start | bytes 1658888 | tf_op jit(solution)/shard_map/ppermute | solution.py:644
  73.2 34.3 %copy-start.20 = (f32[3,576]{1,0:T(4,128)S(1)}, f32[3,576]{1,0:T(4,128)}, u32[]{:S(2)}) copy-start(f32[3,576]{1,0:T(4,128)} %param.10) | copy-start | bytes 20740
  73.2 31.1 %collective-permute-start.11 = (bf16[1024,128]{1,0:T(8,128)(2,1)}, bf16[1024,128]{1,0:T(8,128)(2,1)S(1)}, u32[]{:S(2)}, u32[]{:S(2)}) collective-permute-start(bf16[1024,128]{1,0:T(8,128)(2,1)} %get-tuple-element.93), channel_id=1, source_target_pairs={{0,8},{4,12},{8,0},{12,4},{16,24},{20,28},{24,16},{28,20},{1,9},{5... | collective-permute-start | bytes 786440 | tf_op jit(solution)/shard_map/ppermute | solution.py:644
  104.3 24.6 %copy-start.10 = (bf16[1024,128]{1,0:T(8,128)(2,1)}, bf16[1024,128]{1,0:T(8,128)(2,1)S(1)}, u32[]{:S(2)}) copy-start(bf16[1024,128]{1,0:T(8,128)(2,1)S(1)} %collective-permute-done.11.refs_14_.up1) | copy-start | bytes 786436
  104.3 24.6 %collective-permute-start.12 = (bf16[1040,640]{1,0:T(8,128)(2,1)}, bf16[1040,640]{1,0:T(8,128)(2,1)}, u32[]{:S(2)}, u32[]{:S(2)}) collective-permute-start(bf16[1040,640]{1,0:T(8,128)(2,1)} %collective-permute-done.10.refs_9_), channel_id=1, source_target_pairs={{0,1},{1,0},{2,3},{3,2},{4,5},{5,4},{6,7},{7,6},{8,9},{9,8},{10,11... | collective-permute-start | bytes 3993608 | tf_op jit(solution)/shard_map/ppermute | solution.py:647
  106.4 49.1 %copy-start.2 = (bf16[2,288,960]{2,1,0:T(8,128)(2,1)}, bf16[2,288,960]{2,1,0:T(8,128)(2,1)S(1)}, u32[]{:S(2)}) copy-start(bf16[2,288,960]{2,1,0:T(8,128)(2,1)S(1)} %pad_maximum_fusion.refs_0_) | copy-start | bytes 3317764
  106.4 55.8 %collective-permute-start.18 = (bf16[2,288,960]{2,1,0:T(8,128)(2,1)S(1)}, bf16[2,288,960]{2,1,0:T(8,128)(2,1)}, u32[]{:S(2)}, u32[]{:S(2)}) collective-permute-start(bf16[2,288,960]{2,1,0:T(8,128)(2,1)S(1)} %pad_maximum_fusion.refs_0_), channel_id=1, source_target_pairs={{0,16},{4,20},{8,24},{12,28},{16,0},{20,4},{24,8},{28,12},{1,17},{... | collective-permute-start | bytes 3317768 | tf_op jit(solution)/shard_map/ppermute | solution.py:644
  106.5 22.4 %collective-permute-start.9 = (bf16[2,288,768]{2,1,0:T(8,128)(2,1)}, bf16[2,288,768]{2,1,0:T(8,128)(2,1)}, u32[]{:S(2)}, u32[]{:S(2)}) collective-permute-start(bf16[2,288,768]{2,1,0:T(8,128)(2,1)} %collective-permute-done.2.refs_2_), channel_id=1, source_target_pairs={{0,4},{4,0},{8,12},{12,8},{16,20},{20,16},{24,28},{28,24},{1,5},{5... | collective-permute-start | bytes 2654216 | tf_op jit(solution)/shard_map/ppermute | solution.py:644
  151.1 9.8 %collective-permute-start.15 = (f32[2,3,128]{2,1,0:T(4,128)}, f32[2,3,128]{2,1,0:T(4,128)S(1)}, u32[]{:S(2)}, u32[]{:S(2)}) collective-permute-start(f32[2,3,128]{2,1,0:T(4,128)} %get-tuple-element.99), channel_id=1, source_target_pairs={{0,20},{4,16},{8,28},{12,24},{16,4},{20,0},{24,12},{28,8},{1,21},{... | collective-permute-start | bytes 9224 | tf_op jit(solution)/shard_map/ppermute | solution.py:644
  153.6 7.3 %collective-permute-start.13 = (f32[2,3,128]{2,1,0:T(4,128)}, f32[2,3,128]{2,1,0:T(4,128)S(1)}, u32[]{:S(2)}, u32[]{:S(2)}) collective-permute-start(f32[2,3,128]{2,1,0:T(4,128)} %get-tuple-element.99), channel_id=1, source_target_pairs={{0,4},{4,0},{8,12},{12,8},{16,20},{20,16},{24,28},{28,24},{1,5},{5... | collective-permute-start | bytes 9224 | tf_op jit(solution)/shard_map/ppermute | solution.py:644
  155.2 5.8 %collective-permute-start.14 = (f32[2,3,128]{2,1,0:T(4,128)}, f32[2,3,128]{2,1,0:T(4,128)S(1)}, u32[]{:S(2)}, u32[]{:S(2)}) collective-permute-start(f32[2,3,128]{2,1,0:T(4,128)} %get-tuple-element.99), channel_id=1, source_target_pairs={{0,16},{4,20},{8,24},{12,28},{16,0},{20,4},{24,8},{28,12},{1,17},{... | collective-permute-start | bytes 9224 | tf_op jit(solution)/shard_map/ppermute | solution.py:644
  155.5 43.4 %collective-permute-start.17 = (bf16[2,288,960]{2,1,0:T(8,128)(2,1)S(1)}, bf16[2,288,960]{2,1,0:T(8,128)(2,1)}, u32[]{:S(2)}, u32[]{:S(2)}) collective-permute-start(bf16[2,288,960]{2,1,0:T(8,128)(2,1)S(1)} %pad_maximum_fusion.refs_0_), channel_id=1, source_target_pairs={{0,4},{4,0},{8,12},{12,8},{16,20},{20,16},{24,28},{28,24},{1,5},{5... | collective-permute-start | bytes 3317768 | tf_op jit(solution)/shard_map/ppermute | solution.py:644
  162.2 47.7 %collective-permute-start.19 = (bf16[2,288,960]{2,1,0:T(8,128)(2,1)}, bf16[2,288,960]{2,1,0:T(8,128)(2,1)}, u32[]{:S(2)}, u32[]{:S(2)}) collective-permute-start(bf16[2,288,960]{2,1,0:T(8,128)(2,1)} %collective-permute-done.18.refs_2_), channel_id=1, source_target_pairs={{0,4},{4,0},{8,12},{12,8},{16,20},{20,16},{24,28},{28,24},{1,5},{5... | collective-permute-start | bytes 3317768 | tf_op jit(solution)/shard_map/ppermute | solution.py:644
  184.6 64.9 %collective-permute-start.24 = (bf16[2,288,768]{2,1,0:T(8,128)(2,1)}, bf16[2,288,768]{2,1,0:T(8,128)(2,1)}, u32[]{:S(2)}, u32[]{:S(2)}) collective-permute-start(bf16[2,288,768]{2,1,0:T(8,128)(2,1)} %get-tuple-element.109), channel_id=1, source_target_pairs={{0,4},{4,0},{8,12},{12,8},{16,20},{20,16},{24,28},{28,24},{1,5},{5... | collective-permute-start | bytes 2654216 | tf_op jit(solution)/shard_map/ppermute | solution.py:644
  185.8 13.2 %collective-permute-start.20 = (bf16[1024,256]{1,0:T(8,128)(2,1)}, bf16[1024,256]{1,0:T(8,128)(2,1)S(1)}, u32[]{:S(2)}, u32[]{:S(2)}) collective-permute-start(bf16[1024,256]{1,0:T(8,128)(2,1)} %get-tuple-element.118), channel_id=1, source_target_pairs={{0,8},{4,12},{8,0},{12,4},{16,24},{20,28},{24,16},{28,20},{1,9},{5... | collective-permute-start | bytes 1572872 | tf_op jit(solution)/shard_map/ppermute | solution.py:644
  195.2 67.6 %collective-permute-start.25 = (bf16[2,288,768]{2,1,0:T(8,128)(2,1)}, bf16[2,288,768]{2,1,0:T(8,128)(2,1)}, u32[]{:S(2)}, u32[]{:S(2)}) collective-permute-start(bf16[2,288,768]{2,1,0:T(8,128)(2,1)} %get-tuple-element.112), channel_id=1, source_target_pairs={{0,4},{4,0},{8,12},{12,8},{16,20},{20,16},{24,28},{28,24},{1,5},{5... | collective-permute-start | bytes 2654216 | tf_op jit(solution)/shard_map/ppermute | solution.py:644
  209.9 39.6 %copy-start.12 = (bf16[2,288,768]{2,1,0:T(8,128)(2,1)S(1)}, bf16[2,288,768]{2,1,0:T(8,128)(2,1)}, u32[]{:S(2)}) copy-start(bf16[2,288,768]{2,1,0:T(8,128)(2,1)} %get-tuple-element.110) | copy-start | bytes 2654212
  245.1 6.7 %collective-permute-start.21 = (f32[2,3,160]{2,1,0:T(4,128)}, f32[2,3,160]{2,1,0:T(4,128)S(1)}, u32[]{:S(2)}, u32[]{:S(2)}) collective-permute-start(f32[2,3,160]{2,1,0:T(4,128)} %get-tuple-element.121), channel_id=1, source_target_pairs={{0,4},{4,0},{8,12},{12,8},{16,20},{20,16},{24,28},{28,24},{1,5},{5... | collective-permute-start | bytes 11528 | tf_op jit(solution)/shard_map/ppermute | solution.py:644
  245.8 6.0 %collective-permute-start.22 = (f32[2,3,160]{2,1,0:T(4,128)}, f32[2,3,160]{2,1,0:T(4,128)S(1)}, u32[]{:S(2)}, u32[]{:S(2)}) collective-permute-start(f32[2,3,160]{2,1,0:T(4,128)} %get-tuple-element.121), channel_id=1, source_target_pairs={{0,16},{4,20},{8,24},{12,28},{16,0},{20,4},{24,8},{28,12},{1,17},{... | collective-permute-start | bytes 11528 | tf_op jit(solution)/shard_map/ppermute | solution.py:644
  248.1 14.1 %collective-permute-start.23 = (f32[2,3,160]{2,1,0:T(4,128)}, f32[2,3,160]{2,1,0:T(4,128)S(1)}, u32[]{:S(2)}, u32[]{:S(2)}) collective-permute-start(f32[2,3,160]{2,1,0:T(4,128)} %get-tuple-element.121), channel_id=1, source_target_pairs={{0,20},{4,16},{8,28},{12,24},{16,4},{20,0},{24,12},{28,8},{1,21},{... | collective-permute-start | bytes 11528 | tf_op jit(solution)/shard_map/ppermute | solution.py:644
  262.8 44.7 %collective-permute-start.27 = (bf16[2,288,768]{2,1,0:T(8,128)(2,1)}, bf16[2,288,768]{2,1,0:T(8,128)(2,1)}, u32[]{:S(2)}, u32[]{:S(2)}) collective-permute-start(bf16[2,288,768]{2,1,0:T(8,128)(2,1)} %convert_add_fusion.1), channel_id=1, source_target_pairs={{0,16},{4,20},{8,24},{12,28},{16,0},{20,4},{24,8},{28,12},{1,17},{... | collective-permute-start | bytes 2654216 | tf_op jit(solution)/shard_map/ppermute | solution.py:644
  288.9 23.2 %collective-permute-start.28 = (f32[3,864]{1,0:T(4,128)}, f32[3,864]{1,0:T(4,128)}, u32[]{:S(2)}, u32[]{:S(2)}) collective-permute-start(f32[3,864]{1,0:T(4,128)} %maximum_maximum_fusion), channel_id=1, source_target_pairs={{0,4},{4,0},{8,12},{12,8},{16,20},{20,16},{24,28},{28,24},{1,5},{5... | collective-permute-start | bytes 31112 | tf_op jit(solution)/shard_map/ppermute | solution.py:644
  290.2 21.9 %collective-permute-start.29 = (f32[3,864]{1,0:T(4,128)}, f32[3,864]{1,0:T(4,128)}, u32[]{:S(2)}, u32[]{:S(2)}) collective-permute-start(f32[3,864]{1,0:T(4,128)} %maximum_maximum_fusion), channel_id=1, source_target_pairs={{0,16},{4,20},{8,24},{12,28},{16,0},{20,4},{24,8},{28,12},{1,17},{... | collective-permute-start | bytes 31112 | tf_op jit(solution)/shard_map/ppermute | solution.py:644
  293.1 19.0 %collective-permute-start.30 = (f32[3,864]{1,0:T(4,128)}, f32[3,864]{1,0:T(4,128)}, u32[]{:S(2)}, u32[]{:S(2)}) collective-permute-start(f32[3,864]{1,0:T(4,128)} %maximum_maximum_fusion), channel_id=1, source_target_pairs={{0,20},{4,16},{8,28},{12,24},{16,4},{20,0},{24,12},{28,8},{1,21},{... | collective-permute-start | bytes 31112 | tf_op jit(solution)/shard_map/ppermute | solution.py:644
  304.8 44.0 %collective-permute-start.32 = (bf16[2,288,960]{2,1,0:T(8,128)(2,1)}, bf16[2,288,960]{2,1,0:T(8,128)(2,1)}, u32[]{:S(2)}, u32[]{:S(2)}) collective-permute-start(bf16[2,288,960]{2,1,0:T(8,128)(2,1)} %get-tuple-element.143), channel_id=1, source_target_pairs={{0,4},{4,0},{8,12},{12,8},{16,20},{20,16},{24,28},{28,24},{1,5},{5... | collective-permute-start | bytes 3317768 | tf_op jit(solution)/shard_map/ppermute | solution.py:644
  307.5 10.2 %collective-permute-start.26 = (bf16[1024,288]{0,1:T(8,128)(2,1)S(1)}, bf16[1024,288]{0,1:T(8,128)(2,1)}, u32[]{:S(2)}, u32[]{:S(2)}) collective-permute-start(bf16[1024,288]{0,1:T(8,128)(2,1)S(1)} %copy.19), channel_id=1, source_target_pairs={{0,8},{4,12},{8,0},{12,4},{16,24},{20,28},{24,16},{28,20},{1,9},{5... | collective-permute-start | bytes 1769480 | tf_op jit(solution)/shard_map/ppermute | solution.py:644
  313.0 16.1 %collective-permute-start.31 = (f32[3,288]{1,0:T(4,128)S(1)}, f32[3,288]{1,0:T(4,128)S(1)}, u32[]{:S(2)}, u32[]{:S(2)}) collective-permute-start(f32[3,288]{1,0:T(4,128)S(1)} %pad_maximum_fusion.8), channel_id=1, source_target_pairs={{0,8},{4,12},{8,0},{12,4},{16,24},{20,28},{24,16},{28,20},{1,9},{5... | collective-permute-start | bytes 10376 | tf_op jit(solution)/shard_map/ppermute | solution.py:644
  348.8 14.5 %collective-permute-start.33 = (bf16[2,1024,640]{2,1,0:T(8,128)(2,1)}, bf16[2,1024,640]{2,1,0:T(8,128)(2,1)}, u32[]{:S(2)}, u32[]{:S(2)}) collective-permute-start(bf16[2,1024,640]{2,1,0:T(8,128)(2,1)} %get-tuple-element.151), channel_id=1, source_target_pairs={{0,1},{1,0},{2,3},{3,2},{4,5},{5,4},{6,7},{7,6},{8,9},{9,8},{10,11... | collective-permute-start | bytes 7864328 | tf_op jit(solution)/shard_map/ppermute | solution.py:647
  349.7 12.8 %collective-permute-start.34 = (bf16[288,768]{1,0:T(8,128)(2,1)S(1)}, bf16[288,768]{1,0:T(8,128)(2,1)S(1)}, u32[]{:S(2)}, u32[]{:S(2)}) collective-permute-start(bf16[288,768]{1,0:T(8,128)(2,1)S(1)} %get-tuple-element.153), channel_id=1, source_target_pairs={{0,8},{4,12},{8,0},{12,4},{16,24},{20,28},{24,16},{28,20},{1,9},{5... | collective-permute-start | bytes 1327112 | tf_op jit(solution)/shard_map/ppermute | solution.py:644
  382.5 39.2 %collective-permute-start.35 = (bf16[2,1024,640]{2,1,0:T(8,128)(2,1)}, bf16[2,1024,640]{2,1,0:T(8,128)(2,1)}, u32[]{:S(2)}, u32[]{:S(2)}) collective-permute-start(bf16[2,1024,640]{2,1,0:T(8,128)(2,1)} %get-tuple-element.156), channel_id=1, source_target_pairs={{0,1},{1,0},{2,3},{3,2},{4,5},{5,4},{6,7},{7,6},{8,9},{9,8},{10,11... | collective-permute-start | bytes 7864328 | tf_op jit(solution)/shard_map/ppermute | solution.py:647
  385.3 31.5 %collective-permute-start.37 = (bf16[1024,640]{1,0:T(8,128)(2,1)}, bf16[1024,640]{1,0:T(8,128)(2,1)}, u32[]{:S(2)}, u32[]{:S(2)}) collective-permute-start(bf16[1024,640]{1,0:T(8,128)(2,1)} %join.8), channel_id=1, source_target_pairs={{0,2},{1,3},{2,0},{3,1},{4,6},{5,7},{6,4},{7,5},{8,10},{9,11},{10,... | collective-permute-start | bytes 3932168 | tf_op jit(solution)/shard_map/ppermute | solution.py:647
  386.4 39.1 %collective-permute-start.39 = (bf16[2,288,960]{2,1,0:T(8,128)(2,1)}, bf16[2,288,960]{2,1,0:T(8,128)(2,1)S(1)}, u32[]{:S(2)}, u32[]{:S(2)}) collective-permute-start(bf16[2,288,960]{2,1,0:T(8,128)(2,1)} %get-tuple-element.146), channel_id=1, source_target_pairs={{0,4},{4,0},{8,12},{12,8},{16,20},{20,16},{24,28},{28,24},{1,5},{5... | collective-permute-start | bytes 3317768 | tf_op jit(solution)/shard_map/ppermute | solution.py:644
  394.0 54.4 %collective-permute-start.40 = (bf16[2,288,960]{2,1,0:T(8,128)(2,1)}, bf16[2,288,960]{2,1,0:T(8,128)(2,1)}, u32[]{:S(2)}, u32[]{:S(2)}) collective-permute-start(bf16[2,288,960]{2,1,0:T(8,128)(2,1)} %pad_maximum_fusion.1), channel_id=1, source_target_pairs={{0,16},{4,20},{8,24},{12,28},{16,0},{20,4},{24,8},{28,12},{1,17},{... | collective-permute-start | bytes 3317768 | tf_op jit(solution)/shard_map/ppermute | solution.py:644
  419.9 74.1 %collective-permute-start.38 = (bf16[1024,640]{1,0:T(8,128)(2,1)}, bf16[1024,640]{1,0:T(8,128)(2,1)}, u32[]{:S(2)}, u32[]{:S(2)}) collective-permute-start(bf16[1024,640]{1,0:T(8,128)(2,1)} %join.9), channel_id=1, source_target_pairs={{0,8},{4,12},{8,0},{12,4},{16,24},{20,28},{24,16},{28,20},{1,9},{5... | collective-permute-start | bytes 3932168 | tf_op jit(solution)/shard_map/ppermute | solution.py:644
  424.3 69.7 %collective-permute-start.36 = (bf16[1024,640]{1,0:T(8,128)(2,1)}, bf16[1024,640]{1,0:T(8,128)(2,1)}, u32[]{:S(2)}, u32[]{:S(2)}) collective-permute-start(bf16[1024,640]{1,0:T(8,128)(2,1)} %join.7), channel_id=1, source_target_pairs={{0,2},{1,3},{2,0},{3,1},{4,6},{5,7},{6,4},{7,5},{8,10},{9,11},{10,... | collective-permute-start | bytes 3932168 | tf_op jit(solution)/shard_map/ppermute | solution.py:647
  450.6 36.5 %collective-permute-start.41 = (bf16[288,960]{1,0:T(8,128)(2,1)}, bf16[288,960]{1,0:T(8,128)(2,1)S(1)}, u32[]{:S(2)}, u32[]{:S(2)}) collective-permute-start(bf16[288,960]{1,0:T(8,128)(2,1)} %join.13), channel_id=1, source_target_pairs={{0,8},{4,12},{8,0},{12,4},{16,24},{20,28},{24,16},{28,20},{1,9},{5... | collective-permute-start | bytes 1658888 | tf_op jit(solution)/shard_map/ppermute | solution.py:644
  (19 other events, 187.6 us)

commit v3 on v2

--- a/solution.py
+++ b/solution.py
@@ -14,6 +14,7 @@
 TM = 64
 ROWS = 256
 EDGE = 16
+GAP = 8
 VMEM = 62 << 20
 WIDTHS = (128, 160)
 
@@ -30,8 +31,16 @@
     return jnp.where(pos, r, er), jnp.where(pos, er, r)
 
 
+def group(k, lo, w, count=6):
+    return slice(count * lo + k * w, count * lo + (k + 1) * w)
+
+
 def load_up(ref, rows, lo, w):
     return ref[rows, lo : lo + w].astype(F32)
+
+
+def spread(row, span):
+    return pl.ds(pl.multiple_of(row + row // span * GAP, 8), TM)
 
 
 def cuts(c):
@@ -64,10 +73,11 @@
             v = ref[k].astype(F32)
             mine = jnp.where(low, v[:, :half], v[:, half:])
             other = jnp.where(low, v[:, half:], v[:, :half])
-            at, w = list(offsets(widths))[share]
-            lo = (tap * 3 + k) * w
-            outs[0][:, lo : lo + w] = mine[:, at : at + w].astype(BF)
-            outs[1][:, lo : lo + w] = other[:, at : at + w].astype(BF)
+            at, c = list(offsets(widths))[share]
+            for _, lo, w in cuts(c):
+                to = group(tap * 3 + k, lo, w)
+                outs[0][:, to] = mine[:, at + lo : at + lo + w].astype(BF)
+                outs[1][:, to] = other[:, at + lo : at + lo + w].astype(BF)
 
 
 def pack_weights(widths, share, place, w_now, w_prev):
@@ -200,6 +210,7 @@
             for r in range(ROWS // TM):
                 rows = pl.ds(pl.multiple_of(base + r * TM, TM), TM)
                 full = pl.ds(pl.multiple_of(slot * t + base + r * TM, TM), TM)
+                apart = spread(base + r * TM, t // SEGS)
                 if xrel:
                     flags = xs[full, dl:pad].astype(F32)
                     keep = jnp.concatenate([flags] * (LANES // (pad - dl)), axis=1)
@@ -209,17 +220,17 @@
                 for k_l, lo, w in lanes:
                     g = []
                     for k in range(3):
-                        now = p_s[8 + r * TM : 8 + (r + 1) * TM, k * c + lo : k * c + lo + w]
-                        before = p_s[7 + r * TM : 7 + (r + 1) * TM, (3 + k) * c + lo : (3 + k) * c + lo + w]
+                        now = p_s[8 + r * TM : 8 + (r + 1) * TM, group(k, lo, w)]
+                        before = p_s[7 + r * TM : 7 + (r + 1) * TM, group(3 + k, lo, w)]
                         v = now + keep[:, :w] * before + bias_ref[k : k + 1, lo : lo + w]
                         g_ref[k, full, lo : lo + w] = v
                         g.append(v)
                     f, intake = both(g[1])
                     o, _ = both(g[2])
                     d = keep[:, :w] * f
-                    d_s[slot, k_l, rows, :w] = d
-                    s_s[slot, k_l, rows, :w] = intake * jnp.tanh(g[0])
-                    q_s[slot, k_l, rows, :w] = d * (load_up(up_ref, rows, slot * up_at + lo, w) * o)
+                    d_s[slot, k_l, apart, :w] = d
+                    s_s[slot, k_l, apart, :w] = intake * jnp.tanh(g[0])
+                    q_s[slot, k_l, apart, :w] = d * (load_up(up_ref, rows, slot * up_at + lo, w) * o)
             p_s[7:8, :] = p_s[ROWS + 7 : ROWS + 8, :]
             return 0
 
@@ -229,7 +240,7 @@
     one, zero = jnp.ones((SEGS, LANES), F32), jnp.zeros((SEGS, LANES), F32)
 
     def step(j, carry):
-        at, back = pl.ds(j, SEGS, stride=span), pl.ds(span - 1 - j, SEGS, stride=span)
+        at, back = pl.ds(j, SEGS, stride=span + GAP), pl.ds(span - 1 - j, SEGS, stride=span + GAP)
         new = []
         for (slot, k_l), (pa, ps, pr) in zip(chains, carry):
             d = d_s[slot, k_l, at, :]
@@ -289,9 +300,9 @@
             pltpu.VMEM((2 * EDGE, m * pad), BF),
             pltpu.VMEM((m, pad, width), BF),
             pltpu.VMEM((ROWS + 8, width), F32),
-            pltpu.VMEM((2, lt, t, LANES), F32),
-            pltpu.VMEM((2, lt, t, LANES), F32),
-            pltpu.VMEM((2, lt, t, LANES), F32),
+            pltpu.VMEM((2, lt, t + SEGS * GAP, LANES), F32),
+            pltpu.VMEM((2, lt, t + SEGS * GAP, LANES), F32),
+            pltpu.VMEM((2, lt, t + SEGS * GAP, LANES), F32),
             pltpu.VMEM((3, SEGS, LANES), F32),
             pltpu.SemaphoreType.DMA((max(2, len(x)),)),
             pltpu.SemaphoreType.DMA((max(1, len(x)),)),
@@ -316,13 +327,14 @@
         def act(r, _, slot=slot):
             rows = pl.ds(pl.multiple_of(r * TM, TM), TM)
             full = pl.ds(pl.multiple_of(slot * t + r * TM, TM), TM)
+            apart = spread(r * TM, span)
             for k_l, lo, w in lanes:
                 ch = slice(lo, lo + w)
                 f, i = both(g_ref[1, full, ch])
                 o, _ = both(g_ref[2, full, ch])
-                d_s[slot, k_l, rows, :w] = keep_ref[full, :w] * f
-                s_s[slot, k_l, rows, :w] = i * jnp.tanh(g_ref[0, full, ch])
-                q_s[slot, k_l, rows, :w] = load_up(ups[slot], rows, slot * up_at + lo, w) * o
+                d_s[slot, k_l, apart, :w] = keep_ref[full, :w] * f
+                s_s[slot, k_l, apart, :w] = i * jnp.tanh(g_ref[0, full, ch])
+                q_s[slot, k_l, apart, :w] = load_up(ups[slot], rows, slot * up_at + lo, w) * o
             return 0
 
         lax.fori_loop(0, t // TM, act, 0)
@@ -354,7 +366,7 @@
     chains = [(slot, k_l) for slot in range(2) for k_l, _, _ in lanes]
 
     def step(j, carry):
-        at, back = pl.ds(j, SEGS, stride=span), pl.ds(span - 1 - j, SEGS, stride=span)
+        at, back = pl.ds(j, SEGS, stride=span + GAP), pl.ds(span - 1 - j, SEGS, stride=span + GAP)
         new = []
         for (slot, k_l), (h, r) in zip(chains, carry):
             dh = d_s[slot, k_l, at, :] * h
@@ -377,6 +389,7 @@
             r = t // TM - 1 - i
             rows = pl.ds(pl.multiple_of(r * TM, TM), TM)
             full = pl.ds(pl.multiple_of(slot * t + r * TM, TM), TM)
+            apart = spread(r * TM, span)
             last = lax.broadcasted_iota(jnp.int32, (TM, LANES), 0) == TM - 1
             new, first = [], []
             for k_l, lo, w in lanes:
@@ -385,20 +398,20 @@
                 o, cl = both(g_ref[2, full, ch])
                 z = jnp.tanh(g_ref[0, full, ch])
                 keep = keep_ref[full, :w]
-                gs = q_s[slot, k_l, rows, :w]
-                oh = o * s_s[slot, k_l, rows, :w]
+                gs = q_s[slot, k_l, apart, :w]
+                oh = o * s_s[slot, k_l, apart, :w]
                 hids[slot][rows, ch] = oh.astype(BF)
                 gi = gs * intake
                 grads = (
                     gi * (1.0 - z * z),
-                    gi * (p_s[slot, k_l, rows, :w] - f * z),
+                    gi * (p_s[slot, k_l, apart, :w] - f * z),
                     load_up(ups[slot], rows, slot * up_at + lo, w) * oh * cl,
                 )
                 for k, v in enumerate(grads):
-                    gg_ref[full, k * c + lo : k * c + lo + w] = v.astype(BF)
+                    gg_ref[full, group(k, lo, w)] = v.astype(BF)
                     kept = keep * v
                     moved = jnp.where(last[:, :w], nxt[len(new)], pltpu.roll(kept, TM - 1, 0))
-                    gg_ref[full, (3 + k) * c + lo : (3 + k) * c + lo + w] = moved.astype(BF)
+                    gg_ref[full, group(3 + k, lo, w)] = moved.astype(BF)
                     first.append(kept[:1])
                     new.append(acc[len(new)] + jnp.sum(v.reshape(TM // 8, 8, w), axis=0))
             return tuple(new), tuple(first)
@@ -407,8 +420,8 @@
         sums, firsts = lax.fori_loop(0, t // TM, out, (tuple(sums), zeros))
         for k_l, lo, w in lanes:
             for k in range(3):
-                gf_ref[slot : slot + 1, k * c + lo : k * c + lo + w] = firsts[3 * k_l + k]
-                gp_ref[slot * EDGE : slot * EDGE + EDGE, (3 + k) * c + lo : (3 + k) * c + lo + w] = jnp.where(
+                gf_ref[slot : slot + 1, group(k, lo, w, 3)] = firsts[3 * k_l + k]
+                gp_ref[slot * EDGE : slot * EDGE + EDGE, group(3 + k, lo, w)] = jnp.where(
                     top[:, :w], firsts[3 * k_l + k], 0.0
                 ).astype(BF)
     for k_l, lo, w in lanes:
@@ -431,106 +444,118 @@
             shape((2 * EDGE, 6 * c), BF),
             shape((1, 3 * c), F32),
         ],
-        scratch_shapes=[pltpu.VMEM((2, lt, t, LANES), F32)] * 4 + [pltpu.VMEM((2, 2, lt, SEGS, LANES), F32)],
+        scratch_shapes=[pltpu.VMEM((2, lt, t + SEGS * GAP, LANES), F32)] * 4 + [pltpu.VMEM((2, 2, lt, SEGS, LANES), F32)],
         compiler_params=params(),
         cost_estimate=TINY,
         name="finish",
     )(place, gates, *ups, keep_w, seg, every)
 
 
-def wgrad_kernel(dw, place, x_ref, halo_ref, gg_ref, gp_ref, here_ref, away_ref, acc):
+def wgrad_kernel(dw, place, x_ref, halo_ref, gg_ref, gp_ref, *refs):
+    *outs, acc = refs
     over_tokens = (((0,), (0,)), ((), ()))
     v = lax.dot_general(x_ref[...], gg_ref[...], over_tokens, preferred_element_type=F32)
     acc[...] = v + lax.dot_general(halo_ref[...], gp_ref[...], over_tokens, preferred_element_type=F32)
     p = place[2]
-    here_ref[0] = acc[pl.ds(pl.multiple_of(p * dw, 16), dw), :].astype(BF)
-    away_ref[0] = acc[pl.ds(pl.multiple_of((1 - p) * dw, 16), dw), :].astype(BF)
-
-
-def weight_grads(heads, kh, dw, pad, place, x_all, halo, gg, gp):
+    step = pl.program_id(0)
+    for k in range(len(outs) // 2):
+
+        @pl.when(step // 2 == k)
+        def _(k=k):
+            outs[2 * k][0] = acc[pl.ds(pl.multiple_of(p * dw, 16), dw), :].astype(BF)
+            outs[2 * k + 1][0] = acc[pl.ds(pl.multiple_of((1 - p) * dw, 16), dw), :].astype(BF)
+
+
+def weight_grads(heads, dw, pad, place, x_all, halo, gg, gp):
     width = gg.shape[1]
 
     def lanes(i, at):
-        return (0, lax.rem(at[0] + kh, heads) * 2 + (at[1] ^ (1 - i)))
+        kh = lax.rem(i // 2 + 1, heads)
+        return (0, lax.rem(at[0] + kh, heads) * 2 + (at[1] ^ (1 - lax.rem(i, 2))))
+
+    def out(k):
+        return pl.BlockSpec((1, dw, width), lambda i, at: (jnp.clip(i - 2 * k, 0, 1), 0, 0))
 
     whole = lambda i, at: (0, 0)
-    return pl.pallas_call(
+    res = pl.pallas_call(
         functools.partial(wgrad_kernel, dw),
         grid_spec=pltpu.PrefetchScalarGridSpec(
             num_scalar_prefetch=1,
-            grid=(2,),
+            grid=(2 * heads,),
             in_specs=[
                 pl.BlockSpec((x_all.shape[0], pad), lanes),
                 pl.BlockSpec((halo.shape[0], pad), lanes),
                 pl.BlockSpec(gg.shape, whole),
                 pl.BlockSpec(gp.shape, whole),
             ],
-            out_specs=[pl.BlockSpec((1, dw, width), lambda i, at: (i, 0, 0))] * 2,
+            out_specs=[out(k) for k in range(heads) for _ in range(2)],
             scratch_shapes=[pltpu.VMEM((pad, width), F32)],
         ),
-        out_shape=[jax.ShapeDtypeStruct((2, dw, width), BF)] * 2,
+        out_shape=[jax.ShapeDtypeStruct((2, dw, width), BF)] * (2 * heads),
         compiler_params=params(),
         cost_estimate=TINY,
         name="weight_grads",
     )(place, x_all, halo, gg, gp)
-
-
-def xgrad_kernel(slot, place, *refs):
-    count = (len(refs) - 3) // 4
+    return [((k + 1) % heads, res[2 * k], res[2 * k + 1]) for k in range(heads)]
+
+
+def xgrad_kernel(place, *refs):
+    count = (len(refs) - 5) // 4
     gg_in, nx, w_in = refs[:count], refs[count : 2 * count], refs[2 * count : 3 * count]
-    send_ref, keep_ref = refs[3 * count : 3 * count + 2]
-    gg_s, sem = refs[3 * count + 2 : 4 * count + 2], refs[4 * count + 2]
-    i = pl.program_id(0)
-    t = gg_s[0].shape[0]
-
-    @pl.when(i == 0)
+    outs = refs[3 * count : 3 * count + 4]
+    gg_s, sem = refs[3 * count + 4 : 4 * count + 4], refs[4 * count + 4]
+    i, turn = pl.program_id(0), pl.program_id(1)
+    t = gg_s[0].shape[0] // 2
+
+    @pl.when((i == 0) & (turn == 0))
     def _():
-        copies = [
-            pltpu.make_async_copy(gg_in[k].at[pl.ds(slot * t, t)], gg_s[k], sem.at[k]) for k in range(count)
-        ]
+        copies = [pltpu.make_async_copy(gg_in[k], gg_s[k], sem.at[k]) for k in range(count)]
         for copy in copies:
             copy.start()
         for k, copy in enumerate(copies):
             copy.wait()
-            c3 = nx[k].shape[1]
-            old = gg_s[k][t - EDGE :, c3:].astype(F32)
-            last = lax.broadcasted_iota(jnp.int32, (EDGE, c3), 0) == EDGE - 1
-            gg_s[k][t - EDGE :, c3:] = jnp.where(last, nx[k][slot : slot + 1, :], old).astype(BF)
-
+            for _, lo, w in cuts(nx[k].shape[1] // 3):
+                last = lax.broadcasted_iota(jnp.int32, (EDGE, 3 * w), 0) == EDGE - 1
+                there = slice(6 * lo + 3 * w, 6 * lo + 6 * w)
+                for slot in range(2):
+                    rows = slice((slot + 1) * t - EDGE, (slot + 1) * t)
+                    old = gg_s[k][rows, there].astype(F32)
+                    new = nx[k][slot : slot + 1, 3 * lo : 3 * lo + 3 * w]
+                    gg_s[k][rows, there] = jnp.where(last, new, old).astype(BF)
+
+    rows = pl.ds(pl.multiple_of((1 - turn) * t, t), t)
     v = 0.0
     for k in range(count):
-        v = v + lax.dot_general(gg_s[k][...], w_in[k][0], (((1,), (1,)), ((), ())), preferred_element_type=F32)
-
-    @pl.when(i < 2)
-    def _():
-        send_ref[0] = v.astype(BF)
-
-    @pl.when(i >= 2)
-    def _():
-        keep_ref[0] = v.astype(BF)
-
-
-def input_grads(slot, place, ggs, nexts, ws):
+        v = v + lax.dot_general(
+            gg_s[k][rows, :], w_in[k][0], (((1,), (1,)), ((), ())), preferred_element_type=F32
+        )
+    v = v.astype(BF)
+    for k in range(4):
+
+        @pl.when((turn == k // 2) & ((i < 2) == (k % 2 == 0)))
+        def _(k=k):
+            outs[k][0] = v
+
+
+def input_grads(place, ggs, nexts, ws):
     count = len(ggs)
     t = ggs[0].shape[0] // 2
     m, pad, _ = ws[0].shape
     order = lambda i: jnp.where(i < 2, 2 * i + 1, 2 * i - 4)
+    sent = pl.BlockSpec((1, t, pad), lambda i, turn, at: (jnp.minimum(i, 1), 0, 0))
+    kept = pl.BlockSpec((1, t, pad), lambda i, turn, at: (jnp.maximum(i - 2, 0), 0, 0))
     return pl.pallas_call(
-        functools.partial(xgrad_kernel, slot),
+        xgrad_kernel,
         grid_spec=pltpu.PrefetchScalarGridSpec(
             num_scalar_prefetch=1,
-            grid=(m,),
+            grid=(m, 2),
             in_specs=[ANY_SPEC] * count
-            + [pl.BlockSpec(v.shape, lambda i, at: (0, 0)) for v in nexts]
-            + [pl.BlockSpec((1, pad, w.shape[2]), lambda i, at: (order(i), 0, 0)) for w in ws],
-            out_specs=[
-                pl.BlockSpec((1, t, pad), lambda i, at: (jnp.minimum(i, 1), 0, 0)),
-                pl.BlockSpec((1, t, pad), lambda i, at: (jnp.maximum(i - 2, 0), 0, 0)),
-            ],
-            scratch_shapes=[pltpu.VMEM((t, gg.shape[1]), BF) for gg in ggs]
-            + [pltpu.SemaphoreType.DMA((count,))],
+            + [pl.BlockSpec(v.shape, lambda i, turn, at: (0, 0)) for v in nexts]
+            + [pl.BlockSpec((1, pad, w.shape[2]), lambda i, turn, at: (order(i), 0, 0)) for w in ws],
+            out_specs=[sent, kept, sent, kept],
+            scratch_shapes=[pltpu.VMEM(gg.shape, BF) for gg in ggs] + [pltpu.SemaphoreType.DMA((count,))],
         ),
-        out_shape=[jax.ShapeDtypeStruct((2, t, pad), BF)] * 2,
+        out_shape=[jax.ShapeDtypeStruct((2, t, pad), BF)] * 4,
         compiler_params=params(),
         cost_estimate=TINY,
         name="input_grads",
@@ -575,10 +600,10 @@
     for tap in range(2):
         for k in range(3):
             mine, other = [], []
-            for i, w in enumerate(widths):
-                lo = (tap * 3 + k) * w
-                mine.append(refs[2 * i][:, lo : lo + w].astype(F32))
-                other.append(refs[2 * i + 1][:, lo : lo + w].astype(F32))
+            for i, c in enumerate(widths):
+                for _, lo, w in cuts(c):
+                    mine.append(refs[2 * i][:, group(tap * 3 + k, lo, w)].astype(F32))
+                    other.append(refs[2 * i + 1][:, group(tap * 3 + k, lo, w)].astype(F32))
             mine, other = jnp.concatenate(mine, axis=1), jnp.concatenate(other, axis=1)
             outs[tap][k] = jnp.concatenate([jnp.where(low, mine, other), jnp.where(low, other, mine)], axis=1)
 
@@ -680,18 +705,19 @@
     y0 = gate_to(x0, 1, 0)
     x1 = seq_to(after(x0, near), 0, 1, 0)
     first_p = got[0][0, 1]
-    c0, cy0 = gate_to(after(x0, y0, first_p), 0, 1), gate_to(after(y0, first_p), 0, 1)
     up_packed = pack_up(widths, place, after(grad_out, x0))
-    ups = [[up_packed[0], seq_to(after(up_packed[1], first_p), 0, 1, 0)]]
-    x1_here = after(x1, c0, cy0)
+    ups = [[up_packed[0], seq_to(after(up_packed[1], near), 0, 1, 0)]]
+    hop = [got[0][kh, 0] for kh in range(1, heads)]
+    c0, cy0 = gate_to(after(x0, y0, first_p, *hop), 0, 1), gate_to(after(y0, first_p, *hop), 0, 1)
+    x1_here = after(x1, y0, first_p)
     y1, c1 = gate_to(x1_here, 1, 0), gate_to(x1_here, 0, 1)
-    finish_share(got[0], c1)
+    finish_share(got[0])
     for i in range(1, count):
         packed = pack_weights(widths, i, place, after(w_now, near), w_prev)
-        near = seq_to(after(packed[1], c0, cy0, x1), 0, 1, 0)
+        near = seq_to(packed[1], 0, 1, 0)
         got.append(share_w(jnp.stack([packed[0], near]), c1, *[got[i - 1][kh, 0] for kh in range(1, heads)]))
         ups.append([up_packed[2 * i], seq_to(after(up_packed[2 * i + 1], near), 0, 1, 0)])
-    cy1 = gate_to(after(y1, ups[0][1]), 0, 1)
+    cy1 = gate_to(after(y1, ups[0][1], *[got[0][kh, 1] for kh in range(1, heads)]), 0, 1)
     xs = {(0, 0, 0): x0, (0, 1, 0): y0, (0, 0, 1): c0, (0, 1, 1): cy0}
     xs |= {(1, 0, 0): x1, (1, 1, 0): y1, (1, 0, 1): c1, (1, 1, 1): cy1}
     hidden_mine, hidden_other, grads, wide_w, g_first, g_bias, w_pairs = [], [], [], [], [], [], []
@@ -701,11 +727,7 @@
 
     def weight_parts(gg, gp, *needs):
         if dw % 16 == 0 and n == 2 * m:
-            parts = [
-                (kh, *weight_grads(heads, kh, dw, pad, place, x_all, halo, gg, gp)) for kh in range(1, heads)
-            ]
-            gp = after(gp, parts[-1][1], *needs)
-            return parts + [(0, *weight_grads(heads, 0, dw, pad, place, x_all, halo, gg, gp))]
+            return weight_grads(heads, dw, pad, place, x_all, halo, gg, after(gp, *needs) if needs else gp)
         dots = jnp.einsum("td,tn->dn", x_all, gg, preferred_element_type=F32)
         dots = dots + jnp.einsum("td,tn->dn", halo, gp, preferred_element_type=F32)
         v = dots.astype(BF).reshape(m, pad, -1)[:, :dl].reshape(heads, 2, 2, dw, gg.shape[1])
@@ -735,7 +757,7 @@
         dims = (n, m, dw, dl, t, c)
         bias_i = half_bias[:, at : at + c]
         if i > 0:
-            finish_share(got[i], every)
+            finish_share(got[i], every, ups[i][1])
         w_in, wrel = weights_in(got[i], c)
         if i == 0:
             xrel = list(xs)
@@ -747,7 +769,7 @@
             gates, seg, tot, w_rel = gates_and_totals(
                 dims, 0, place, w_in, wrel, [x_all, halo], [], bias_i, ups[i], keep_w
             )
-        every = spread_totals(tot)
+        every = spread_totals(after(tot, *[g[0, 1] for g in got[i + 1 : i + 2]]) if i + 1 < count else tot)
         wide_w.append(w_rel)
         if i > 0:
             sums = over_p(waiting, tot)
@@ -758,23 +780,23 @@
         hidden_other.append(h1)
         g_first.append(gf)
         g_bias.append(gb)
-        needs = []
         if i == count - 1:
             parts = jnp.concatenate([jnp.concatenate(g_first, axis=1), jnp.concatenate(g_bias, axis=1)], axis=0)
-            came = [parts if r == (0, 0) else seq_to(parts, r[0], 0, r[1]) for r in group]
+            around = [parts if r == (0, 0) else seq_to(parts, r[0], 0, r[1]) for r in group]
             hidden_came = seq_to(after(jnp.concatenate(hidden_other, axis=1), parts), 0, 1, 0)
+        needs = list(around) if i == count - 1 else []
         if i > 0:
-            total = over_h(waiting, h_sums, gg)
+            total = over_h(waiting, h_sums)
             needs.append(total)
-        if i == count - 1:
-            came = [after(v, *needs) for v in came]
-            around = jnp.stack(came)
-            needs += [around, hidden_came]
-        waiting_next = weight_parts(gg, gp, *needs)
+        waiting_next = weight_parts(gg, gp)
+        if needs:
+            waiting_next = [(kh, here, after(away, *needs)) for kh, here, away in waiting_next]
         if i > 0:
-            w_pairs += [total[1], seq_to(after(total[0], waiting_next[-1][1]), 0, 1, 0)]
+            w_pairs += [total[1], seq_to(total[0], 0, 1, 0)]
         waiting = waiting_next
         grads.append(gg)
+    around = jnp.stack(around)
+
     full_bias = jnp.sum(around[:, 2], axis=0)
     nexts = []
     for slot in range(2):
@@ -793,27 +815,25 @@
         at += 3 * c
     bias_half = jnp.concatenate(bias_half, axis=1)
     bias_other = seq_to(bias_half, 0, 1, 0)
-    nexts[0] = after(nexts[0], bias_other, *[v[2] for v in waiting])
-    sent1, kept1 = input_grads(1, place, grads, nexts, wide_w)
-
+    nexts[0] = after(nexts[0], *[v[2] for v in waiting])
+    sent1, kept1, sent0, kept0 = input_grads(place, grads, nexts, wide_w)
     p_came = []
     for v in waiting:
         p_came.append(after(seq_to(v[2], 0, 0, 1), *p_came[-1:]))
-    c_came1 = gate_to(after(sent1, p_came[0]), 0, 1)
-    nexts[0] = after(nexts[0], c_came1, *w_pairs)
+    sent1, sent0, *_ = lax.optimization_barrier((sent1, sent0, p_came[0], hidden_came, bias_other, *w_pairs))
+    c_came1, c_came0 = gate_to(sent1, 0, 1), gate_to(sent0, 0, 1)
     h_came = []
     for k, (kh, here, _) in enumerate(waiting[:-1]):
-        both_l = jnp.stack([join([(here, d), (p_came[k], d)], URGENT) for d in range(2)])
+        both_l = (here.astype(F32) + p_came[k].astype(F32)).astype(BF)
+        c_came1 = after(c_came1, both_l)
         h_came.append(seq_to(both_l, kh, 0, 0))
-    y_came1 = gate_to(join([(kept1, 1), (c_came1, 1)], URGENT), 1, 0)
-    sent0, kept0 = input_grads(0, place, grads, nexts, wide_w)
-    c_came0 = gate_to(sent0, 0, 1)
-    l_came = seq_to(join([(kept1, 0), (c_came1, 0), (y_came1, None)], URGENT), 0, 1, 0)
+    y_came1 = gate_to(join([(kept1, 1), (c_came1, 1)], LATER), 1, 0)
+    y_came0 = gate_to(join([(kept0, 1), (c_came0, 1)], LATER), 1, 0)
+    l_came = seq_to(join([(kept1, 0), (c_came1, 0), (y_came1, None)], LATER), 0, 1, 0)
     total = [
         join([(waiting[-1][1], d), (p_came[-1], d)] + [(v, d) for v in h_came], LATER) for d in range(2)
     ]
     w_pairs += [total[1], seq_to(total[0], 0, 1, 0)]
-    y_came0 = gate_to(join([(kept0, 1), (c_came0, 1)], 1), 1, 0)
     grad_x = kept0[0].astype(F32) + c_came0[0].astype(F32) + y_came0.astype(F32) + l_came.astype(F32)
     grad_x = grad_x[:, :dl].astype(BF)
 

time: 499 us -> 431 us (0.86)
  Pallas kernels: 210 us -> 173 us
  waiting for transfers between devices: 195 us -> 167 us
    ppermute x31, waiting for transfers between devices: 174 us -> 131 us  [seq_to(): return lax.ppermute(v, 'seq', route)]
    ppermute x10, waiting for transfers between devices: 20.9 us -> 35.1 us  [gate_to(): return lax.ppermute(v, 'gate', [(i, i ^ d_a * 2 + d_b) for i in range(m)])]
    pallas_call x2, Pallas kernels: 57.3 us -> 46.9 us  [gates_and_totals(): pl.pallas_call(functools.partial(gates_kernel, plan), in_specs=[SMEM_SPEC...]
    pallas_call x2, Pallas kernels: 35.4 us -> 25 us  [finish(): pl.pallas_call(functools.partial(finish_kernel, n, up_at), in_specs=[SMEM...]
    pallas_call x4 -> x2, Pallas kernels: 41.9 us -> 34 us  [weight_grads(): pl.pallas_call(functools.partial(wgrad_kernel, dw), grid_spec=pltpu.Prefe...]
    pallas_call x2 -> x1, Pallas kernels: 38.8 us -> 34.2 us  [input_grads(): pl.pallas_call(xgrad_kernel, grid_spec=pltpu.PrefetchScalarGridSpec(num_s...]
    pallas_call x7 -> x5, Pallas kernels: 17.1 us -> 13 us  [join(): pl.pallas_call(join_kernel, grid=(steps,), in_specs=[spec(v, at) for v, a...]
    unnamed x53 -> x43, local copies, waits for them, and re-layouts: 11.1 us -> 7.53 us
  transfers between devices with their start and end apart: 42 -> 42, of which waited for: 14 -> 17; matrix products, arithmetic and copies ran while one was open for 6% -> 7% of each run, Pallas kernels for 38% -> 40%
where the time goes in v3:
time: 431 us; the launch traced here: 430 us
  Pallas kernels  173 us (40%)
  waiting for transfers between devices  167 us (39%)
  starting transfers between devices  51 us (12%)
  other arithmetic  21.9 us (5%)
  local copies, waits for them, and re-layouts  15.2 us (4%)
    ppermute x31, waiting for transfers between devices, seq_to(): return lax.ppermute(v, 'seq', route)  131 us
    pallas_call x2, Pallas kernels, gates_and_totals(): pl.pallas_call(functools.partial(gates_kernel, plan), in_specs=[SMEM_SPEC...  46.9 us
    ppermute x31, starting transfers between devices, seq_to(): return lax.ppermute(v, 'seq', route)  42.9 us
    ppermute x10, waiting for transfers between devices, gate_to(): return lax.ppermute(v, 'gate', [(i, i ^ d_a * 2 + d_b) for i in range(m)])  35.1 us
    pallas_call x1, Pallas kernels, input_grads(): pl.pallas_call(xgrad_kernel, grid_spec=pltpu.PrefetchScalarGridSpec(num_s...  34.2 us
    pallas_call x2, Pallas kernels, weight_grads(): pl.pallas_call(functools.partial(wgrad_kernel, dw), grid_spec=pltpu.Prefe...  34 us
    pallas_call x2, Pallas kernels, finish(): pl.pallas_call(functools.partial(finish_kernel, n, up_at), in_specs=[SMEM...  25 us
    pallas_call x5, Pallas kernels, join(): pl.pallas_call(join_kernel, grid=(steps,), in_specs=[spec(v, at) for v, a...  13 us
  transfers between devices with their start and end apart: 42, of which 17 were waited for; matrix products, arithmetic and copies ran while one was open for 7% of the time, Pallas kernels for 40%

profile of v3, /device:TPU:0, one launch (start us, length us, event | category | flops | bytes accessed | tf_op | source)
XLA Modules:
  0.0 429.9 jit_solution(1940942400081033006)
XLA Ops:
  1.4 3.3 pack_weights.2
  4.7 3.0 collective-permute-start
  8.5 3.4 collective-permute-start.4
  15.2 2.9 collective-permute-done
  18.1 4.8 %collective-permute-start.8 = (bf16[1040,640]{1,0:T(8,128)(2,1)S(1)}, bf16[1040,640]{1,0:T(8,128)(2,1)}, u32[]{:S(2)}, u32[]{:S(2)}) collective-permute-start(bf16[1040,640]{1,0:T(8,128)(2,1)S(1)} %fusion.6.refs_4_), channel_id=1, source_target_pairs={{0,8},{4,12},{8,0},{12,4},{16,24},{20,28},{24,16},{28,20},{1,9},{5... | collective-permute-start | bytes 3993608 | tf_op jit(solution)/shard_map/ppermute | solution.py:669
  23.0 2.7 collective-permute-start.2
  25.7 17.0 %collective-permute-done.1.refs_1_ = bf16[2,288,768]{2,1,0:T(8,128)(2,1)S(1)} collective-permute-done((bf16[2,288,768]{2,1,0:T(8,128)(2,1)S(1)}, bf16[2,288,768]{2,1,0:T(8,128)(2,1)S(1)}, u32[]{:S(2)}, u32[]{:S(2)}) %collective-permute-start.1) | collective-permute-done | bytes 884768 | tf_op jit(solution)/shard_map/ppermute | solution.py:669
  43.5 26.2 %collective-permute-done.8.refs_8_ = bf16[1040,640]{1,0:T(8,128)(2,1)} collective-permute-done((bf16[1040,640]{1,0:T(8,128)(2,1)S(1)}, bf16[1040,640]{1,0:T(8,128)(2,1)}, u32[]{:S(2)}, u32[]{:S(2)}) %collective-permute-start.8) | collective-permute-done | bytes 1331232 | tf_op jit(solution)/shard_map/ppermute | solution.py:669
  72.0 5.0 %pack_up.1 = (bf16[1024,128]{1,0:T(8,128)(2,1)}, bf16[1024,128]{1,0:T(8,128)(2,1)}, bf16[1024,160]{1,0:T(8,128)(2,1)}, bf16[1024,256]{1,0:T(8,128)(2,1)}) custom-call(s32[5]{0:T(128)} %stack.91.place, bf16[1024,576]{1,0:T(8,128)(2,1)} %copy.18.up_ref), custom_call_target="tpu_custom_call" | custom-call | flops 1024 | bytes 1024 | tf_op jit(solution)/shard_map/pack_up/pallas_call | solution.py:114
  77.0 2.0 collective-permute-start.11
  78.9 4.0 pack_weights.3
  83.0 3.3 collective-permute-done.11.refs_14_.up1
  86.3 6.4 %collective-permute-done.3.refs_3_ = bf16[2,288,768]{2,1,0:T(8,128)(2,1)} collective-permute-done((bf16[2,288,768]{2,1,0:T(8,128)(2,1)}, bf16[2,288,768]{2,1,0:T(8,128)(2,1)}, u32[]{:S(2)}, u32[]{:S(2)}) %collective-permute-start.3) | collective-permute-done | bytes 884768 | tf_op jit(solution)/shard_map/ppermute | solution.py:669
  92.7 6.2 %collective-permute-done.9.refs_9_ = bf16[1040,640]{1,0:T(8,128)(2,1)} collective-permute-done((bf16[1040,640]{1,0:T(8,128)(2,1)}, bf16[1040,640]{1,0:T(8,128)(2,1)}, u32[]{:S(2)}, u32[]{:S(2)}) %collective-permute-start.9) | collective-permute-done | bytes 1331232 | tf_op jit(solution)/shard_map/ppermute | solution.py:672
  98.9 2.2 pad_maximum_fusion.refs_0_
  102.2 2.6 collective-permute-start.18
  104.8 1.8 collective-permute-start.19
  108.4 20.2 %gates_and_totals.2 = (f32[3,2048,128]{2,1,0:T(8,128)}, f32[2,3,8,128]{3,2,1,0:T(8,128)}, f32[2,3,128]{2,1,0:T(4,128)}, bf16[2048,2560]{1,0:T(8,128)(2,1)}, bf16...) custom-call(s32[5]{0:T(128)} %stack.91.place, bf16[2,288,768]{2,1,0:T(8,128)(2,1)} %copy-done.2, ...), custom_call_target="tpu_custom_call" | custom-call | flops 1024 | bytes 1024 | tf_op jit(solution)/shard_map/gates_and_totals/pallas_call | solution.py:293
  130.5 2.3 collective-permute-start.16
  134.2 22.2 %collective-permute-done.16 = f32[2,3,128]{2,1,0:T(4,128)S(1)} collective-permute-done((f32[2,3,128]{2,1,0:T(4,128)}, f32[2,3,128]{2,1,0:T(4,128)S(1)}, u32[]{:S(2)}, u32[]{:S(2)}) %collective-permute-start.16) | collective-permute-done | bytes 3104 | tf_op jit(solution)/shard_map/ppermute | solution.py:669
  159.5 8.7 %finish.2 = (bf16[1024,128]{1,0:T(8,128)(2,1)}, bf16[1024,128]{1,0:T(8,128)(2,1)}, bf16[2048,768]{1,0:T(8,128)(2,1)}, f32[2,384]{1,0:T(2,128)}, bf16[32,768]{1,0:T(8,128)(2,1)}, /*index=5*/f32[1,384]{1,0:T(1,128)}) custom-call(s32[5]{0:T(128)} %stack.91.place, f32[3,2048,128]{2,1,0:T(8,128)} %get-tuple-element.89.g_ref, ...), custom_call_target="tpu_custom_call" | custom-call | flops 1024 | bytes 1024 | tf_op jit(solution)/shard_map/finish/pallas_call | solution.py:436
  168.2 15.2 %weight_grads.2 = (bf16[2,288,768]{2,1,0:T(8,128)(2,1)}, bf16[2,288,768]{2,1,0:T(8,128)(2,1)}, bf16[2,288,768]{2,1,0:T(8,128)(2,1)}, bf16[2,288,768]{2,1,0:T(8,128)(2,1)}) custom-call(s32[5]{0:T(128)} %stack.91.place, bf16[2048,2560]{1,0:T(8,128)(2,1)} %get-tuple-element.98.x_ref.refs_4_, bf16[32,2560]{1,0:T(8,128)(2,1)} %get-tuple-element.99.halo_ref.refs_5_, ...), custom_call_target="tpu_custom_call" | custom-call | flops 1024 | bytes 1024 | tf_op jit(solution)/shard_map/weight_grads/pallas_call | solution.py:480
  188.1 26.7 %gates_and_totals.3 = (f32[3,2048,160]{2,1,0:T(8,128)}, f32[2,3,8,160]{3,2,1,0:T(8,128)}, f32[2,3,160]{2,1,0:T(4,128)}, bf16[4,640,960]{2,1,0:T(8,128)(2,1)}) custom-call(s32[5]{0:T(128)} %stack.91.place, bf16[2,288,960]{2,1,0:T(8,128)(2,1)} %pad_maximum_fusion.refs_0_, bf16[2,288,960]{2,1,0:T(8,128)(2,1)} %collective-permute-done.14.refs_1_, ...), custom_call_target="tpu_custom_call" | custom-call | flops 1024 | bytes 1024 | tf_op jit(solution)/shard_map/gates_and_totals/pallas_call | solution.py:293
  215.7 3.5 collective-permute-start.23
  219.2 2.6 convert_add_fusion.1
  221.9 2.8 collective-permute-done.21
  226.6 16.4 %finish.3 = (bf16[1024,160]{1,0:T(8,128)(2,1)}, bf16[1024,160]{1,0:T(8,128)(2,1)}, bf16[2048,960]{1,0:T(8,128)(2,1)}, f32[2,480]{1,0:T(2,128)}, bf16[32,960]{1,0:T(8,128)(2,1)}, /*index=5*/f32[1,480]{1,0:T(1,128)}) custom-call(s32[5]{0:T(128)} %stack.91.place, f32[3,2048,160]{2,1,0:T(8,128)} %get-tuple-element.110.g_ref, ...), custom_call_target="tpu_custom_call" | custom-call | flops 1024 | bytes 1024 | tf_op jit(solution)/shard_map/finish/pallas_call | solution.py:436
  245.2 2.9 collective-permute-start.28
  251.0 4.5 %collective-permute-start.26 = (bf16[1024,288]{0,1:T(8,128)(2,1)}, bf16[1024,288]{0,1:T(8,128)(2,1)}, u32[]{:S(2)}, u32[]{:S(2)}) collective-permute-start(bf16[1024,288]{0,1:T(8,128)(2,1)} %copy.19), channel_id=1, source_target_pairs={{0,8},{4,12},{8,0},{12,4},{16,24},{20,28},{24,16},{28,20},{1,9},{5... | collective-permute-start | bytes 1769480 | tf_op jit(solution)/shard_map/ppermute | solution.py:669
  255.5 18.8 %weight_grads.3 = (bf16[2,288,960]{2,1,0:T(8,128)(2,1)}, bf16[2,288,960]{2,1,0:T(8,128)(2,1)}, bf16[2,288,960]{2,1,0:T(8,128)(2,1)}, bf16[2,288,960]{2,1,0:T(8,128)(2,1)}) custom-call(s32[5]{0:T(128)} %stack.91.place, bf16[2048,2560]{1,0:T(8,128)(2,1)} %get-tuple-element.98.x_ref.refs_4_, bf16[32,2560]{1,0:T(8,128)(2,1)} %get-tuple-element.99.halo_ref.refs_5_, ...), custom_call_target="tpu_custom_call" | custom-call | flops 1024 | bytes 1024 | tf_op jit(solution)/shard_map/weight_grads/pallas_call | solution.py:480
  278.4 2.0 collective-permute-start.32
  281.6 34.2 %input_grads.1 = (bf16[2,1024,640]{2,1,0:T(8,128)(2,1)}, bf16[2,1024,640]{2,1,0:T(8,128)(2,1)}, bf16[2,1024,640]{2,1,0:T(8,128)(2,1)}, bf16[2,1024,640]{2,1,0:T(8,128)(2,1)}) custom-call(s32[5]{0:T(128)} %stack.91.place, bf16[2048,768]{1,0:T(8,128)(2,1)} %get-tuple-element.100.gg_ref.refs_0_, bf16[2048,960]{1,0:T(8,128)(2,1)} %get-tuple-element.126.gg_ref.refs_1_, ...), custom_call_target="tpu_custom_call" | custom-call | flops 1024 | bytes 1024 | tf_op jit(solution)/shard_map/input_grads/pallas_call | solution.py:547
  316.4 2.8 add_convert_fusion
  319.1 2.0 collective-permute-done.36.refs_1_
  321.1 2.7 join.6
  325.2 2.7 join.5
  329.7 26.1 %collective-permute-done.37.refs_2_ = bf16[1024,640]{1,0:T(8,128)(2,1)} collective-permute-done((bf16[1024,640]{1,0:T(8,128)(2,1)}, bf16[1024,640]{1,0:T(8,128)(2,1)}, u32[]{:S(2)}, u32[]{:S(2)}) %collective-permute-start.37) | collective-permute-done | bytes 1310752 | tf_op jit(solution)/shard_map/ppermute | solution.py:672
  355.7 3.2 join.7
  359.0 19.8 %collective-permute-done.40.refs_2_ = bf16[2,288,960]{2,1,0:T(8,128)(2,1)} collective-permute-done((bf16[2,288,960]{2,1,0:T(8,128)(2,1)}, bf16[2,288,960]{2,1,0:T(8,128)(2,1)}, u32[]{:S(2)}, u32[]{:S(2)}) %collective-permute-start.40) | collective-permute-done | bytes 1105952 | tf_op jit(solution)/shard_map/ppermute | solution.py:669
  378.8 2.2 join.9
  381.7 2.2 copy.20.refs_2_
  383.9 3.8 unpack_hidden.1
  387.8 2.4 copy.21
  390.2 2.2 join.8.refs_2_
  392.4 26.9 %collective-permute-done.41.refs_3_ = bf16[288,960]{1,0:T(8,128)(2,1)S(1)} collective-permute-done((bf16[288,960]{1,0:T(8,128)(2,1)}, bf16[288,960]{1,0:T(8,128)(2,1)S(1)}, u32[]{:S(2)}, u32[]{:S(2)}) %collective-permute-start.41) | collective-permute-done | bytes 552992 | tf_op jit(solution)/shard_map/ppermute | solution.py:669
  420.1 4.0 unpack_weights.1
  424.2 2.0 add_bitcast_fusion
  426.2 2.3 fusion.4
  (132 shorter events, 41.9 us)
Async XLA Ops:
  4.7 13.4 %collective-permute-start = (bf16[288,768]{1,0:T(8,128)(2,1)}, bf16[288,768]{1,0:T(8,128)(2,1)S(1)}, u32[]{:S(2)}, u32[]{:S(2)}) collective-permute-start(bf16[288,768]{1,0:T(8,128)(2,1)} %get-tuple-element.78), channel_id=1, source_target_pairs={{0,8},{4,12},{8,0},{12,4},{16,24},{20,28},{24,16},{28,20},{1,9},{5... | collective-permute-start | bytes 1327112 | tf_op jit(solution)/shard_map/ppermute | solution.py:669
  8.5 4.7 %collective-permute-start.4 = (bf16[1,576]{1,0:T(2,128)(2,1)S(1)}, bf16[1,576]{1,0:T(2,128)(2,1)S(1)}, u32[]{:S(2)}, u32[]{:S(2)}) collective-permute-start(bf16[1,576]{1,0:T(2,128)(2,1)S(1)} %slice.61), channel_id=1, source_target_pairs={{0,4},{4,8},{8,12},{12,16},{16,20},{20,24},{24,28},{1,5},{5,9},{9,... | collective-permute-start | bytes 3464 | tf_op jit(solution)/shard_map/ppermute | solution.py:677
  13.6 79.1 %copy-start = (bf16[1040,640]{1,0:T(8,128)(2,1)}, bf16[1040,640]{1,0:T(8,128)(2,1)S(1)}, u32[]{:S(2)}) copy-start(bf16[1040,640]{1,0:T(8,128)(2,1)S(1)} %fusion.6.refs_4_) | copy-start | bytes 3993604
  13.6 56.9 %copy-start.9 = (bf16[1024,576]{0,1:T(8,128)(2,1)S(1)}, bf16[1024,576]{0,1:T(8,128)(2,1)}, u32[]{:S(2)}) copy-start(bf16[1024,576]{0,1:T(8,128)(2,1)} %param.11) | copy-start | bytes 3538948
  13.6 29.9 %collective-permute-start.5 = (bf16[1040,640]{1,0:T(8,128)(2,1)S(1)}, bf16[1040,640]{1,0:T(8,128)(2,1)S(1)}, u32[]{:S(2)}, u32[]{:S(2)}) collective-permute-start(bf16[1040,640]{1,0:T(8,128)(2,1)S(1)} %fusion.6.refs_4_), channel_id=1, source_target_pairs={{0,2},{1,3},{2,0},{3,1},{4,6},{5,7},{6,4},{7,5},{8,10},{9,11},{10,... | collective-permute-start | bytes 3993608 | tf_op jit(solution)/shard_map/ppermute | solution.py:672
  18.1 51.6 %collective-permute-start.8 = (bf16[1040,640]{1,0:T(8,128)(2,1)S(1)}, bf16[1040,640]{1,0:T(8,128)(2,1)}, u32[]{:S(2)}, u32[]{:S(2)}) collective-permute-start(bf16[1040,640]{1,0:T(8,128)(2,1)S(1)} %fusion.6.refs_4_), channel_id=1, source_target_pairs={{0,8},{4,12},{8,0},{12,4},{16,24},{20,28},{24,16},{28,20},{1,9},{5... | collective-permute-start | bytes 3993608 | tf_op jit(solution)/shard_map/ppermute | solution.py:669
  23.0 46.7 %copy-start.2 = (bf16[2,288,768]{2,1,0:T(8,128)(2,1)}, bf16[2,288,768]{2,1,0:T(8,128)(2,1)S(1)}, u32[]{:S(2)}) copy-start(bf16[2,288,768]{2,1,0:T(8,128)(2,1)S(1)} %pad_maximum_fusion.1.refs_0_) | copy-start | bytes 2654212
  23.0 19.7 %collective-permute-start.1 = (bf16[2,288,768]{2,1,0:T(8,128)(2,1)S(1)}, bf16[2,288,768]{2,1,0:T(8,128)(2,1)S(1)}, u32[]{:S(2)}, u32[]{:S(2)}) collective-permute-start(bf16[2,288,768]{2,1,0:T(8,128)(2,1)S(1)} %pad_maximum_fusion.1.refs_0_), channel_id=1, source_target_pairs={{0,4},{4,0},{8,12},{12,8},{16,20},{20,16},{24,28},{28,24},{1,5},{5... | collective-permute-start | bytes 2654216 | tf_op jit(solution)/shard_map/ppermute | solution.py:669
  23.0 47.2 %collective-permute-start.2 = (bf16[2,288,768]{2,1,0:T(8,128)(2,1)S(1)}, bf16[2,288,768]{2,1,0:T(8,128)(2,1)}, u32[]{:S(2)}, u32[]{:S(2)}) collective-permute-start(bf16[2,288,768]{2,1,0:T(8,128)(2,1)S(1)} %pad_maximum_fusion.1.refs_0_), channel_id=1, source_target_pairs={{0,16},{4,20},{8,24},{12,28},{16,0},{20,4},{24,8},{28,12},{1,17},{... | collective-permute-start | bytes 2654216 | tf_op jit(solution)/shard_map/ppermute | solution.py:669
  42.7 27.5 %copy-start.12 = (bf16[2,288,768]{2,1,0:T(8,128)(2,1)}, bf16[2,288,768]{2,1,0:T(8,128)(2,1)S(1)}, u32[]{:S(2)}) copy-start(bf16[2,288,768]{2,1,0:T(8,128)(2,1)S(1)} %collective-permute-done.1.refs_1_) | copy-start | bytes 2654212
  43.5 26.7 %copy-start.4 = (bf16[1040,640]{1,0:T(8,128)(2,1)}, bf16[1040,640]{1,0:T(8,128)(2,1)S(1)}, u32[]{:S(2)}) copy-start(bf16[1040,640]{1,0:T(8,128)(2,1)S(1)} %collective-permute-done.5.refs_5_) | copy-start | bytes 3993604
  69.7 29.2 %collective-permute-start.9 = (bf16[1040,640]{1,0:T(8,128)(2,1)}, bf16[1040,640]{1,0:T(8,128)(2,1)}, u32[]{:S(2)}, u32[]{:S(2)}) collective-permute-start(bf16[1040,640]{1,0:T(8,128)(2,1)} %collective-permute-done.8.refs_8_), channel_id=1, source_target_pairs={{0,2},{1,3},{2,0},{3,1},{4,6},{5,7},{6,4},{7,5},{8,10},{9,11},{10,... | collective-permute-start | bytes 3993608 | tf_op jit(solution)/shard_map/ppermute | solution.py:672
  70.2 32.0 %collective-permute-start.10 = (bf16[1040,640]{1,0:T(8,128)(2,1)}, bf16[1040,640]{1,0:T(8,128)(2,1)}, u32[]{:S(2)}, u32[]{:S(2)}) collective-permute-start(bf16[1040,640]{1,0:T(8,128)(2,1)} %collective-permute-done.8.refs_8_), channel_id=1, source_target_pairs={{0,1},{1,0},{2,3},{3,2},{4,5},{5,4},{6,7},{7,6},{8,9},{9,8},{10,11... | collective-permute-start | bytes 3993608 | tf_op jit(solution)/shard_map/ppermute | solution.py:672
  70.2 22.4 %collective-permute-start.3 = (bf16[2,288,768]{2,1,0:T(8,128)(2,1)}, bf16[2,288,768]{2,1,0:T(8,128)(2,1)}, u32[]{:S(2)}, u32[]{:S(2)}) collective-permute-start(bf16[2,288,768]{2,1,0:T(8,128)(2,1)} %collective-permute-done.2.refs_2_), channel_id=1, source_target_pairs={{0,4},{4,0},{8,12},{12,8},{16,20},{20,16},{24,28},{28,24},{1,5},{5... | collective-permute-start | bytes 2654216 | tf_op jit(solution)/shard_map/ppermute | solution.py:669
  77.0 9.3 %collective-permute-start.11 = (bf16[1024,128]{1,0:T(8,128)(2,1)}, bf16[1024,128]{1,0:T(8,128)(2,1)S(1)}, u32[]{:S(2)}, u32[]{:S(2)}) collective-permute-start(bf16[1024,128]{1,0:T(8,128)(2,1)} %get-tuple-element.86), channel_id=1, source_target_pairs={{0,8},{4,12},{8,0},{12,4},{16,24},{20,28},{24,16},{28,20},{1,9},{5... | collective-permute-start | bytes 786440 | tf_op jit(solution)/shard_map/ppermute | solution.py:669
  82.9 16.0 %collective-permute-start.13 = (bf16[288,960]{1,0:T(8,128)(2,1)}, bf16[288,960]{1,0:T(8,128)(2,1)S(1)}, u32[]{:S(2)}, u32[]{:S(2)}) collective-permute-start(bf16[288,960]{1,0:T(8,128)(2,1)} %get-tuple-element.95), channel_id=1, source_target_pairs={{0,8},{4,12},{8,0},{12,4},{16,24},{20,28},{24,16},{28,20},{1,9},{5... | collective-permute-start | bytes 1658888 | tf_op jit(solution)/shard_map/ppermute | solution.py:669
  86.3 18.5 %collective-permute-start.7 = (bf16[1040,640]{1,0:T(8,128)(2,1)}, bf16[1040,640]{1,0:T(8,128)(2,1)}, u32[]{:S(2)}, u32[]{:S(2)}) collective-permute-start(bf16[1040,640]{1,0:T(8,128)(2,1)} %copy-done.4), channel_id=1, source_target_pairs={{0,1},{1,0},{2,3},{3,2},{4,5},{5,4},{6,7},{7,6},{8,9},{9,8},{10,11... | collective-permute-start | bytes 3993608 | tf_op jit(solution)/shard_map/ppermute | solution.py:672
  92.7 14.6 %collective-permute-start.6 = (bf16[1040,640]{1,0:T(8,128)(2,1)S(1)}, bf16[1040,640]{1,0:T(8,128)(2,1)S(1)}, u32[]{:S(2)}, u32[]{:S(2)}) collective-permute-start(bf16[1040,640]{1,0:T(8,128)(2,1)S(1)} %fusion.6.refs_4_), channel_id=1, source_target_pairs={{0,1},{1,0},{2,3},{3,2},{4,5},{5,4},{6,7},{7,6},{8,9},{9,8},{10,11... | collective-permute-start | bytes 3993608 | tf_op jit(solution)/shard_map/ppermute | solution.py:672
  98.9 9.5 %collective-permute-start.12 = (bf16[1040,640]{1,0:T(8,128)(2,1)}, bf16[1040,640]{1,0:T(8,128)(2,1)}, u32[]{:S(2)}, u32[]{:S(2)}) collective-permute-start(bf16[1040,640]{1,0:T(8,128)(2,1)} %collective-permute-done.9.refs_9_), channel_id=1, source_target_pairs={{0,1},{1,0},{2,3},{3,2},{4,5},{5,4},{6,7},{7,6},{8,9},{9,8},{10,11... | collective-permute-start | bytes 3993608 | tf_op jit(solution)/shard_map/ppermute | solution.py:672
  101.1 28.7 %collective-permute-start.14 = (bf16[2,288,960]{2,1,0:T(8,128)(2,1)}, bf16[2,288,960]{2,1,0:T(8,128)(2,1)}, u32[]{:S(2)}, u32[]{:S(2)}) collective-permute-start(bf16[2,288,960]{2,1,0:T(8,128)(2,1)} %pad_maximum_fusion.refs_0_), channel_id=1, source_target_pairs={{0,4},{4,0},{8,12},{12,8},{16,20},{20,16},{24,28},{28,24},{1,5},{5... | collective-permute-start | bytes 3317768 | tf_op jit(solution)/shard_map/ppermute | solution.py:669
  102.2 56.6 %collective-permute-start.18 = (bf16[2,288,960]{2,1,0:T(8,128)(2,1)}, bf16[2,288,960]{2,1,0:T(8,128)(2,1)}, u32[]{:S(2)}, u32[]{:S(2)}) collective-permute-start(bf16[2,288,960]{2,1,0:T(8,128)(2,1)} %pad_maximum_fusion.refs_0_), channel_id=1, source_target_pairs={{0,16},{4,20},{8,24},{12,28},{16,0},{20,4},{24,8},{28,12},{1,17},{... | collective-permute-start | bytes 3317768 | tf_op jit(solution)/shard_map/ppermute | solution.py:669
  104.8 54.0 %collective-permute-start.19 = (bf16[1024,256]{1,0:T(8,128)(2,1)}, bf16[1024,256]{1,0:T(8,128)(2,1)S(1)}, u32[]{:S(2)}, u32[]{:S(2)}) collective-permute-start(bf16[1024,256]{1,0:T(8,128)(2,1)} %get-tuple-element.107), channel_id=1, source_target_pairs={{0,8},{4,12},{8,0},{12,4},{16,24},{20,28},{24,16},{28,20},{1,9},{5... | collective-permute-start | bytes 1572872 | tf_op jit(solution)/shard_map/ppermute | solution.py:669
  129.8 4.4 %collective-permute-start.15 = (f32[2,3,128]{2,1,0:T(4,128)}, f32[2,3,128]{2,1,0:T(4,128)S(1)}, u32[]{:S(2)}, u32[]{:S(2)}) collective-permute-start(f32[2,3,128]{2,1,0:T(4,128)} %get-tuple-element.96), channel_id=1, source_target_pairs={{0,4},{4,0},{8,12},{12,8},{16,20},{20,16},{24,28},{28,24},{1,5},{5... | collective-permute-start | bytes 9224 | tf_op jit(solution)/shard_map/ppermute | solution.py:669
  130.5 25.9 %collective-permute-start.16 = (f32[2,3,128]{2,1,0:T(4,128)}, f32[2,3,128]{2,1,0:T(4,128)S(1)}, u32[]{:S(2)}, u32[]{:S(2)}) collective-permute-start(f32[2,3,128]{2,1,0:T(4,128)} %get-tuple-element.96), channel_id=1, source_target_pairs={{0,16},{4,20},{8,24},{12,28},{16,0},{20,4},{24,8},{28,12},{1,17},{... | collective-permute-start | bytes 9224 | tf_op jit(solution)/shard_map/ppermute | solution.py:669
  132.9 24.7 %collective-permute-start.17 = (f32[2,3,128]{2,1,0:T(4,128)}, f32[2,3,128]{2,1,0:T(4,128)S(1)}, u32[]{:S(2)}, u32[]{:S(2)}) collective-permute-start(f32[2,3,128]{2,1,0:T(4,128)} %get-tuple-element.96), channel_id=1, source_target_pairs={{0,20},{4,16},{8,28},{12,24},{16,4},{20,0},{24,12},{28,8},{1,21},{... | collective-permute-start | bytes 9224 | tf_op jit(solution)/shard_map/ppermute | solution.py:669
  158.9 28.2 %collective-permute-start.20 = (bf16[2,288,960]{2,1,0:T(8,128)(2,1)}, bf16[2,288,960]{2,1,0:T(8,128)(2,1)S(1)}, u32[]{:S(2)}, u32[]{:S(2)}) collective-permute-start(bf16[2,288,960]{2,1,0:T(8,128)(2,1)} %collective-permute-done.18.refs_2_), channel_id=1, source_target_pairs={{0,4},{4,0},{8,12},{12,8},{16,20},{20,16},{24,28},{28,24},{1,5},{5... | collective-permute-start | bytes 3317768 | tf_op jit(solution)/shard_map/ppermute | solution.py:669
  183.4 35.8 %collective-permute-start.24 = (bf16[2,288,768]{2,1,0:T(8,128)(2,1)}, bf16[2,288,768]{2,1,0:T(8,128)(2,1)}, u32[]{:S(2)}, u32[]{:S(2)}) collective-permute-start(bf16[2,288,768]{2,1,0:T(8,128)(2,1)} %get-tuple-element.102), channel_id=1, source_target_pairs={{0,4},{4,0},{8,12},{12,8},{16,20},{20,16},{24,28},{28,24},{1,5},{5... | collective-permute-start | bytes 2654216 | tf_op jit(solution)/shard_map/ppermute | solution.py:669
  184.9 40.4 %collective-permute-start.25 = (bf16[2,288,768]{2,1,0:T(8,128)(2,1)}, bf16[2,288,768]{2,1,0:T(8,128)(2,1)}, u32[]{:S(2)}, u32[]{:S(2)}) collective-permute-start(bf16[2,288,768]{2,1,0:T(8,128)(2,1)} %get-tuple-element.103), channel_id=1, source_target_pairs={{0,4},{4,0},{8,12},{12,8},{16,20},{20,16},{24,28},{28,24},{1,5},{5... | collective-permute-start | bytes 2654216 | tf_op jit(solution)/shard_map/ppermute | solution.py:669
  214.8 9.9 %collective-permute-start.21 = (f32[2,3,160]{2,1,0:T(4,128)}, f32[2,3,160]{2,1,0:T(4,128)S(1)}, u32[]{:S(2)}, u32[]{:S(2)}) collective-permute-start(f32[2,3,160]{2,1,0:T(4,128)} %get-tuple-element.112), channel_id=1, source_target_pairs={{0,4},{4,0},{8,12},{12,8},{16,20},{20,16},{24,28},{28,24},{1,5},{5... | collective-permute-start | bytes 11528 | tf_op jit(solution)/shard_map/ppermute | solution.py:669
  215.4 9.2 %collective-permute-start.22 = (f32[2,3,160]{2,1,0:T(4,128)}, f32[2,3,160]{2,1,0:T(4,128)S(1)}, u32[]{:S(2)}, u32[]{:S(2)}) collective-permute-start(f32[2,3,160]{2,1,0:T(4,128)} %get-tuple-element.112), channel_id=1, source_target_pairs={{0,16},{4,20},{8,24},{12,28},{16,0},{20,4},{24,8},{28,12},{1,17},{... | collective-permute-start | bytes 11528 | tf_op jit(solution)/shard_map/ppermute | solution.py:669
  215.7 8.9 %collective-permute-start.23 = (f32[2,3,160]{2,1,0:T(4,128)}, f32[2,3,160]{2,1,0:T(4,128)S(1)}, u32[]{:S(2)}, u32[]{:S(2)}) collective-permute-start(f32[2,3,160]{2,1,0:T(4,128)} %get-tuple-element.112), channel_id=1, source_target_pairs={{0,20},{4,16},{8,28},{12,24},{16,4},{20,0},{24,12},{28,8},{1,21},{... | collective-permute-start | bytes 11528 | tf_op jit(solution)/shard_map/ppermute | solution.py:669
  225.3 49.0 %collective-permute-start.30 = (bf16[2,288,768]{2,1,0:T(8,128)(2,1)}, bf16[2,288,768]{2,1,0:T(8,128)(2,1)}, u32[]{:S(2)}, u32[]{:S(2)}) collective-permute-start(bf16[2,288,768]{2,1,0:T(8,128)(2,1)} %convert_add_fusion.1), channel_id=1, source_target_pairs={{0,16},{4,20},{8,24},{12,28},{16,0},{20,4},{24,8},{28,12},{1,17},{... | collective-permute-start | bytes 2654216 | tf_op jit(solution)/shard_map/ppermute | solution.py:669
  244.3 31.3 %collective-permute-start.27 = (f32[3,864]{1,0:T(4,128)}, f32[3,864]{1,0:T(4,128)}, u32[]{:S(2)}, u32[]{:S(2)}) collective-permute-start(f32[3,864]{1,0:T(4,128)} %get-tuple-element.166), channel_id=1, source_target_pairs={{0,4},{4,0},{8,12},{12,8},{16,20},{20,16},{24,28},{28,24},{1,5},{5... | collective-permute-start | bytes 31112 | tf_op jit(solution)/shard_map/ppermute | solution.py:669
  245.2 30.5 %collective-permute-start.28 = (f32[3,864]{1,0:T(4,128)}, f32[3,864]{1,0:T(4,128)}, u32[]{:S(2)}, u32[]{:S(2)}) collective-permute-start(f32[3,864]{1,0:T(4,128)} %get-tuple-element.166), channel_id=1, source_target_pairs={{0,16},{4,20},{8,24},{12,28},{16,0},{20,4},{24,8},{28,12},{1,17},{... | collective-permute-start | bytes 31112 | tf_op jit(solution)/shard_map/ppermute | solution.py:669
  248.1 27.6 %collective-permute-start.29 = (f32[3,864]{1,0:T(4,128)}, f32[3,864]{1,0:T(4,128)}, u32[]{:S(2)}, u32[]{:S(2)}) collective-permute-start(f32[3,864]{1,0:T(4,128)} %get-tuple-element.166), channel_id=1, source_target_pairs={{0,20},{4,16},{8,28},{12,24},{16,4},{20,0},{24,12},{28,8},{1,21},{... | collective-permute-start | bytes 31112 | tf_op jit(solution)/shard_map/ppermute | solution.py:669
  251.0 64.8 %collective-permute-start.26 = (bf16[1024,288]{0,1:T(8,128)(2,1)}, bf16[1024,288]{0,1:T(8,128)(2,1)}, u32[]{:S(2)}, u32[]{:S(2)}) collective-permute-start(bf16[1024,288]{0,1:T(8,128)(2,1)} %copy.19), channel_id=1, source_target_pairs={{0,8},{4,12},{8,0},{12,4},{16,24},{20,28},{24,16},{28,20},{1,9},{5... | collective-permute-start | bytes 1769480 | tf_op jit(solution)/shard_map/ppermute | solution.py:669
  275.7 40.1 %collective-permute-start.31 = (bf16[2,288,960]{2,1,0:T(8,128)(2,1)}, bf16[2,288,960]{2,1,0:T(8,128)(2,1)}, u32[]{:S(2)}, u32[]{:S(2)}) collective-permute-start(bf16[2,288,960]{2,1,0:T(8,128)(2,1)} %get-tuple-element.131), channel_id=1, source_target_pairs={{0,4},{4,0},{8,12},{12,8},{16,20},{20,16},{24,28},{28,24},{1,5},{5... | collective-permute-start | bytes 3317768 | tf_op jit(solution)/shard_map/ppermute | solution.py:669
  278.4 37.4 %collective-permute-start.33 = (bf16[288,768]{1,0:T(8,128)(2,1)S(1)}, bf16[288,768]{1,0:T(8,128)(2,1)}, u32[]{:S(2)}, u32[]{:S(2)}) collective-permute-start(bf16[288,768]{1,0:T(8,128)(2,1)S(1)} %get-tuple-element.159), channel_id=1, source_target_pairs={{0,8},{4,12},{8,0},{12,4},{16,24},{20,28},{24,16},{28,20},{1,9},{5... | collective-permute-start | bytes 1327112 | tf_op jit(solution)/shard_map/ppermute | solution.py:669
  278.4 37.4 %collective-permute-start.32 = (f32[3,288]{1,0:T(4,128)S(1)}, f32[3,288]{1,0:T(4,128)S(1)}, u32[]{:S(2)}, u32[]{:S(2)}) collective-permute-start(f32[3,288]{1,0:T(4,128)S(1)} %pad_maximum_fusion.7), channel_id=1, source_target_pairs={{0,8},{4,12},{8,0},{12,4},{16,24},{20,28},{24,16},{28,20},{1,9},{5... | collective-permute-start | bytes 10376 | tf_op jit(solution)/shard_map/ppermute | solution.py:669
  281.6 34.8 %copy-start.7 = (bf16[2,288,960]{2,1,0:T(8,128)(2,1)S(1)}, bf16[2,288,960]{2,1,0:T(8,128)(2,1)}, u32[]{:S(2)}) copy-start(bf16[2,288,960]{2,1,0:T(8,128)(2,1)} %get-tuple-element.143) | copy-start | bytes 3317764
  315.8 5.3 %collective-permute-start.36 = (bf16[2,1024,640]{2,1,0:T(8,128)(2,1)}, bf16[2,1024,640]{2,1,0:T(8,128)(2,1)}, u32[]{:S(2)}, u32[]{:S(2)}) collective-permute-start(bf16[2,1024,640]{2,1,0:T(8,128)(2,1)} %get-tuple-element.142), channel_id=1, source_target_pairs={{0,1},{1,0},{2,3},{3,2},{4,5},{5,4},{6,7},{7,6},{8,9},{9,8},{10,11... | collective-permute-start | bytes 7864328 | tf_op jit(solution)/shard_map/ppermute | solution.py:672
  315.9 9.3 %collective-permute-start.34 = (bf16[2,1024,640]{2,1,0:T(8,128)(2,1)}, bf16[2,1024,640]{2,1,0:T(8,128)(2,1)}, u32[]{:S(2)}, u32[]{:S(2)}) collective-permute-start(bf16[2,1024,640]{2,1,0:T(8,128)(2,1)} %get-tuple-element.140), channel_id=1, source_target_pairs={{0,1},{1,0},{2,3},{3,2},{4,5},{5,4},{6,7},{7,6},{8,9},{9,8},{10,11... | collective-permute-start | bytes 7864328 | tf_op jit(solution)/shard_map/ppermute | solution.py:672
  323.8 31.9 %collective-permute-start.37 = (bf16[1024,640]{1,0:T(8,128)(2,1)}, bf16[1024,640]{1,0:T(8,128)(2,1)}, u32[]{:S(2)}, u32[]{:S(2)}) collective-permute-start(bf16[1024,640]{1,0:T(8,128)(2,1)} %join.6), channel_id=1, source_target_pairs={{0,2},{1,3},{2,0},{3,1},{4,6},{5,7},{6,4},{7,5},{8,10},{9,11},{10,... | collective-permute-start | bytes 3932168 | tf_op jit(solution)/shard_map/ppermute | solution.py:672
  324.1 34.8 %collective-permute-start.39 = (bf16[2,288,960]{2,1,0:T(8,128)(2,1)}, bf16[2,288,960]{2,1,0:T(8,128)(2,1)S(1)}, u32[]{:S(2)}, u32[]{:S(2)}) collective-permute-start(bf16[2,288,960]{2,1,0:T(8,128)(2,1)} %get-tuple-element.133), channel_id=1, source_target_pairs={{0,4},{4,0},{8,12},{12,8},{16,20},{20,16},{24,28},{28,24},{1,5},{5... | collective-permute-start | bytes 3317768 | tf_op jit(solution)/shard_map/ppermute | solution.py:669
  325.2 53.6 %collective-permute-start.40 = (bf16[2,288,960]{2,1,0:T(8,128)(2,1)}, bf16[2,288,960]{2,1,0:T(8,128)(2,1)}, u32[]{:S(2)}, u32[]{:S(2)}) collective-permute-start(bf16[2,288,960]{2,1,0:T(8,128)(2,1)} %add_convert_fusion), channel_id=1, source_target_pairs={{0,16},{4,20},{8,24},{12,28},{16,0},{20,4},{24,8},{28,12},{1,17},{... | collective-permute-start | bytes 3317768 | tf_op jit(solution)/shard_map/ppermute | solution.py:669
  327.9 98.2 %collective-permute-start.35 = (bf16[1024,640]{1,0:T(8,128)(2,1)}, bf16[1024,640]{1,0:T(8,128)(2,1)}, u32[]{:S(2)}, u32[]{:S(2)}) collective-permute-start(bf16[1024,640]{1,0:T(8,128)(2,1)} %join.5), channel_id=1, source_target_pairs={{0,2},{1,3},{2,0},{3,1},{4,6},{5,7},{6,4},{7,5},{8,10},{9,11},{10,... | collective-permute-start | bytes 3932168 | tf_op jit(solution)/shard_map/ppermute | solution.py:672
  358.9 67.3 %collective-permute-start.38 = (bf16[1024,640]{1,0:T(8,128)(2,1)}, bf16[1024,640]{1,0:T(8,128)(2,1)}, u32[]{:S(2)}, u32[]{:S(2)}) collective-permute-start(bf16[1024,640]{1,0:T(8,128)(2,1)} %join.7), channel_id=1, source_target_pairs={{0,8},{4,12},{8,0},{12,4},{16,24},{20,28},{24,16},{28,20},{1,9},{5... | collective-permute-start | bytes 3932168 | tf_op jit(solution)/shard_map/ppermute | solution.py:669
  381.0 38.3 %collective-permute-start.41 = (bf16[288,960]{1,0:T(8,128)(2,1)}, bf16[288,960]{1,0:T(8,128)(2,1)S(1)}, u32[]{:S(2)}, u32[]{:S(2)}) collective-permute-start(bf16[288,960]{1,0:T(8,128)(2,1)} %join.9), channel_id=1, source_target_pairs={{0,8},{4,12},{8,0},{12,4},{16,24},{20,28},{24,16},{28,20},{1,9},{5... | collective-permute-start | bytes 1658888 | tf_op jit(solution)/shard_map/ppermute | solution.py:669
  (14 other events, 134.0 us)

commit v4 on v3

--- a/solution.py
+++ b/solution.py
@@ -765,16 +765,21 @@
                 dims, 0, place, w_in, wrel, [xs[r] for r in xrel], xrel, bias_i, ups[i]
             )
         else:
-            w_in[0] = after(w_in[0], *[v[2] for v in waiting])
+            w_in[0] = after(w_in[0], *[v[2] for v in waiting[:-1]])
             gates, seg, tot, w_rel = gates_and_totals(
                 dims, 0, place, w_in, wrel, [x_all, halo], [], bias_i, ups[i], keep_w
             )
         every = spread_totals(after(tot, *[g[0, 1] for g in got[i + 1 : i + 2]]) if i + 1 < count else tot)
         wide_w.append(w_rel)
         if i > 0:
-            sums = over_p(waiting, tot)
+            (kh0, here0, away0), *others = waiting[::-1]
+            others = others[::-1]
+            sums = over_p(others, tot)
+            every_now = after(every, *sums)
             h_sums = [after(v, every) for v in sums]
-            every = after(every, *sums)
+            (near_sum,) = over_p([(kh0, here0, after(away0, every))])
+            h_sums.append(near_sum)
+            every = every_now
         h0, h1, gg, gf, gp, gb = finish(n, 0, place, gates, ups[i], keep_w, seg, every)
         hidden_mine.append(h0)
         hidden_other.append(h1)
@@ -822,20 +827,23 @@
         p_came.append(after(seq_to(v[2], 0, 0, 1), *p_came[-1:]))
     sent1, sent0, *_ = lax.optimization_barrier((sent1, sent0, p_came[0], hidden_came, bias_other, *w_pairs))
     c_came1, c_came0 = gate_to(sent1, 0, 1), gate_to(sent0, 0, 1)
-    h_came = []
-    for k, (kh, here, _) in enumerate(waiting[:-1]):
-        both_l = (here.astype(F32) + p_came[k].astype(F32)).astype(BF)
-        c_came1 = after(c_came1, both_l)
-        h_came.append(seq_to(both_l, kh, 0, 0))
+    farther = [join([(here, 0), (p_came[k], 0)], LATER) for k, (_, here, _) in enumerate(waiting[:-1])]
+    c_came1 = after(c_came1, *farther)
+    h_came = [seq_to(v, waiting[k][0], 0, 0) for k, v in enumerate(farther)]
     y_came1 = gate_to(join([(kept1, 1), (c_came1, 1)], LATER), 1, 0)
+    total = join([(waiting[-1][1], 0), (p_came[-1], 0)] + [(v, None) for v in h_came], LATER)
+    l_total = seq_to(total, 0, 1, 0)
+    x_part = join([(kept1, 0), (c_came1, 0), (after(y_came1, total), None)], LATER)
+    l_came = seq_to(x_part, 0, 1, 0)
+    c_came0 = after(c_came0, x_part)
     y_came0 = gate_to(join([(kept0, 1), (c_came0, 1)], LATER), 1, 0)
-    l_came = seq_to(join([(kept1, 0), (c_came1, 0), (y_came1, None)], LATER), 0, 1, 0)
-    total = [
-        join([(waiting[-1][1], d), (p_came[-1], d)] + [(v, d) for v in h_came], LATER) for d in range(2)
-    ]
-    w_pairs += [total[1], seq_to(total[0], 0, 1, 0)]
+    rest = [join([(here, 1), (p_came[k], 1)], LATER) for k, (_, here, _) in enumerate(waiting[:-1])]
+    h_rest = [seq_to(after(v, y_came1, total), waiting[k][0], 0, 0) for k, v in enumerate(rest)]
     grad_x = kept0[0].astype(F32) + c_came0[0].astype(F32) + y_came0.astype(F32) + l_came.astype(F32)
     grad_x = grad_x[:, :dl].astype(BF)
+    h_rest = [after(v, grad_x) for v in h_rest]
+    total = join([(waiting[-1][1], 1), (p_came[-1], 1)] + [(v, None) for v in h_rest], LATER)
+    w_pairs += [total, l_total]
 
     grad_bias = jnp.concatenate(
         [jnp.where(low, bias_half, bias_other), jnp.where(low, bias_other, bias_half)], axis=1

time: 431 us -> 421 us (0.977)
  waiting for transfers between devices: 167 us -> 152 us
  starting transfers between devices: 51 us -> 57.6 us
  other arithmetic: 21.9 us -> 16.5 us
    ppermute x10, waiting for transfers between devices: 35.1 us -> 21.9 us  [gate_to(): return lax.ppermute(v, 'gate', [(i, i ^ d_a * 2 + d_b) for i in range(m)])]
    ppermute x31 -> x32, starting transfers between devices: 42.9 us -> 49.5 us  [seq_to(): return lax.ppermute(v, 'seq', route)]
    pallas_call x5 -> x7, Pallas kernels: 13 us -> 17.1 us  [join(): pl.pallas_call(join_kernel, grid=(steps,), in_specs=[spec(v, at) for v, a...]
    ppermute x31 -> x32, waiting for transfers between devices: 131 us -> 129 us  [seq_to(): return lax.ppermute(v, 'seq', route)]
  transfers between devices with their start and end apart: 42 -> 43, of which waited for: 17 -> 18; matrix products, arithmetic and copies ran while one was open for 7% -> 7% of each run, Pallas kernels for 40% -> 40%
where the time goes in v4:
time: 421 us; the launch traced here: 420 us
  Pallas kernels  177 us (42%)
  waiting for transfers between devices  152 us (36%)
  starting transfers between devices  57.6 us (14%)
  other arithmetic  16.5 us (4%)
  local copies, waits for them, and re-layouts  15.6 us (4%)
    ppermute x32, waiting for transfers between devices, seq_to(): return lax.ppermute(v, 'seq', route)  129 us
    ppermute x32, starting transfers between devices, seq_to(): return lax.ppermute(v, 'seq', route)  49.5 us
    pallas_call x2, Pallas kernels, gates_and_totals(): pl.pallas_call(functools.partial(gates_kernel, plan), in_specs=[SMEM_SPEC...  46.9 us
    pallas_call x1, Pallas kernels, input_grads(): pl.pallas_call(xgrad_kernel, grid_spec=pltpu.PrefetchScalarGridSpec(num_s...  34.1 us
    pallas_call x2, Pallas kernels, weight_grads(): pl.pallas_call(functools.partial(wgrad_kernel, dw), grid_spec=pltpu.Prefe...  34.1 us
    pallas_call x2, Pallas kernels, finish(): pl.pallas_call(functools.partial(finish_kernel, n, up_at), in_specs=[SMEM...  25 us
    ppermute x10, waiting for transfers between devices, gate_to(): return lax.ppermute(v, 'gate', [(i, i ^ d_a * 2 + d_b) for i in range(m)])  21.9 us
    pallas_call x7, Pallas kernels, join(): pl.pallas_call(join_kernel, grid=(steps,), in_specs=[spec(v, at) for v, a...  17.1 us
  transfers between devices with their start and end apart: 43, of which 18 were waited for; matrix products, arithmetic and copies ran while one was open for 7% of the time, Pallas kernels for 40%

profile of v4, /device:TPU:0, one launch (start us, length us, event | category | flops | bytes accessed | tf_op | source)
XLA Modules:
  0.0 420.1 jit_solution(11496322224234763315)
XLA Ops:
  1.3 3.3 pack_weights.2
  4.7 3.0 collective-permute-start
  8.4 3.4 collective-permute-start.4
  15.1 2.9 collective-permute-done
  18.1 4.8 %collective-permute-start.8 = (bf16[1040,640]{1,0:T(8,128)(2,1)S(1)}, bf16[1040,640]{1,0:T(8,128)(2,1)}, u32[]{:S(2)}, u32[]{:S(2)}) collective-permute-start(bf16[1040,640]{1,0:T(8,128)(2,1)S(1)} %fusion.6.refs_4_), channel_id=1, source_target_pairs={{0,8},{4,12},{8,0},{12,4},{16,24},{20,28},{24,16},{28,20},{1,9},{5... | collective-permute-start | bytes 3993608 | tf_op jit(solution)/shard_map/ppermute | solution.py:669
  23.0 2.7 collective-permute-start.2
  25.6 17.0 %collective-permute-done.1.refs_1_ = bf16[2,288,768]{2,1,0:T(8,128)(2,1)S(1)} collective-permute-done((bf16[2,288,768]{2,1,0:T(8,128)(2,1)S(1)}, bf16[2,288,768]{2,1,0:T(8,128)(2,1)S(1)}, u32[]{:S(2)}, u32[]{:S(2)}) %collective-permute-start.1) | collective-permute-done | bytes 884768 | tf_op jit(solution)/shard_map/ppermute | solution.py:669
  43.4 26.2 %collective-permute-done.8.refs_8_ = bf16[1040,640]{1,0:T(8,128)(2,1)} collective-permute-done((bf16[1040,640]{1,0:T(8,128)(2,1)S(1)}, bf16[1040,640]{1,0:T(8,128)(2,1)}, u32[]{:S(2)}, u32[]{:S(2)}) %collective-permute-start.8) | collective-permute-done | bytes 1331232 | tf_op jit(solution)/shard_map/ppermute | solution.py:669
  71.9 5.0 %pack_up.1 = (bf16[1024,128]{1,0:T(8,128)(2,1)}, bf16[1024,128]{1,0:T(8,128)(2,1)}, bf16[1024,160]{1,0:T(8,128)(2,1)}, bf16[1024,256]{1,0:T(8,128)(2,1)}) custom-call(s32[5]{0:T(128)} %stack.91.place, bf16[1024,576]{1,0:T(8,128)(2,1)} %copy.18.up_ref), custom_call_target="tpu_custom_call" | custom-call | flops 1024 | bytes 1024 | tf_op jit(solution)/shard_map/pack_up/pallas_call | solution.py:114
  76.9 2.0 collective-permute-start.11
  78.9 4.0 pack_weights.3
  82.9 3.3 collective-permute-done.11.refs_14_.up1
  86.2 6.4 %collective-permute-done.3.refs_3_ = bf16[2,288,768]{2,1,0:T(8,128)(2,1)} collective-permute-done((bf16[2,288,768]{2,1,0:T(8,128)(2,1)}, bf16[2,288,768]{2,1,0:T(8,128)(2,1)}, u32[]{:S(2)}, u32[]{:S(2)}) %collective-permute-start.3) | collective-permute-done | bytes 884768 | tf_op jit(solution)/shard_map/ppermute | solution.py:669
  92.6 6.2 %collective-permute-done.9.refs_9_ = bf16[1040,640]{1,0:T(8,128)(2,1)} collective-permute-done((bf16[1040,640]{1,0:T(8,128)(2,1)}, bf16[1040,640]{1,0:T(8,128)(2,1)}, u32[]{:S(2)}, u32[]{:S(2)}) %collective-permute-start.9) | collective-permute-done | bytes 1331232 | tf_op jit(solution)/shard_map/ppermute | solution.py:672
  98.8 2.2 pad_maximum_fusion.refs_0_
  102.2 2.6 collective-permute-start.18
  108.3 20.2 %gates_and_totals.2 = (f32[3,2048,128]{2,1,0:T(8,128)}, f32[2,3,8,128]{3,2,1,0:T(8,128)}, f32[2,3,128]{2,1,0:T(4,128)}, bf16[2048,2560]{1,0:T(8,128)(2,1)}, bf16...) custom-call(s32[5]{0:T(128)} %stack.91.place, bf16[2,288,768]{2,1,0:T(8,128)(2,1)} %copy-done.3, ...), custom_call_target="tpu_custom_call" | custom-call | flops 1024 | bytes 1024 | tf_op jit(solution)/shard_map/gates_and_totals/pallas_call | solution.py:293
  130.5 2.3 collective-permute-start.16
  134.1 22.2 %collective-permute-done.16 = f32[2,3,128]{2,1,0:T(4,128)S(1)} collective-permute-done((f32[2,3,128]{2,1,0:T(4,128)}, f32[2,3,128]{2,1,0:T(4,128)S(1)}, u32[]{:S(2)}, u32[]{:S(2)}) %collective-permute-start.16) | collective-permute-done | bytes 3104 | tf_op jit(solution)/shard_map/ppermute | solution.py:669
  159.5 8.7 %finish.2 = (bf16[1024,128]{1,0:T(8,128)(2,1)}, bf16[1024,128]{1,0:T(8,128)(2,1)}, bf16[2048,768]{1,0:T(8,128)(2,1)}, f32[2,384]{1,0:T(2,128)}, bf16[32,768]{1,0:T(8,128)(2,1)}, /*index=5*/f32[1,384]{1,0:T(1,128)}) custom-call(s32[5]{0:T(128)} %stack.91.place, f32[3,2048,128]{2,1,0:T(8,128)} %get-tuple-element.92.g_ref, ...), custom_call_target="tpu_custom_call" | custom-call | flops 1024 | bytes 1024 | tf_op jit(solution)/shard_map/finish/pallas_call | solution.py:436
  168.2 15.2 %weight_grads.2 = (bf16[2,288,768]{2,1,0:T(8,128)(2,1)}, bf16[2,288,768]{2,1,0:T(8,128)(2,1)}, bf16[2,288,768]{2,1,0:T(8,128)(2,1)}, bf16[2,288,768]{2,1,0:T(8,128)(2,1)}) custom-call(s32[5]{0:T(128)} %stack.91.place, bf16[2048,2560]{1,0:T(8,128)(2,1)} %get-tuple-element.101.x_ref.refs_4_, bf16[32,2560]{1,0:T(8,128)(2,1)} %get-tuple-element.102.halo_ref.refs_5_, ...), custom_call_target="tpu_custom_call" | custom-call | flops 1024 | bytes 1024 | tf_op jit(solution)/shard_map/weight_grads/pallas_call | solution.py:480
  188.0 26.7 %gates_and_totals.3 = (f32[3,2048,160]{2,1,0:T(8,128)}, f32[2,3,8,160]{3,2,1,0:T(8,128)}, f32[2,3,160]{2,1,0:T(4,128)}, bf16[4,640,960]{2,1,0:T(8,128)(2,1)}) custom-call(s32[5]{0:T(128)} %stack.91.place, bf16[2,288,960]{2,1,0:T(8,128)(2,1)} %pad_maximum_fusion.refs_0_, bf16[2,288,960]{2,1,0:T(8,128)(2,1)} %collective-permute-done.14.refs_1_, ...), custom_call_target="tpu_custom_call" | custom-call | flops 1024 | bytes 1024 | tf_op jit(solution)/shard_map/gates_and_totals/pallas_call | solution.py:293
  215.7 3.5 collective-permute-start.23
  219.2 2.6 convert_add_fusion
  223.1 3.0 collective-permute-start.30
  226.1 16.3 %finish.3 = (bf16[1024,160]{1,0:T(8,128)(2,1)}, bf16[1024,160]{1,0:T(8,128)(2,1)}, bf16[2048,960]{1,0:T(8,128)(2,1)}, f32[2,480]{1,0:T(2,128)}, bf16[32,960]{1,0:T(8,128)(2,1)}, /*index=5*/f32[1,480]{1,0:T(1,128)}) custom-call(s32[5]{0:T(128)} %stack.91.place, f32[3,2048,160]{2,1,0:T(8,128)} %get-tuple-element.112.g_ref, ...), custom_call_target="tpu_custom_call" | custom-call | flops 1024 | bytes 1024 | tf_op jit(solution)/shard_map/finish/pallas_call | solution.py:436
  245.0 3.2 collective-permute-start.28
  248.2 18.8 %weight_grads.3 = (bf16[2,288,960]{2,1,0:T(8,128)(2,1)}, bf16[2,288,960]{2,1,0:T(8,128)(2,1)}, bf16[2,288,960]{2,1,0:T(8,128)(2,1)}, bf16[2,288,960]{2,1,0:T(8,128)(2,1)}) custom-call(s32[5]{0:T(128)} %stack.91.place, bf16[2048,2560]{1,0:T(8,128)(2,1)} %get-tuple-element.101.x_ref.refs_4_, bf16[32,2560]{1,0:T(8,128)(2,1)} %get-tuple-element.102.halo_ref.refs_5_, ...), custom_call_target="tpu_custom_call" | custom-call | flops 1024 | bytes 1024 | tf_op jit(solution)/shard_map/weight_grads/pallas_call | solution.py:480
  274.4 2.0 collective-permute-start.32
  277.6 34.1 %input_grads.1 = (bf16[2,1024,640]{2,1,0:T(8,128)(2,1)}, bf16[2,1024,640]{2,1,0:T(8,128)(2,1)}, bf16[2,1024,640]{2,1,0:T(8,128)(2,1)}, bf16[2,1024,640]{2,1,0:T(8,128)(2,1)}) custom-call(s32[5]{0:T(128)} %stack.91.place, bf16[2048,768]{1,0:T(8,128)(2,1)} %get-tuple-element.103.gg_ref.refs_0_, bf16[2048,960]{1,0:T(8,128)(2,1)} %get-tuple-element.126.gg_ref.refs_1_, ...), custom_call_target="tpu_custom_call" | custom-call | flops 1024 | bytes 1024 | tf_op jit(solution)/shard_map/input_grads/pallas_call | solution.py:547
  312.7 2.0 join.7
  314.8 2.3 collective-permute-done.35.refs_1_
  317.1 2.7 join.8
  320.9 2.9 collective-permute-start.38
  323.8 24.1 %collective-permute-done.37.refs_1_ = bf16[2,288,960]{2,1,0:T(8,128)(2,1)S(1)} collective-permute-done((bf16[2,288,960]{2,1,0:T(8,128)(2,1)}, bf16[2,288,960]{2,1,0:T(8,128)(2,1)S(1)}, u32[]{:S(2)}, u32[]{:S(2)}) %collective-permute-start.37) | collective-permute-done | bytes 1105952 | tf_op jit(solution)/shard_map/ppermute | solution.py:669
  350.1 2.2 join.9
  352.3 3.2 join.10
  355.5 2.7 join.11
  360.7 2.2 copy.20.refs_2_
  362.9 3.8 unpack_hidden.1
  366.7 2.4 copy.21
  369.1 2.1 join.12
  371.2 2.0 collective-permute-start.42
  376.5 12.6 %collective-permute-done.39 = bf16[1024,640]{1,0:T(8,128)(2,1)S(1)} collective-permute-done((bf16[1024,640]{1,0:T(8,128)(2,1)}, bf16[1024,640]{1,0:T(8,128)(2,1)S(1)}, u32[]{:S(2)}, u32[]{:S(2)}) %collective-permute-start.39) | collective-permute-done | bytes 1310752 | tf_op jit(solution)/shard_map/ppermute | solution.py:672
  389.1 15.5 %collective-permute-done.40 = bf16[1024,640]{1,0:T(8,128)(2,1)} collective-permute-done((bf16[1024,640]{1,0:T(8,128)(2,1)}, bf16[1024,640]{1,0:T(8,128)(2,1)}, u32[]{:S(2)}, u32[]{:S(2)}) %collective-permute-start.40) | collective-permute-done | bytes 1310752 | tf_op jit(solution)/shard_map/ppermute | solution.py:669
  407.9 5.9 %collective-permute-done.41.refs_2_ = bf16[288,960]{1,0:T(8,128)(2,1)} collective-permute-done((bf16[288,960]{1,0:T(8,128)(2,1)}, bf16[288,960]{1,0:T(8,128)(2,1)}, u32[]{:S(2)}, u32[]{:S(2)}) %collective-permute-start.41) | collective-permute-done | bytes 552992 | tf_op jit(solution)/shard_map/ppermute | solution.py:669
  413.8 2.2 join.13.refs_2_
  416.0 4.0 unpack_weights.1
  (136 shorter events, 50.3 us)
Async XLA Ops:
  4.7 13.4 %collective-permute-start = (bf16[288,768]{1,0:T(8,128)(2,1)}, bf16[288,768]{1,0:T(8,128)(2,1)S(1)}, u32[]{:S(2)}, u32[]{:S(2)}) collective-permute-start(bf16[288,768]{1,0:T(8,128)(2,1)} %get-tuple-element.81), channel_id=1, source_target_pairs={{0,8},{4,12},{8,0},{12,4},{16,24},{20,28},{24,16},{28,20},{1,9},{5... | collective-permute-start | bytes 1327112 | tf_op jit(solution)/shard_map/ppermute | solution.py:669
  8.4 4.7 %collective-permute-start.4 = (bf16[1,576]{1,0:T(2,128)(2,1)S(1)}, bf16[1,576]{1,0:T(2,128)(2,1)S(1)}, u32[]{:S(2)}, u32[]{:S(2)}) collective-permute-start(bf16[1,576]{1,0:T(2,128)(2,1)S(1)} %slice.61), channel_id=1, source_target_pairs={{0,4},{4,8},{8,12},{12,16},{16,20},{20,24},{24,28},{1,5},{5,9},{9,... | collective-permute-start | bytes 3464 | tf_op jit(solution)/shard_map/ppermute | solution.py:677
  13.5 79.1 %copy-start = (bf16[1040,640]{1,0:T(8,128)(2,1)}, bf16[1040,640]{1,0:T(8,128)(2,1)S(1)}, u32[]{:S(2)}) copy-start(bf16[1040,640]{1,0:T(8,128)(2,1)S(1)} %fusion.6.refs_4_) | copy-start | bytes 3993604
  13.5 56.9 %copy-start.9 = (bf16[1024,576]{0,1:T(8,128)(2,1)S(1)}, bf16[1024,576]{0,1:T(8,128)(2,1)}, u32[]{:S(2)}) copy-start(bf16[1024,576]{0,1:T(8,128)(2,1)} %param.11) | copy-start | bytes 3538948
  13.6 29.9 %collective-permute-start.5 = (bf16[1040,640]{1,0:T(8,128)(2,1)S(1)}, bf16[1040,640]{1,0:T(8,128)(2,1)S(1)}, u32[]{:S(2)}, u32[]{:S(2)}) collective-permute-start(bf16[1040,640]{1,0:T(8,128)(2,1)S(1)} %fusion.6.refs_4_), channel_id=1, source_target_pairs={{0,2},{1,3},{2,0},{3,1},{4,6},{5,7},{6,4},{7,5},{8,10},{9,11},{10,... | collective-permute-start | bytes 3993608 | tf_op jit(solution)/shard_map/ppermute | solution.py:672
  18.1 51.6 %collective-permute-start.8 = (bf16[1040,640]{1,0:T(8,128)(2,1)S(1)}, bf16[1040,640]{1,0:T(8,128)(2,1)}, u32[]{:S(2)}, u32[]{:S(2)}) collective-permute-start(bf16[1040,640]{1,0:T(8,128)(2,1)S(1)} %fusion.6.refs_4_), channel_id=1, source_target_pairs={{0,8},{4,12},{8,0},{12,4},{16,24},{20,28},{24,16},{28,20},{1,9},{5... | collective-permute-start | bytes 3993608 | tf_op jit(solution)/shard_map/ppermute | solution.py:669
  22.9 46.7 %copy-start.3 = (bf16[2,288,768]{2,1,0:T(8,128)(2,1)}, bf16[2,288,768]{2,1,0:T(8,128)(2,1)S(1)}, u32[]{:S(2)}) copy-start(bf16[2,288,768]{2,1,0:T(8,128)(2,1)S(1)} %pad_maximum_fusion.1.refs_0_) | copy-start | bytes 2654212
  22.9 19.7 %collective-permute-start.1 = (bf16[2,288,768]{2,1,0:T(8,128)(2,1)S(1)}, bf16[2,288,768]{2,1,0:T(8,128)(2,1)S(1)}, u32[]{:S(2)}, u32[]{:S(2)}) collective-permute-start(bf16[2,288,768]{2,1,0:T(8,128)(2,1)S(1)} %pad_maximum_fusion.1.refs_0_), channel_id=1, source_target_pairs={{0,4},{4,0},{8,12},{12,8},{16,20},{20,16},{24,28},{28,24},{1,5},{5... | collective-permute-start | bytes 2654216 | tf_op jit(solution)/shard_map/ppermute | solution.py:669
  23.0 47.2 %collective-permute-start.2 = (bf16[2,288,768]{2,1,0:T(8,128)(2,1)S(1)}, bf16[2,288,768]{2,1,0:T(8,128)(2,1)}, u32[]{:S(2)}, u32[]{:S(2)}) collective-permute-start(bf16[2,288,768]{2,1,0:T(8,128)(2,1)S(1)} %pad_maximum_fusion.1.refs_0_), channel_id=1, source_target_pairs={{0,16},{4,20},{8,24},{12,28},{16,0},{20,4},{24,8},{28,12},{1,17},{... | collective-permute-start | bytes 2654216 | tf_op jit(solution)/shard_map/ppermute | solution.py:669
  42.6 27.5 %copy-start.12 = (bf16[2,288,768]{2,1,0:T(8,128)(2,1)}, bf16[2,288,768]{2,1,0:T(8,128)(2,1)S(1)}, u32[]{:S(2)}) copy-start(bf16[2,288,768]{2,1,0:T(8,128)(2,1)S(1)} %collective-permute-done.1.refs_1_) | copy-start | bytes 2654212
  43.4 26.7 %copy-start.5 = (bf16[1040,640]{1,0:T(8,128)(2,1)}, bf16[1040,640]{1,0:T(8,128)(2,1)S(1)}, u32[]{:S(2)}) copy-start(bf16[1040,640]{1,0:T(8,128)(2,1)S(1)} %collective-permute-done.5.refs_5_) | copy-start | bytes 3993604
  69.7 29.2 %collective-permute-start.9 = (bf16[1040,640]{1,0:T(8,128)(2,1)}, bf16[1040,640]{1,0:T(8,128)(2,1)}, u32[]{:S(2)}, u32[]{:S(2)}) collective-permute-start(bf16[1040,640]{1,0:T(8,128)(2,1)} %collective-permute-done.8.refs_8_), channel_id=1, source_target_pairs={{0,2},{1,3},{2,0},{3,1},{4,6},{5,7},{6,4},{7,5},{8,10},{9,11},{10,... | collective-permute-start | bytes 3993608 | tf_op jit(solution)/shard_map/ppermute | solution.py:672
  70.2 32.0 %collective-permute-start.10 = (bf16[1040,640]{1,0:T(8,128)(2,1)}, bf16[1040,640]{1,0:T(8,128)(2,1)}, u32[]{:S(2)}, u32[]{:S(2)}) collective-permute-start(bf16[1040,640]{1,0:T(8,128)(2,1)} %collective-permute-done.8.refs_8_), channel_id=1, source_target_pairs={{0,1},{1,0},{2,3},{3,2},{4,5},{5,4},{6,7},{7,6},{8,9},{9,8},{10,11... | collective-permute-start | bytes 3993608 | tf_op jit(solution)/shard_map/ppermute | solution.py:672
  70.2 22.4 %collective-permute-start.3 = (bf16[2,288,768]{2,1,0:T(8,128)(2,1)}, bf16[2,288,768]{2,1,0:T(8,128)(2,1)}, u32[]{:S(2)}, u32[]{:S(2)}) collective-permute-start(bf16[2,288,768]{2,1,0:T(8,128)(2,1)} %collective-permute-done.2.refs_2_), channel_id=1, source_target_pairs={{0,4},{4,0},{8,12},{12,8},{16,20},{20,16},{24,28},{28,24},{1,5},{5... | collective-permute-start | bytes 2654216 | tf_op jit(solution)/shard_map/ppermute | solution.py:669
  76.9 9.3 %collective-permute-start.11 = (bf16[1024,128]{1,0:T(8,128)(2,1)}, bf16[1024,128]{1,0:T(8,128)(2,1)S(1)}, u32[]{:S(2)}, u32[]{:S(2)}) collective-permute-start(bf16[1024,128]{1,0:T(8,128)(2,1)} %get-tuple-element.89), channel_id=1, source_target_pairs={{0,8},{4,12},{8,0},{12,4},{16,24},{20,28},{24,16},{28,20},{1,9},{5... | collective-permute-start | bytes 786440 | tf_op jit(solution)/shard_map/ppermute | solution.py:669
  82.9 16.0 %collective-permute-start.13 = (bf16[288,960]{1,0:T(8,128)(2,1)}, bf16[288,960]{1,0:T(8,128)(2,1)S(1)}, u32[]{:S(2)}, u32[]{:S(2)}) collective-permute-start(bf16[288,960]{1,0:T(8,128)(2,1)} %get-tuple-element.98), channel_id=1, source_target_pairs={{0,8},{4,12},{8,0},{12,4},{16,24},{20,28},{24,16},{28,20},{1,9},{5... | collective-permute-start | bytes 1658888 | tf_op jit(solution)/shard_map/ppermute | solution.py:669
  86.2 18.5 %collective-permute-start.7 = (bf16[1040,640]{1,0:T(8,128)(2,1)}, bf16[1040,640]{1,0:T(8,128)(2,1)}, u32[]{:S(2)}, u32[]{:S(2)}) collective-permute-start(bf16[1040,640]{1,0:T(8,128)(2,1)} %copy-done.5), channel_id=1, source_target_pairs={{0,1},{1,0},{2,3},{3,2},{4,5},{5,4},{6,7},{7,6},{8,9},{9,8},{10,11... | collective-permute-start | bytes 3993608 | tf_op jit(solution)/shard_map/ppermute | solution.py:672
  92.6 14.6 %collective-permute-start.6 = (bf16[1040,640]{1,0:T(8,128)(2,1)S(1)}, bf16[1040,640]{1,0:T(8,128)(2,1)S(1)}, u32[]{:S(2)}, u32[]{:S(2)}) collective-permute-start(bf16[1040,640]{1,0:T(8,128)(2,1)S(1)} %fusion.6.refs_4_), channel_id=1, source_target_pairs={{0,1},{1,0},{2,3},{3,2},{4,5},{5,4},{6,7},{7,6},{8,9},{9,8},{10,11... | collective-permute-start | bytes 3993608 | tf_op jit(solution)/shard_map/ppermute | solution.py:672
  98.8 9.5 %collective-permute-start.12 = (bf16[1040,640]{1,0:T(8,128)(2,1)}, bf16[1040,640]{1,0:T(8,128)(2,1)}, u32[]{:S(2)}, u32[]{:S(2)}) collective-permute-start(bf16[1040,640]{1,0:T(8,128)(2,1)} %collective-permute-done.9.refs_9_), channel_id=1, source_target_pairs={{0,1},{1,0},{2,3},{3,2},{4,5},{5,4},{6,7},{7,6},{8,9},{9,8},{10,11... | collective-permute-start | bytes 3993608 | tf_op jit(solution)/shard_map/ppermute | solution.py:672
  101.0 28.7 %collective-permute-start.14 = (bf16[2,288,960]{2,1,0:T(8,128)(2,1)}, bf16[2,288,960]{2,1,0:T(8,128)(2,1)}, u32[]{:S(2)}, u32[]{:S(2)}) collective-permute-start(bf16[2,288,960]{2,1,0:T(8,128)(2,1)} %pad_maximum_fusion.refs_0_), channel_id=1, source_target_pairs={{0,4},{4,0},{8,12},{12,8},{16,20},{20,16},{24,28},{28,24},{1,5},{5... | collective-permute-start | bytes 3317768 | tf_op jit(solution)/shard_map/ppermute | solution.py:669
  102.2 56.6 %collective-permute-start.18 = (bf16[2,288,960]{2,1,0:T(8,128)(2,1)}, bf16[2,288,960]{2,1,0:T(8,128)(2,1)}, u32[]{:S(2)}, u32[]{:S(2)}) collective-permute-start(bf16[2,288,960]{2,1,0:T(8,128)(2,1)} %pad_maximum_fusion.refs_0_), channel_id=1, source_target_pairs={{0,16},{4,20},{8,24},{12,28},{16,0},{20,4},{24,8},{28,12},{1,17},{... | collective-permute-start | bytes 3317768 | tf_op jit(solution)/shard_map/ppermute | solution.py:669
  104.8 54.0 %collective-permute-start.19 = (bf16[1024,256]{1,0:T(8,128)(2,1)}, bf16[1024,256]{1,0:T(8,128)(2,1)S(1)}, u32[]{:S(2)}, u32[]{:S(2)}) collective-permute-start(bf16[1024,256]{1,0:T(8,128)(2,1)} %get-tuple-element.109), channel_id=1, source_target_pairs={{0,8},{4,12},{8,0},{12,4},{16,24},{20,28},{24,16},{28,20},{1,9},{5... | collective-permute-start | bytes 1572872 | tf_op jit(solution)/shard_map/ppermute | solution.py:669
  129.7 4.4 %collective-permute-start.15 = (f32[2,3,128]{2,1,0:T(4,128)}, f32[2,3,128]{2,1,0:T(4,128)S(1)}, u32[]{:S(2)}, u32[]{:S(2)}) collective-permute-start(f32[2,3,128]{2,1,0:T(4,128)} %get-tuple-element.99), channel_id=1, source_target_pairs={{0,4},{4,0},{8,12},{12,8},{16,20},{20,16},{24,28},{28,24},{1,5},{5... | collective-permute-start | bytes 9224 | tf_op jit(solution)/shard_map/ppermute | solution.py:669
  130.5 25.9 %collective-permute-start.16 = (f32[2,3,128]{2,1,0:T(4,128)}, f32[2,3,128]{2,1,0:T(4,128)S(1)}, u32[]{:S(2)}, u32[]{:S(2)}) collective-permute-start(f32[2,3,128]{2,1,0:T(4,128)} %get-tuple-element.99), channel_id=1, source_target_pairs={{0,16},{4,20},{8,24},{12,28},{16,0},{20,4},{24,8},{28,12},{1,17},{... | collective-permute-start | bytes 9224 | tf_op jit(solution)/shard_map/ppermute | solution.py:669
  132.8 24.7 %collective-permute-start.17 = (f32[2,3,128]{2,1,0:T(4,128)}, f32[2,3,128]{2,1,0:T(4,128)S(1)}, u32[]{:S(2)}, u32[]{:S(2)}) collective-permute-start(f32[2,3,128]{2,1,0:T(4,128)} %get-tuple-element.99), channel_id=1, source_target_pairs={{0,20},{4,16},{8,28},{12,24},{16,4},{20,0},{24,12},{28,8},{1,21},{... | collective-permute-start | bytes 9224 | tf_op jit(solution)/shard_map/ppermute | solution.py:669
  158.8 28.1 %collective-permute-start.20 = (bf16[2,288,960]{2,1,0:T(8,128)(2,1)}, bf16[2,288,960]{2,1,0:T(8,128)(2,1)S(1)}, u32[]{:S(2)}, u32[]{:S(2)}) collective-permute-start(bf16[2,288,960]{2,1,0:T(8,128)(2,1)} %collective-permute-done.18.refs_2_), channel_id=1, source_target_pairs={{0,4},{4,0},{8,12},{12,8},{16,20},{20,16},{24,28},{28,24},{1,5},{5... | collective-permute-start | bytes 3317768 | tf_op jit(solution)/shard_map/ppermute | solution.py:669
  183.4 35.7 %collective-permute-start.24 = (bf16[2,288,768]{2,1,0:T(8,128)(2,1)}, bf16[2,288,768]{2,1,0:T(8,128)(2,1)}, u32[]{:S(2)}, u32[]{:S(2)}) collective-permute-start(bf16[2,288,768]{2,1,0:T(8,128)(2,1)} %get-tuple-element.105), channel_id=1, source_target_pairs={{0,4},{4,0},{8,12},{12,8},{16,20},{20,16},{24,28},{28,24},{1,5},{5... | collective-permute-start | bytes 2654216 | tf_op jit(solution)/shard_map/ppermute | solution.py:669
  214.7 7.0 %collective-permute-start.21 = (f32[2,3,160]{2,1,0:T(4,128)}, f32[2,3,160]{2,1,0:T(4,128)S(1)}, u32[]{:S(2)}, u32[]{:S(2)}) collective-permute-start(f32[2,3,160]{2,1,0:T(4,128)} %get-tuple-element.114), channel_id=1, source_target_pairs={{0,4},{4,0},{8,12},{12,8},{16,20},{20,16},{24,28},{28,24},{1,5},{5... | collective-permute-start | bytes 11528 | tf_op jit(solution)/shard_map/ppermute | solution.py:669
  215.4 6.3 %collective-permute-start.22 = (f32[2,3,160]{2,1,0:T(4,128)}, f32[2,3,160]{2,1,0:T(4,128)S(1)}, u32[]{:S(2)}, u32[]{:S(2)}) collective-permute-start(f32[2,3,160]{2,1,0:T(4,128)} %get-tuple-element.114), channel_id=1, source_target_pairs={{0,16},{4,20},{8,24},{12,28},{16,0},{20,4},{24,8},{28,12},{1,17},{... | collective-permute-start | bytes 11528 | tf_op jit(solution)/shard_map/ppermute | solution.py:669
  215.7 6.1 %collective-permute-start.23 = (f32[2,3,160]{2,1,0:T(4,128)}, f32[2,3,160]{2,1,0:T(4,128)S(1)}, u32[]{:S(2)}, u32[]{:S(2)}) collective-permute-start(f32[2,3,160]{2,1,0:T(4,128)} %get-tuple-element.114), channel_id=1, source_target_pairs={{0,20},{4,16},{8,28},{12,24},{16,4},{20,0},{24,12},{28,8},{1,21},{... | collective-permute-start | bytes 11528 | tf_op jit(solution)/shard_map/ppermute | solution.py:669
  222.4 47.0 %collective-permute-start.29 = (bf16[2,288,768]{2,1,0:T(8,128)(2,1)}, bf16[2,288,768]{2,1,0:T(8,128)(2,1)S(1)}, u32[]{:S(2)}, u32[]{:S(2)}) collective-permute-start(bf16[2,288,768]{2,1,0:T(8,128)(2,1)} %get-tuple-element.131), channel_id=1, source_target_pairs={{0,4},{4,0},{8,12},{12,8},{16,20},{20,16},{24,28},{28,24},{1,5},{5... | collective-permute-start | bytes 2654216 | tf_op jit(solution)/shard_map/ppermute | solution.py:669
  223.1 47.9 %collective-permute-start.30 = (bf16[2,288,768]{2,1,0:T(8,128)(2,1)}, bf16[2,288,768]{2,1,0:T(8,128)(2,1)S(1)}, u32[]{:S(2)}, u32[]{:S(2)}) collective-permute-start(bf16[2,288,768]{2,1,0:T(8,128)(2,1)} %convert_add_fusion), channel_id=1, source_target_pairs={{0,16},{4,20},{8,24},{12,28},{16,0},{20,4},{24,8},{28,12},{1,17},{... | collective-permute-start | bytes 2654216 | tf_op jit(solution)/shard_map/ppermute | solution.py:669
  243.8 27.5 %collective-permute-start.26 = (f32[3,864]{1,0:T(4,128)}, f32[3,864]{1,0:T(4,128)}, u32[]{:S(2)}, u32[]{:S(2)}) collective-permute-start(f32[3,864]{1,0:T(4,128)} %get-tuple-element.172), channel_id=1, source_target_pairs={{0,4},{4,0},{8,12},{12,8},{16,20},{20,16},{24,28},{28,24},{1,5},{5... | collective-permute-start | bytes 31112 | tf_op jit(solution)/shard_map/ppermute | solution.py:669
  244.3 27.0 %collective-permute-start.27 = (f32[3,864]{1,0:T(4,128)}, f32[3,864]{1,0:T(4,128)}, u32[]{:S(2)}, u32[]{:S(2)}) collective-permute-start(f32[3,864]{1,0:T(4,128)} %get-tuple-element.172), channel_id=1, source_target_pairs={{0,16},{4,20},{8,24},{12,28},{16,0},{20,4},{24,8},{28,12},{1,17},{... | collective-permute-start | bytes 31112 | tf_op jit(solution)/shard_map/ppermute | solution.py:669
  245.0 26.3 %collective-permute-start.28 = (f32[3,864]{1,0:T(4,128)}, f32[3,864]{1,0:T(4,128)}, u32[]{:S(2)}, u32[]{:S(2)}) collective-permute-start(f32[3,864]{1,0:T(4,128)} %get-tuple-element.172), channel_id=1, source_target_pairs={{0,20},{4,16},{8,28},{12,24},{16,4},{20,0},{24,12},{28,8},{1,21},{... | collective-permute-start | bytes 31112 | tf_op jit(solution)/shard_map/ppermute | solution.py:669
  269.4 42.4 %collective-permute-start.25 = (bf16[1024,288]{0,1:T(8,128)(2,1)}, bf16[1024,288]{0,1:T(8,128)(2,1)}, u32[]{:S(2)}, u32[]{:S(2)}) collective-permute-start(bf16[1024,288]{0,1:T(8,128)(2,1)} %copy.19), channel_id=1, source_target_pairs={{0,8},{4,12},{8,0},{12,4},{16,24},{20,28},{24,16},{28,20},{1,9},{5... | collective-permute-start | bytes 1769480 | tf_op jit(solution)/shard_map/ppermute | solution.py:669
  271.3 40.4 %collective-permute-start.31 = (bf16[2,288,960]{2,1,0:T(8,128)(2,1)}, bf16[2,288,960]{2,1,0:T(8,128)(2,1)S(1)}, u32[]{:S(2)}, u32[]{:S(2)}) collective-permute-start(bf16[2,288,960]{2,1,0:T(8,128)(2,1)} %get-tuple-element.133), channel_id=1, source_target_pairs={{0,4},{4,0},{8,12},{12,8},{16,20},{20,16},{24,28},{28,24},{1,5},{5... | collective-permute-start | bytes 3317768 | tf_op jit(solution)/shard_map/ppermute | solution.py:669
  274.3 37.4 %collective-permute-start.33 = (bf16[288,768]{1,0:T(8,128)(2,1)S(1)}, bf16[288,768]{1,0:T(8,128)(2,1)}, u32[]{:S(2)}, u32[]{:S(2)}) collective-permute-start(bf16[288,768]{1,0:T(8,128)(2,1)S(1)} %get-tuple-element.165), channel_id=1, source_target_pairs={{0,8},{4,12},{8,0},{12,4},{16,24},{20,28},{24,16},{28,20},{1,9},{5... | collective-permute-start | bytes 1327112 | tf_op jit(solution)/shard_map/ppermute | solution.py:669
  274.4 37.4 %collective-permute-start.32 = (f32[3,288]{1,0:T(4,128)S(1)}, f32[3,288]{1,0:T(4,128)S(1)}, u32[]{:S(2)}, u32[]{:S(2)}) collective-permute-start(f32[3,288]{1,0:T(4,128)S(1)} %pad_maximum_fusion.7), channel_id=1, source_target_pairs={{0,8},{4,12},{8,0},{12,4},{16,24},{20,28},{24,16},{28,20},{1,9},{5... | collective-permute-start | bytes 10376 | tf_op jit(solution)/shard_map/ppermute | solution.py:669
  311.8 5.3 %collective-permute-start.35 = (bf16[2,1024,640]{2,1,0:T(8,128)(2,1)}, bf16[2,1024,640]{2,1,0:T(8,128)(2,1)}, u32[]{:S(2)}, u32[]{:S(2)}) collective-permute-start(bf16[2,1024,640]{2,1,0:T(8,128)(2,1)} %get-tuple-element.144), channel_id=1, source_target_pairs={{0,1},{1,0},{2,3},{3,2},{4,5},{5,4},{6,7},{7,6},{8,9},{9,8},{10,11... | collective-permute-start | bytes 7864328 | tf_op jit(solution)/shard_map/ppermute | solution.py:672
  311.8 43.7 %collective-permute-start.34 = (bf16[2,1024,640]{2,1,0:T(8,128)(2,1)}, bf16[2,1024,640]{2,1,0:T(8,128)(2,1)}, u32[]{:S(2)}, u32[]{:S(2)}) collective-permute-start(bf16[2,1024,640]{2,1,0:T(8,128)(2,1)} %get-tuple-element.142), channel_id=1, source_target_pairs={{0,1},{1,0},{2,3},{3,2},{4,5},{5,4},{6,7},{7,6},{8,9},{9,8},{10,11... | collective-permute-start | bytes 7864328 | tf_op jit(solution)/shard_map/ppermute | solution.py:672
  319.7 32.6 %collective-permute-start.36 = (bf16[1024,640]{1,0:T(8,128)(2,1)}, bf16[1024,640]{1,0:T(8,128)(2,1)}, u32[]{:S(2)}, u32[]{:S(2)}) collective-permute-start(bf16[1024,640]{1,0:T(8,128)(2,1)} %join.8), channel_id=1, source_target_pairs={{0,2},{1,3},{2,0},{3,1},{4,6},{5,7},{6,4},{7,5},{8,10},{9,11},{10,... | collective-permute-start | bytes 3932168 | tf_op jit(solution)/shard_map/ppermute | solution.py:672
  320.0 28.0 %collective-permute-start.37 = (bf16[2,288,960]{2,1,0:T(8,128)(2,1)}, bf16[2,288,960]{2,1,0:T(8,128)(2,1)S(1)}, u32[]{:S(2)}, u32[]{:S(2)}) collective-permute-start(bf16[2,288,960]{2,1,0:T(8,128)(2,1)} %get-tuple-element.135), channel_id=1, source_target_pairs={{0,4},{4,0},{8,12},{12,8},{16,20},{20,16},{24,28},{28,24},{1,5},{5... | collective-permute-start | bytes 3317768 | tf_op jit(solution)/shard_map/ppermute | solution.py:669
  320.9 28.4 %collective-permute-start.38 = (bf16[288,960]{1,0:T(8,128)(2,1)}, bf16[288,960]{1,0:T(8,128)(2,1)S(1)}, u32[]{:S(2)}, u32[]{:S(2)}) collective-permute-start(bf16[288,960]{1,0:T(8,128)(2,1)} %join.7), channel_id=1, source_target_pairs={{0,16},{4,20},{8,24},{12,28},{16,0},{20,4},{24,8},{28,12},{1,17},{... | collective-permute-start | bytes 1658888 | tf_op jit(solution)/shard_map/ppermute | solution.py:669
  358.2 30.9 %collective-permute-start.39 = (bf16[1024,640]{1,0:T(8,128)(2,1)}, bf16[1024,640]{1,0:T(8,128)(2,1)S(1)}, u32[]{:S(2)}, u32[]{:S(2)}) collective-permute-start(bf16[1024,640]{1,0:T(8,128)(2,1)} %join.11), channel_id=1, source_target_pairs={{0,2},{1,3},{2,0},{3,1},{4,6},{5,7},{6,4},{7,5},{8,10},{9,11},{10,... | collective-permute-start | bytes 3932168 | tf_op jit(solution)/shard_map/ppermute | solution.py:672
  360.0 44.6 %collective-permute-start.40 = (bf16[1024,640]{1,0:T(8,128)(2,1)}, bf16[1024,640]{1,0:T(8,128)(2,1)}, u32[]{:S(2)}, u32[]{:S(2)}) collective-permute-start(bf16[1024,640]{1,0:T(8,128)(2,1)} %join.10), channel_id=1, source_target_pairs={{0,8},{4,12},{8,0},{12,4},{16,24},{20,28},{24,16},{28,20},{1,9},{5... | collective-permute-start | bytes 3932168 | tf_op jit(solution)/shard_map/ppermute | solution.py:669
  371.2 44.9 %collective-permute-start.42 = (bf16[288,960]{1,0:T(8,128)(2,1)S(1)}, bf16[288,960]{1,0:T(8,128)(2,1)}, u32[]{:S(2)}, u32[]{:S(2)}) collective-permute-start(bf16[288,960]{1,0:T(8,128)(2,1)S(1)} %copy-done.13), channel_id=1, source_target_pairs={{0,8},{4,12},{8,0},{12,4},{16,24},{20,28},{24,16},{28,20},{1,9},{5... | collective-permute-start | bytes 1658888 | tf_op jit(solution)/shard_map/ppermute | solution.py:669
  373.2 40.6 %collective-permute-start.41 = (bf16[288,960]{1,0:T(8,128)(2,1)}, bf16[288,960]{1,0:T(8,128)(2,1)}, u32[]{:S(2)}, u32[]{:S(2)}) collective-permute-start(bf16[288,960]{1,0:T(8,128)(2,1)} %join.12), channel_id=1, source_target_pairs={{0,16},{4,20},{8,24},{12,28},{16,0},{20,4},{24,8},{28,12},{1,17},{... | collective-permute-start | bytes 1658888 | tf_op jit(solution)/shard_map/ppermute | solution.py:669
  (16 other events, 121.9 us)

commit v5 on v4

--- a/solution.py
+++ b/solution.py
@@ -315,13 +315,21 @@
     )(place, *w, *x, bias, *ups, *([] if xrel else [keep_w]))
 
 
-def finish_kernel(n, up_at, place, g_ref, up0, up1, keep_ref, seg_ref, all_ref, h0, h1, gg_ref, gf_ref, gp_ref, gb_ref, d_s, s_s, q_s, p_s, c_s):
+def finish_kernel(n, up_at, place, g_ref, up0, up1, keep_ref, seg_ref, all_ref, *refs):
+    count = len(refs) - 11
+    before, refs = refs[:count], refs[count:]
+    h0, h1, gg_ref, gf_ref, gp_ref, gb_ref, d_s, s_s, q_s, p_s, c_s = refs
     t, c = up0.shape
     span = t // SEGS
     lanes = cuts(c)
     heads = n // 4
     hh, ll, pp = place[0], place[1], place[2]
     ups, hids = (up0, up1), (h0, h1)
+    at = 0
+    for ref in before:
+        h1[:, at : at + ref.shape[1]] = ref[...]
+        at += ref.shape[1]
+    firsts_at = (0, at)
     for slot in range(2):
 
         def act(r, _, slot=slot):
@@ -400,7 +408,7 @@
                 keep = keep_ref[full, :w]
                 gs = q_s[slot, k_l, apart, :w]
                 oh = o * s_s[slot, k_l, apart, :w]
-                hids[slot][rows, ch] = oh.astype(BF)
+                hids[slot][rows, firsts_at[slot] + lo : firsts_at[slot] + lo + w] = oh.astype(BF)
                 gi = gs * intake
                 grads = (
                     gi * (1.0 - z * z),
@@ -429,16 +437,16 @@
             gb_ref[0:1, k * c + lo : k * c + lo + w] = jnp.sum(sums[3 * k_l + k], axis=0, keepdims=True)
 
 
-def finish(n, up_at, place, gates, ups, keep_w, seg, every):
+def finish(n, up_at, place, gates, ups, keep_w, seg, every, before=()):
     t, c = ups[0].shape
     lt = len(cuts(c))
     shape = jax.ShapeDtypeStruct
     return pl.pallas_call(
         functools.partial(finish_kernel, n, up_at),
-        in_specs=[SMEM_SPEC] + [VMEM_SPEC] * 6,
+        in_specs=[SMEM_SPEC] + [VMEM_SPEC] * (6 + len(before)),
         out_shape=[
             shape((t, c), BF),
-            shape((t, c), BF),
+            shape((t, ceil_to(c + sum(v.shape[1] for v in before), LANES if before else 1)), BF),
             shape((2 * t, 6 * c), BF),
             shape((2, 3 * c), F32),
             shape((2 * EDGE, 6 * c), BF),
@@ -448,7 +456,7 @@
         compiler_params=params(),
         cost_estimate=TINY,
         name="finish",
-    )(place, gates, *ups, keep_w, seg, every)
+    )(place, gates, *ups, keep_w, seg, every, *before)
 
 
 def wgrad_kernel(dw, place, x_ref, halo_ref, gg_ref, gp_ref, *refs):
@@ -593,32 +601,41 @@
     )(*arrays)
 
 
-def unpack_w_kernel(widths, place, *refs):
+def unpack_w_kernel(widths, terms, place, *refs):
     count = len(widths)
-    outs = refs[2 * count :]
+    outs = refs[-2:]
+    last = [
+        ref if at is None else ref.at[at] for ref, at in zip(refs[2 * count - 2 :], terms)
+    ]
+    pieces = [*refs[: 2 * count - 2], None, refs[2 * count - 2 + len(terms)]]
     low = place[1] == 0
     for tap in range(2):
         for k in range(3):
             mine, other = [], []
             for i, c in enumerate(widths):
                 for _, lo, w in cuts(c):
-                    mine.append(refs[2 * i][:, group(tap * 3 + k, lo, w)].astype(F32))
-                    other.append(refs[2 * i + 1][:, group(tap * 3 + k, lo, w)].astype(F32))
+                    cols = group(tap * 3 + k, lo, w)
+                    if pieces[2 * i] is None:
+                        mine.append(functools.reduce(lambda v, ref: v + ref[:, cols].astype(F32), last, 0.0))
+                    else:
+                        mine.append(pieces[2 * i][:, cols].astype(F32))
+                    other.append(pieces[2 * i + 1][:, cols].astype(F32))
             mine, other = jnp.concatenate(mine, axis=1), jnp.concatenate(other, axis=1)
             outs[tap][k] = jnp.concatenate([jnp.where(low, mine, other), jnp.where(low, other, mine)], axis=1)
 
 
-def unpack_weights(widths, place, pairs):
-    rows = pairs[0].shape[0]
+def unpack_weights(widths, place, pairs, last, other):
+    rows = other.shape[0]
     shape = jax.ShapeDtypeStruct((3, rows, 2 * sum(widths)), F32)
+
     return pl.pallas_call(
-        functools.partial(unpack_w_kernel, widths),
-        in_specs=[SMEM_SPEC] + [VMEM_SPEC] * len(pairs),
+        functools.partial(unpack_w_kernel, widths, tuple(at for _, at in last)),
+        in_specs=[SMEM_SPEC] + [VMEM_SPEC] * (len(pairs) + len(last) + 1),
         out_shape=[shape, shape],
         compiler_params=params(),
         cost_estimate=TINY,
         name="unpack_weights",
-    )(place, *pairs)
+    )(place, *pairs, *[v for v, _ in last], other)
 
 
 def unpack_h_kernel(widths, place, *refs):
@@ -628,7 +645,7 @@
     def body(r, _):
         rows = pl.ds(pl.multiple_of(r * TM, TM), TM)
         mine = jnp.concatenate([refs[i][rows, :].astype(F32) for i in range(len(widths))], axis=1)
-        other = refs[len(widths)][rows, :].astype(F32)
+        other = refs[len(widths)][rows, : sum(widths)].astype(F32)
         both_halves = jnp.concatenate([jnp.where(low, mine, other), jnp.where(low, other, mine)], axis=1)
         out_ref[rows, :] = both_halves.astype(BF)
         return 0
@@ -780,7 +797,8 @@
             (near_sum,) = over_p([(kh0, here0, after(away0, every))])
             h_sums.append(near_sum)
             every = every_now
-        h0, h1, gg, gf, gp, gb = finish(n, 0, place, gates, ups[i], keep_w, seg, every)
+        before = hidden_other if i == count - 1 else ()
+        h0, h1, gg, gf, gp, gb = finish(n, 0, place, gates, ups[i], keep_w, seg, every, before)
         hidden_mine.append(h0)
         hidden_other.append(h1)
         g_first.append(gf)
@@ -788,7 +806,7 @@
         if i == count - 1:
             parts = jnp.concatenate([jnp.concatenate(g_first, axis=1), jnp.concatenate(g_bias, axis=1)], axis=0)
             around = [parts if r == (0, 0) else seq_to(parts, r[0], 0, r[1]) for r in group]
-            hidden_came = seq_to(after(jnp.concatenate(hidden_other, axis=1), parts), 0, 1, 0)
+            hidden_came = seq_to(after(h1, parts), 0, 1, 0)
         needs = list(around) if i == count - 1 else []
         if i > 0:
             total = over_h(waiting, h_sums)
@@ -842,14 +860,13 @@
     grad_x = kept0[0].astype(F32) + c_came0[0].astype(F32) + y_came0.astype(F32) + l_came.astype(F32)
     grad_x = grad_x[:, :dl].astype(BF)
     h_rest = [after(v, grad_x) for v in h_rest]
-    total = join([(waiting[-1][1], 1), (p_came[-1], 1)] + [(v, None) for v in h_rest], LATER)
-    w_pairs += [total, l_total]
+    last = [(waiting[-1][1], 1), (p_came[-1], 1)] + [(v, None) for v in h_rest]
 
     grad_bias = jnp.concatenate(
         [jnp.where(low, bias_half, bias_other), jnp.where(low, bias_other, bias_half)], axis=1
     )
     hidden = unpack_hidden(widths, place, hidden_mine, hidden_came)
-    grad_now, grad_prev = unpack_weights(widths, place, w_pairs)
+    grad_now, grad_prev = unpack_weights(widths, place, w_pairs, last, l_total)
     return hidden, grad_x, grad_now, grad_prev, grad_bias
 
 

time: 421 us -> 420 us (level)
    pallas_call x7 -> x6, Pallas kernels: 17.1 us -> 14.8 us  [join(): pl.pallas_call(join_kernel, grid=(steps,), in_specs=[spec(v, at) for v, a...]
    unnamed x45 -> x47, local copies, waits for them, and re-layouts: 7.93 us -> 8.74 us
  transfers between devices with their start and end apart: 43 -> 43, of which waited for: 18 -> 19; matrix products, arithmetic and copies ran while one was open for 7% -> 5% of each run, Pallas kernels for 40% -> 39%
where the time goes in v5:
time: 420 us
  Pallas kernels  176 us (42%)
  waiting for transfers between devices  156 us (37%)
  starting transfers between devices  57.7 us (14%)
  other arithmetic  15 us (4%)
  local copies, waits for them, and re-layouts  13.3 us (3%)
    ppermute x32, waiting for transfers between devices, seq_to(): return lax.ppermute(v, 'seq', route)  131 us
    ppermute x32, starting transfers between devices, seq_to(): return lax.ppermute(v, 'seq', route)  49.7 us
    pallas_call x2, Pallas kernels, gates_and_totals(): pl.pallas_call(functools.partial(gates_kernel, plan), in_specs=[SMEM_SPEC...  46.9 us
    pallas_call x2, Pallas kernels, weight_grads(): pl.pallas_call(functools.partial(wgrad_kernel, dw), grid_spec=pltpu.Prefe...  34.2 us
    pallas_call x1, Pallas kernels, input_grads(): pl.pallas_call(xgrad_kernel, grid_spec=pltpu.PrefetchScalarGridSpec(num_s...  34.1 us
    pallas_call x2, Pallas kernels, finish(): pl.pallas_call(functools.partial(finish_kernel, n, up_at), in_specs=[SMEM...  25.1 us
    ppermute x10, waiting for transfers between devices, gate_to(): return lax.ppermute(v, 'gate', [(i, i ^ d_a * 2 + d_b) for i in range(m)])  24.2 us
    pallas_call x6, Pallas kernels, join(): pl.pallas_call(join_kernel, grid=(steps,), in_specs=[spec(v, at) for v, a...  14.8 us
  transfers between devices with their start and end apart: 43, of which 19 were waited for; matrix products, arithmetic and copies ran while one was open for 5% of the time, Pallas kernels for 39%

profile of v5, /device:TPU:0, one launch (start us, length us, event | category | flops | bytes accessed | tf_op | source)
XLA Modules:
  0.0 419.6 jit_solution(4431578217500470155)
XLA Ops:
  1.4 3.3 pack_weights.2
  4.7 3.0 collective-permute-start
  8.5 3.4 collective-permute-start.4
  15.2 2.9 collective-permute-done
  18.1 4.8 %collective-permute-start.8 = (bf16[1040,640]{1,0:T(8,128)(2,1)S(1)}, bf16[1040,640]{1,0:T(8,128)(2,1)}, u32[]{:S(2)}, u32[]{:S(2)}) collective-permute-start(bf16[1040,640]{1,0:T(8,128)(2,1)S(1)} %fusion.6.refs_4_), channel_id=1, source_target_pairs={{0,8},{4,12},{8,0},{12,4},{16,24},{20,28},{24,16},{28,20},{1,9},{5... | collective-permute-start | bytes 3993608 | tf_op jit(solution)/shard_map/ppermute | solution.py:686
  23.1 2.7 collective-permute-start.2
  25.7 17.0 %collective-permute-done.1.refs_1_ = bf16[2,288,768]{2,1,0:T(8,128)(2,1)S(1)} collective-permute-done((bf16[2,288,768]{2,1,0:T(8,128)(2,1)S(1)}, bf16[2,288,768]{2,1,0:T(8,128)(2,1)S(1)}, u32[]{:S(2)}, u32[]{:S(2)}) %collective-permute-start.1) | collective-permute-done | bytes 884768 | tf_op jit(solution)/shard_map/ppermute | solution.py:686
  43.5 26.2 %collective-permute-done.8.refs_8_ = bf16[1040,640]{1,0:T(8,128)(2,1)} collective-permute-done((bf16[1040,640]{1,0:T(8,128)(2,1)S(1)}, bf16[1040,640]{1,0:T(8,128)(2,1)}, u32[]{:S(2)}, u32[]{:S(2)}) %collective-permute-start.8) | collective-permute-done | bytes 1331232 | tf_op jit(solution)/shard_map/ppermute | solution.py:686
  72.0 5.1 %pack_up.1 = (bf16[1024,128]{1,0:T(8,128)(2,1)}, bf16[1024,128]{1,0:T(8,128)(2,1)}, bf16[1024,160]{1,0:T(8,128)(2,1)}, bf16[1024,256]{1,0:T(8,128)(2,1)}) custom-call(s32[5]{0:T(128)} %stack.91.place, bf16[1024,576]{1,0:T(8,128)(2,1)} %copy.13.up_ref), custom_call_target="tpu_custom_call" | custom-call | flops 1024 | bytes 1024 | tf_op jit(solution)/shard_map/pack_up/pallas_call | solution.py:114
  77.0 2.0 collective-permute-start.11
  79.0 4.0 pack_weights.3
  83.0 3.3 collective-permute-done.11.refs_14_.up1
  86.3 6.3 %collective-permute-done.3.refs_3_ = bf16[2,288,768]{2,1,0:T(8,128)(2,1)} collective-permute-done((bf16[2,288,768]{2,1,0:T(8,128)(2,1)}, bf16[2,288,768]{2,1,0:T(8,128)(2,1)}, u32[]{:S(2)}, u32[]{:S(2)}) %collective-permute-start.3) | collective-permute-done | bytes 884768 | tf_op jit(solution)/shard_map/ppermute | solution.py:686
  92.7 6.2 %collective-permute-done.9.refs_9_ = bf16[1040,640]{1,0:T(8,128)(2,1)} collective-permute-done((bf16[1040,640]{1,0:T(8,128)(2,1)}, bf16[1040,640]{1,0:T(8,128)(2,1)}, u32[]{:S(2)}, u32[]{:S(2)}) %collective-permute-start.9) | collective-permute-done | bytes 1331232 | tf_op jit(solution)/shard_map/ppermute | solution.py:689
  98.9 2.2 pad_maximum_fusion.refs_0_
  102.3 2.6 collective-permute-start.18
  108.4 20.2 %gates_and_totals.2 = (f32[3,2048,128]{2,1,0:T(8,128)}, f32[2,3,8,128]{3,2,1,0:T(8,128)}, f32[2,3,128]{2,1,0:T(4,128)}, bf16[2048,2560]{1,0:T(8,128)(2,1)}, bf16...) custom-call(s32[5]{0:T(128)} %stack.91.place, bf16[2,288,768]{2,1,0:T(8,128)(2,1)} %copy-done.3, ...), custom_call_target="tpu_custom_call" | custom-call | flops 1024 | bytes 1024 | tf_op jit(solution)/shard_map/gates_and_totals/pallas_call | solution.py:293
  130.5 2.4 collective-permute-start.16
  134.2 22.2 %collective-permute-done.16 = f32[2,3,128]{2,1,0:T(4,128)S(1)} collective-permute-done((f32[2,3,128]{2,1,0:T(4,128)}, f32[2,3,128]{2,1,0:T(4,128)S(1)}, u32[]{:S(2)}, u32[]{:S(2)}) %collective-permute-start.16) | collective-permute-done | bytes 3104 | tf_op jit(solution)/shard_map/ppermute | solution.py:686
  159.5 8.7 %finish.2 = (bf16[1024,128]{1,0:T(8,128)(2,1)}, bf16[1024,128]{1,0:T(8,128)(2,1)}, bf16[2048,768]{1,0:T(8,128)(2,1)}, f32[2,384]{1,0:T(2,128)}, bf16[32,768]{1,0:T(8,128)(2,1)}, /*index=5*/f32[1,384]{1,0:T(1,128)}) custom-call(s32[5]{0:T(128)} %stack.91.place, f32[3,2048,128]{2,1,0:T(8,128)} %get-tuple-element.92.g_ref, ...), custom_call_target="tpu_custom_call" | custom-call | flops 1024 | bytes 1024 | tf_op jit(solution)/shard_map/finish/pallas_call | solution.py:444
  168.2 15.2 %weight_grads.2 = (bf16[2,288,768]{2,1,0:T(8,128)(2,1)}, bf16[2,288,768]{2,1,0:T(8,128)(2,1)}, bf16[2,288,768]{2,1,0:T(8,128)(2,1)}, bf16[2,288,768]{2,1,0:T(8,128)(2,1)}) custom-call(s32[5]{0:T(128)} %stack.91.place, bf16[2048,2560]{1,0:T(8,128)(2,1)} %get-tuple-element.101.x_ref.refs_4_, bf16[32,2560]{1,0:T(8,128)(2,1)} %get-tuple-element.102.halo_ref.refs_5_, ...), custom_call_target="tpu_custom_call" | custom-call | flops 1024 | bytes 1024 | tf_op jit(solution)/shard_map/weight_grads/pallas_call | solution.py:488
  188.1 26.7 %gates_and_totals.3 = (f32[3,2048,160]{2,1,0:T(8,128)}, f32[2,3,8,160]{3,2,1,0:T(8,128)}, f32[2,3,160]{2,1,0:T(4,128)}, bf16[4,640,960]{2,1,0:T(8,128)(2,1)}) custom-call(s32[5]{0:T(128)} %stack.91.place, bf16[2,288,960]{2,1,0:T(8,128)(2,1)} %pad_maximum_fusion.refs_0_, bf16[2,288,960]{2,1,0:T(8,128)(2,1)} %collective-permute-done.14.refs_1_, ...), custom_call_target="tpu_custom_call" | custom-call | flops 1024 | bytes 1024 | tf_op jit(solution)/shard_map/gates_and_totals/pallas_call | solution.py:293
  215.7 3.5 collective-permute-start.23
  219.2 2.6 convert_add_fusion
  223.2 3.0 collective-permute-start.30
  226.2 16.4 %finish.3 = (bf16[1024,160]{1,0:T(8,128)(2,1)}, bf16[1024,384]{1,0:T(8,128)(2,1)}, bf16[2048,960]{1,0:T(8,128)(2,1)}, f32[2,480]{1,0:T(2,128)}, bf16[32,960]{1,0:T(8,128)(2,1)}, /*index=5*/f32[1,480]{1,0:T(1,128)}) custom-call(s32[5]{0:T(128)} %stack.91.place, f32[3,2048,160]{2,1,0:T(8,128)} %get-tuple-element.112.g_ref, ...), custom_call_target="tpu_custom_call" | custom-call | flops 1024 | bytes 1024 | tf_op jit(solution)/shard_map/finish/pallas_call | solution.py:444
  244.6 3.2 collective-permute-start.28
  247.8 18.9 %weight_grads.3 = (bf16[2,288,960]{2,1,0:T(8,128)(2,1)}, bf16[2,288,960]{2,1,0:T(8,128)(2,1)}, bf16[2,288,960]{2,1,0:T(8,128)(2,1)}, bf16[2,288,960]{2,1,0:T(8,128)(2,1)}) custom-call(s32[5]{0:T(128)} %stack.91.place, bf16[2048,2560]{1,0:T(8,128)(2,1)} %get-tuple-element.101.x_ref.refs_4_, bf16[32,2560]{1,0:T(8,128)(2,1)} %get-tuple-element.102.halo_ref.refs_5_, ...), custom_call_target="tpu_custom_call" | custom-call | flops 1024 | bytes 1024 | tf_op jit(solution)/shard_map/weight_grads/pallas_call | solution.py:488
  272.4 2.0 collective-permute-start.32
  275.6 34.1 %input_grads.1 = (bf16[2,1024,640]{2,1,0:T(8,128)(2,1)}, bf16[2,1024,640]{2,1,0:T(8,128)(2,1)}, bf16[2,1024,640]{2,1,0:T(8,128)(2,1)}, bf16[2,1024,640]{2,1,0:T(8,128)(2,1)}) custom-call(s32[5]{0:T(128)} %stack.91.place, bf16[2048,768]{1,0:T(8,128)(2,1)} %get-tuple-element.103.gg_ref.refs_0_, bf16[2048,960]{1,0:T(8,128)(2,1)} %get-tuple-element.126.gg_ref.refs_1_, ...), custom_call_target="tpu_custom_call" | custom-call | flops 1024 | bytes 1024 | tf_op jit(solution)/shard_map/input_grads/pallas_call | solution.py:555
  310.8 2.0 join.6
  312.8 2.3 collective-permute-done.35.refs_1_
  315.1 2.7 join.7
  318.9 2.9 collective-permute-start.38
  321.8 24.2 %collective-permute-done.37.refs_1_.refs_3_ = bf16[2,288,960]{2,1,0:T(8,128)(2,1)S(1)} collective-permute-done((bf16[2,288,960]{2,1,0:T(8,128)(2,1)}, bf16[2,288,960]{2,1,0:T(8,128)(2,1)S(1)}, u32[]{:S(2)}, u32[]{:S(2)}) %collective-permute-start.37) | collective-permute-done | bytes 1105952 | tf_op jit(solution)/shard_map/ppermute | solution.py:686
  348.1 2.3 join.8
  350.4 3.2 join.9
  353.5 2.7 join.10
  358.6 3.8 unpack_hidden.1
  362.5 2.4 copy.14
  364.9 2.0 join.11
  366.9 2.0 collective-permute-start.42
  370.3 2.0 add_bitcast_fusion
  372.2 14.9 %collective-permute-done.39 = bf16[1024,640]{1,0:T(8,128)(2,1)S(1)} collective-permute-done((bf16[1024,640]{1,0:T(8,128)(2,1)}, bf16[1024,640]{1,0:T(8,128)(2,1)S(1)}, u32[]{:S(2)}, u32[]{:S(2)}) %collective-permute-start.39) | collective-permute-done | bytes 1310752 | tf_op jit(solution)/shard_map/ppermute | solution.py:689
  387.1 15.5 %collective-permute-done.40 = bf16[1024,640]{1,0:T(8,128)(2,1)} collective-permute-done((bf16[1024,640]{1,0:T(8,128)(2,1)}, bf16[1024,640]{1,0:T(8,128)(2,1)}, u32[]{:S(2)}, u32[]{:S(2)}) %collective-permute-start.40) | collective-permute-done | bytes 1310752 | tf_op jit(solution)/shard_map/ppermute | solution.py:686
  405.9 5.9 %collective-permute-done.41.refs_4_ = bf16[288,960]{1,0:T(8,128)(2,1)} collective-permute-done((bf16[288,960]{1,0:T(8,128)(2,1)}, bf16[288,960]{1,0:T(8,128)(2,1)}, u32[]{:S(2)}, u32[]{:S(2)}) %collective-permute-start.41) | collective-permute-done | bytes 552992 | tf_op jit(solution)/shard_map/ppermute | solution.py:686
  411.8 2.1 collective-permute-done.42.refs_5_
  414.7 4.9 %unpack_weights.1 = (f32[3,288,576]{2,1,0:T(8,128)}, f32[3,288,576]{2,1,0:T(8,128)}) custom-call(s32[5]{0:T(128)} %stack.91.place, bf16[288,768]{1,0:T(8,128)(2,1)} %get-tuple-element.161.refs_0_, bf16[288,768]{1,0:T(8,128)(2,1)} %copy-done.15, bf16[2,288,960]{2,1,0:T(8,128)(2,1)} %get-tuple-element.147.refs_0_.refs_2_, bf16[2,288,960]{2,1,0:T(8,128)(2,1)} %copy-done.1, ...), custom_call_target="tpu_custom_call" | custom-call | flops 1024 | bytes 1024 | tf_op jit(solution)/shard_map/unpack_weights/pallas_call | solution.py:631
  (134 shorter events, 46.8 us)
Async XLA Ops:
  4.7 13.4 %collective-permute-start = (bf16[288,768]{1,0:T(8,128)(2,1)}, bf16[288,768]{1,0:T(8,128)(2,1)S(1)}, u32[]{:S(2)}, u32[]{:S(2)}) collective-permute-start(bf16[288,768]{1,0:T(8,128)(2,1)} %get-tuple-element.81), channel_id=1, source_target_pairs={{0,8},{4,12},{8,0},{12,4},{16,24},{20,28},{24,16},{28,20},{1,9},{5... | collective-permute-start | bytes 1327112 | tf_op jit(solution)/shard_map/ppermute | solution.py:686
  8.5 4.7 %collective-permute-start.4 = (bf16[1,576]{1,0:T(2,128)(2,1)S(1)}, bf16[1,576]{1,0:T(2,128)(2,1)S(1)}, u32[]{:S(2)}, u32[]{:S(2)}) collective-permute-start(bf16[1,576]{1,0:T(2,128)(2,1)S(1)} %slice.61), channel_id=1, source_target_pairs={{0,4},{4,8},{8,12},{12,16},{16,20},{20,24},{24,28},{1,5},{5,9},{9,... | collective-permute-start | bytes 3464 | tf_op jit(solution)/shard_map/ppermute | solution.py:694
  13.6 79.1 %copy-start = (bf16[1040,640]{1,0:T(8,128)(2,1)}, bf16[1040,640]{1,0:T(8,128)(2,1)S(1)}, u32[]{:S(2)}) copy-start(bf16[1040,640]{1,0:T(8,128)(2,1)S(1)} %fusion.6.refs_4_) | copy-start | bytes 3993604
  13.6 56.9 %copy-start.9 = (bf16[1024,576]{0,1:T(8,128)(2,1)S(1)}, bf16[1024,576]{0,1:T(8,128)(2,1)}, u32[]{:S(2)}) copy-start(bf16[1024,576]{0,1:T(8,128)(2,1)} %param.11) | copy-start | bytes 3538948
  13.6 29.9 %collective-permute-start.5 = (bf16[1040,640]{1,0:T(8,128)(2,1)S(1)}, bf16[1040,640]{1,0:T(8,128)(2,1)S(1)}, u32[]{:S(2)}, u32[]{:S(2)}) collective-permute-start(bf16[1040,640]{1,0:T(8,128)(2,1)S(1)} %fusion.6.refs_4_), channel_id=1, source_target_pairs={{0,2},{1,3},{2,0},{3,1},{4,6},{5,7},{6,4},{7,5},{8,10},{9,11},{10,... | collective-permute-start | bytes 3993608 | tf_op jit(solution)/shard_map/ppermute | solution.py:689
  18.1 51.6 %collective-permute-start.8 = (bf16[1040,640]{1,0:T(8,128)(2,1)S(1)}, bf16[1040,640]{1,0:T(8,128)(2,1)}, u32[]{:S(2)}, u32[]{:S(2)}) collective-permute-start(bf16[1040,640]{1,0:T(8,128)(2,1)S(1)} %fusion.6.refs_4_), channel_id=1, source_target_pairs={{0,8},{4,12},{8,0},{12,4},{16,24},{20,28},{24,16},{28,20},{1,9},{5... | collective-permute-start | bytes 3993608 | tf_op jit(solution)/shard_map/ppermute | solution.py:686
  23.0 46.7 %copy-start.3 = (bf16[2,288,768]{2,1,0:T(8,128)(2,1)}, bf16[2,288,768]{2,1,0:T(8,128)(2,1)S(1)}, u32[]{:S(2)}) copy-start(bf16[2,288,768]{2,1,0:T(8,128)(2,1)S(1)} %pad_maximum_fusion.1.refs_0_) | copy-start | bytes 2654212
  23.0 19.7 %collective-permute-start.1 = (bf16[2,288,768]{2,1,0:T(8,128)(2,1)S(1)}, bf16[2,288,768]{2,1,0:T(8,128)(2,1)S(1)}, u32[]{:S(2)}, u32[]{:S(2)}) collective-permute-start(bf16[2,288,768]{2,1,0:T(8,128)(2,1)S(1)} %pad_maximum_fusion.1.refs_0_), channel_id=1, source_target_pairs={{0,4},{4,0},{8,12},{12,8},{16,20},{20,16},{24,28},{28,24},{1,5},{5... | collective-permute-start | bytes 2654216 | tf_op jit(solution)/shard_map/ppermute | solution.py:686
  23.1 47.2 %collective-permute-start.2 = (bf16[2,288,768]{2,1,0:T(8,128)(2,1)S(1)}, bf16[2,288,768]{2,1,0:T(8,128)(2,1)}, u32[]{:S(2)}, u32[]{:S(2)}) collective-permute-start(bf16[2,288,768]{2,1,0:T(8,128)(2,1)S(1)} %pad_maximum_fusion.1.refs_0_), channel_id=1, source_target_pairs={{0,16},{4,20},{8,24},{12,28},{16,0},{20,4},{24,8},{28,12},{1,17},{... | collective-permute-start | bytes 2654216 | tf_op jit(solution)/shard_map/ppermute | solution.py:686
  42.7 27.5 %copy-start.12 = (bf16[2,288,768]{2,1,0:T(8,128)(2,1)}, bf16[2,288,768]{2,1,0:T(8,128)(2,1)S(1)}, u32[]{:S(2)}) copy-start(bf16[2,288,768]{2,1,0:T(8,128)(2,1)S(1)} %collective-permute-done.1.refs_1_) | copy-start | bytes 2654212
  43.5 26.7 %copy-start.5 = (bf16[1040,640]{1,0:T(8,128)(2,1)}, bf16[1040,640]{1,0:T(8,128)(2,1)S(1)}, u32[]{:S(2)}) copy-start(bf16[1040,640]{1,0:T(8,128)(2,1)S(1)} %collective-permute-done.5.refs_5_) | copy-start | bytes 3993604
  69.7 29.2 %collective-permute-start.9 = (bf16[1040,640]{1,0:T(8,128)(2,1)}, bf16[1040,640]{1,0:T(8,128)(2,1)}, u32[]{:S(2)}, u32[]{:S(2)}) collective-permute-start(bf16[1040,640]{1,0:T(8,128)(2,1)} %collective-permute-done.8.refs_8_), channel_id=1, source_target_pairs={{0,2},{1,3},{2,0},{3,1},{4,6},{5,7},{6,4},{7,5},{8,10},{9,11},{10,... | collective-permute-start | bytes 3993608 | tf_op jit(solution)/shard_map/ppermute | solution.py:689
  70.2 32.1 %collective-permute-start.10 = (bf16[1040,640]{1,0:T(8,128)(2,1)}, bf16[1040,640]{1,0:T(8,128)(2,1)}, u32[]{:S(2)}, u32[]{:S(2)}) collective-permute-start(bf16[1040,640]{1,0:T(8,128)(2,1)} %collective-permute-done.8.refs_8_), channel_id=1, source_target_pairs={{0,1},{1,0},{2,3},{3,2},{4,5},{5,4},{6,7},{7,6},{8,9},{9,8},{10,11... | collective-permute-start | bytes 3993608 | tf_op jit(solution)/shard_map/ppermute | solution.py:689
  70.2 22.4 %collective-permute-start.3 = (bf16[2,288,768]{2,1,0:T(8,128)(2,1)}, bf16[2,288,768]{2,1,0:T(8,128)(2,1)}, u32[]{:S(2)}, u32[]{:S(2)}) collective-permute-start(bf16[2,288,768]{2,1,0:T(8,128)(2,1)} %collective-permute-done.2.refs_2_), channel_id=1, source_target_pairs={{0,4},{4,0},{8,12},{12,8},{16,20},{20,16},{24,28},{28,24},{1,5},{5... | collective-permute-start | bytes 2654216 | tf_op jit(solution)/shard_map/ppermute | solution.py:686
  77.0 9.3 %collective-permute-start.11 = (bf16[1024,128]{1,0:T(8,128)(2,1)}, bf16[1024,128]{1,0:T(8,128)(2,1)S(1)}, u32[]{:S(2)}, u32[]{:S(2)}) collective-permute-start(bf16[1024,128]{1,0:T(8,128)(2,1)} %get-tuple-element.89), channel_id=1, source_target_pairs={{0,8},{4,12},{8,0},{12,4},{16,24},{20,28},{24,16},{28,20},{1,9},{5... | collective-permute-start | bytes 786440 | tf_op jit(solution)/shard_map/ppermute | solution.py:686
  83.0 15.9 %collective-permute-start.13 = (bf16[288,960]{1,0:T(8,128)(2,1)}, bf16[288,960]{1,0:T(8,128)(2,1)S(1)}, u32[]{:S(2)}, u32[]{:S(2)}) collective-permute-start(bf16[288,960]{1,0:T(8,128)(2,1)} %get-tuple-element.98), channel_id=1, source_target_pairs={{0,8},{4,12},{8,0},{12,4},{16,24},{20,28},{24,16},{28,20},{1,9},{5... | collective-permute-start | bytes 1658888 | tf_op jit(solution)/shard_map/ppermute | solution.py:686
  86.3 18.5 %collective-permute-start.7 = (bf16[1040,640]{1,0:T(8,128)(2,1)}, bf16[1040,640]{1,0:T(8,128)(2,1)}, u32[]{:S(2)}, u32[]{:S(2)}) collective-permute-start(bf16[1040,640]{1,0:T(8,128)(2,1)} %copy-done.5), channel_id=1, source_target_pairs={{0,1},{1,0},{2,3},{3,2},{4,5},{5,4},{6,7},{7,6},{8,9},{9,8},{10,11... | collective-permute-start | bytes 3993608 | tf_op jit(solution)/shard_map/ppermute | solution.py:689
  92.7 14.6 %collective-permute-start.6 = (bf16[1040,640]{1,0:T(8,128)(2,1)S(1)}, bf16[1040,640]{1,0:T(8,128)(2,1)S(1)}, u32[]{:S(2)}, u32[]{:S(2)}) collective-permute-start(bf16[1040,640]{1,0:T(8,128)(2,1)S(1)} %fusion.6.refs_4_), channel_id=1, source_target_pairs={{0,1},{1,0},{2,3},{3,2},{4,5},{5,4},{6,7},{7,6},{8,9},{9,8},{10,11... | collective-permute-start | bytes 3993608 | tf_op jit(solution)/shard_map/ppermute | solution.py:689
  98.9 9.5 %collective-permute-start.12 = (bf16[1040,640]{1,0:T(8,128)(2,1)}, bf16[1040,640]{1,0:T(8,128)(2,1)}, u32[]{:S(2)}, u32[]{:S(2)}) collective-permute-start(bf16[1040,640]{1,0:T(8,128)(2,1)} %collective-permute-done.9.refs_9_), channel_id=1, source_target_pairs={{0,1},{1,0},{2,3},{3,2},{4,5},{5,4},{6,7},{7,6},{8,9},{9,8},{10,11... | collective-permute-start | bytes 3993608 | tf_op jit(solution)/shard_map/ppermute | solution.py:689
  101.1 28.7 %collective-permute-start.14 = (bf16[2,288,960]{2,1,0:T(8,128)(2,1)}, bf16[2,288,960]{2,1,0:T(8,128)(2,1)}, u32[]{:S(2)}, u32[]{:S(2)}) collective-permute-start(bf16[2,288,960]{2,1,0:T(8,128)(2,1)} %pad_maximum_fusion.refs_0_), channel_id=1, source_target_pairs={{0,4},{4,0},{8,12},{12,8},{16,20},{20,16},{24,28},{28,24},{1,5},{5... | collective-permute-start | bytes 3317768 | tf_op jit(solution)/shard_map/ppermute | solution.py:686
  102.3 56.6 %collective-permute-start.18 = (bf16[2,288,960]{2,1,0:T(8,128)(2,1)}, bf16[2,288,960]{2,1,0:T(8,128)(2,1)}, u32[]{:S(2)}, u32[]{:S(2)}) collective-permute-start(bf16[2,288,960]{2,1,0:T(8,128)(2,1)} %pad_maximum_fusion.refs_0_), channel_id=1, source_target_pairs={{0,16},{4,20},{8,24},{12,28},{16,0},{20,4},{24,8},{28,12},{1,17},{... | collective-permute-start | bytes 3317768 | tf_op jit(solution)/shard_map/ppermute | solution.py:686
  104.9 54.0 %collective-permute-start.19 = (bf16[1024,256]{1,0:T(8,128)(2,1)}, bf16[1024,256]{1,0:T(8,128)(2,1)S(1)}, u32[]{:S(2)}, u32[]{:S(2)}) collective-permute-start(bf16[1024,256]{1,0:T(8,128)(2,1)} %get-tuple-element.109), channel_id=1, source_target_pairs={{0,8},{4,12},{8,0},{12,4},{16,24},{20,28},{24,16},{28,20},{1,9},{5... | collective-permute-start | bytes 1572872 | tf_op jit(solution)/shard_map/ppermute | solution.py:686
  129.8 4.4 %collective-permute-start.15 = (f32[2,3,128]{2,1,0:T(4,128)}, f32[2,3,128]{2,1,0:T(4,128)S(1)}, u32[]{:S(2)}, u32[]{:S(2)}) collective-permute-start(f32[2,3,128]{2,1,0:T(4,128)} %get-tuple-element.99), channel_id=1, source_target_pairs={{0,4},{4,0},{8,12},{12,8},{16,20},{20,16},{24,28},{28,24},{1,5},{5... | collective-permute-start | bytes 9224 | tf_op jit(solution)/shard_map/ppermute | solution.py:686
  130.5 25.9 %collective-permute-start.16 = (f32[2,3,128]{2,1,0:T(4,128)}, f32[2,3,128]{2,1,0:T(4,128)S(1)}, u32[]{:S(2)}, u32[]{:S(2)}) collective-permute-start(f32[2,3,128]{2,1,0:T(4,128)} %get-tuple-element.99), channel_id=1, source_target_pairs={{0,16},{4,20},{8,24},{12,28},{16,0},{20,4},{24,8},{28,12},{1,17},{... | collective-permute-start | bytes 9224 | tf_op jit(solution)/shard_map/ppermute | solution.py:686
  132.9 24.7 %collective-permute-start.17 = (f32[2,3,128]{2,1,0:T(4,128)}, f32[2,3,128]{2,1,0:T(4,128)S(1)}, u32[]{:S(2)}, u32[]{:S(2)}) collective-permute-start(f32[2,3,128]{2,1,0:T(4,128)} %get-tuple-element.99), channel_id=1, source_target_pairs={{0,20},{4,16},{8,28},{12,24},{16,4},{20,0},{24,12},{28,8},{1,21},{... | collective-permute-start | bytes 9224 | tf_op jit(solution)/shard_map/ppermute | solution.py:686
  158.9 28.2 %collective-permute-start.20 = (bf16[2,288,960]{2,1,0:T(8,128)(2,1)}, bf16[2,288,960]{2,1,0:T(8,128)(2,1)S(1)}, u32[]{:S(2)}, u32[]{:S(2)}) collective-permute-start(bf16[2,288,960]{2,1,0:T(8,128)(2,1)} %collective-permute-done.18.refs_2_), channel_id=1, source_target_pairs={{0,4},{4,0},{8,12},{12,8},{16,20},{20,16},{24,28},{28,24},{1,5},{5... | collective-permute-start | bytes 3317768 | tf_op jit(solution)/shard_map/ppermute | solution.py:686
  183.5 35.8 %collective-permute-start.24 = (bf16[2,288,768]{2,1,0:T(8,128)(2,1)}, bf16[2,288,768]{2,1,0:T(8,128)(2,1)}, u32[]{:S(2)}, u32[]{:S(2)}) collective-permute-start(bf16[2,288,768]{2,1,0:T(8,128)(2,1)} %get-tuple-element.105), channel_id=1, source_target_pairs={{0,4},{4,0},{8,12},{12,8},{16,20},{20,16},{24,28},{28,24},{1,5},{5... | collective-permute-start | bytes 2654216 | tf_op jit(solution)/shard_map/ppermute | solution.py:686
  214.8 7.0 %collective-permute-start.21 = (f32[2,3,160]{2,1,0:T(4,128)}, f32[2,3,160]{2,1,0:T(4,128)S(1)}, u32[]{:S(2)}, u32[]{:S(2)}) collective-permute-start(f32[2,3,160]{2,1,0:T(4,128)} %get-tuple-element.114), channel_id=1, source_target_pairs={{0,4},{4,0},{8,12},{12,8},{16,20},{20,16},{24,28},{28,24},{1,5},{5... | collective-permute-start | bytes 11528 | tf_op jit(solution)/shard_map/ppermute | solution.py:686
  215.5 6.3 %collective-permute-start.22 = (f32[2,3,160]{2,1,0:T(4,128)}, f32[2,3,160]{2,1,0:T(4,128)S(1)}, u32[]{:S(2)}, u32[]{:S(2)}) collective-permute-start(f32[2,3,160]{2,1,0:T(4,128)} %get-tuple-element.114), channel_id=1, source_target_pairs={{0,16},{4,20},{8,24},{12,28},{16,0},{20,4},{24,8},{28,12},{1,17},{... | collective-permute-start | bytes 11528 | tf_op jit(solution)/shard_map/ppermute | solution.py:686
  215.7 6.1 %collective-permute-start.23 = (f32[2,3,160]{2,1,0:T(4,128)}, f32[2,3,160]{2,1,0:T(4,128)S(1)}, u32[]{:S(2)}, u32[]{:S(2)}) collective-permute-start(f32[2,3,160]{2,1,0:T(4,128)} %get-tuple-element.114), channel_id=1, source_target_pairs={{0,20},{4,16},{8,28},{12,24},{16,4},{20,0},{24,12},{28,8},{1,21},{... | collective-permute-start | bytes 11528 | tf_op jit(solution)/shard_map/ppermute | solution.py:686
  222.4 44.3 %collective-permute-start.29 = (bf16[2,288,768]{2,1,0:T(8,128)(2,1)}, bf16[2,288,768]{2,1,0:T(8,128)(2,1)S(1)}, u32[]{:S(2)}, u32[]{:S(2)}) collective-permute-start(bf16[2,288,768]{2,1,0:T(8,128)(2,1)} %get-tuple-element.131), channel_id=1, source_target_pairs={{0,4},{4,0},{8,12},{12,8},{16,20},{20,16},{24,28},{28,24},{1,5},{5... | collective-permute-start | bytes 2654216 | tf_op jit(solution)/shard_map/ppermute | solution.py:686
  223.2 45.3 %collective-permute-start.30 = (bf16[2,288,768]{2,1,0:T(8,128)(2,1)}, bf16[2,288,768]{2,1,0:T(8,128)(2,1)}, u32[]{:S(2)}, u32[]{:S(2)}) collective-permute-start(bf16[2,288,768]{2,1,0:T(8,128)(2,1)} %convert_add_fusion), channel_id=1, source_target_pairs={{0,16},{4,20},{8,24},{12,28},{16,0},{20,4},{24,8},{28,12},{1,17},{... | collective-permute-start | bytes 2654216 | tf_op jit(solution)/shard_map/ppermute | solution.py:686
  243.3 26.6 %collective-permute-start.26 = (f32[3,864]{1,0:T(4,128)S(1)}, f32[3,864]{1,0:T(4,128)S(1)}, u32[]{:S(2)}, u32[]{:S(2)}) collective-permute-start(f32[3,864]{1,0:T(4,128)S(1)} %get-tuple-element.167), channel_id=1, source_target_pairs={{0,4},{4,0},{8,12},{12,8},{16,20},{20,16},{24,28},{28,24},{1,5},{5... | collective-permute-start | bytes 31112 | tf_op jit(solution)/shard_map/ppermute | solution.py:686
  243.9 26.0 %collective-permute-start.27 = (f32[3,864]{1,0:T(4,128)S(1)}, f32[3,864]{1,0:T(4,128)S(1)}, u32[]{:S(2)}, u32[]{:S(2)}) collective-permute-start(f32[3,864]{1,0:T(4,128)S(1)} %get-tuple-element.167), channel_id=1, source_target_pairs={{0,16},{4,20},{8,24},{12,28},{16,0},{20,4},{24,8},{28,12},{1,17},{... | collective-permute-start | bytes 31112 | tf_op jit(solution)/shard_map/ppermute | solution.py:686
  244.6 25.3 %collective-permute-start.28 = (f32[3,864]{1,0:T(4,128)S(1)}, f32[3,864]{1,0:T(4,128)S(1)}, u32[]{:S(2)}, u32[]{:S(2)}) collective-permute-start(f32[3,864]{1,0:T(4,128)S(1)} %get-tuple-element.167), channel_id=1, source_target_pairs={{0,20},{4,16},{8,28},{12,24},{16,4},{20,0},{24,12},{28,8},{1,21},{... | collective-permute-start | bytes 31112 | tf_op jit(solution)/shard_map/ppermute | solution.py:686
  266.7 43.0 %collective-permute-start.25 = (bf16[1024,384]{1,0:T(8,128)(2,1)}, bf16[1024,384]{1,0:T(8,128)(2,1)}, u32[]{:S(2)}, u32[]{:S(2)}) collective-permute-start(bf16[1024,384]{1,0:T(8,128)(2,1)} %get-tuple-element.125), channel_id=1, source_target_pairs={{0,8},{4,12},{8,0},{12,4},{16,24},{20,28},{24,16},{28,20},{1,9},{5... | collective-permute-start | bytes 2359304 | tf_op jit(solution)/shard_map/ppermute | solution.py:686
  269.9 39.8 %collective-permute-start.31 = (bf16[2,288,960]{2,1,0:T(8,128)(2,1)}, bf16[2,288,960]{2,1,0:T(8,128)(2,1)S(1)}, u32[]{:S(2)}, u32[]{:S(2)}) collective-permute-start(bf16[2,288,960]{2,1,0:T(8,128)(2,1)} %get-tuple-element.133), channel_id=1, source_target_pairs={{0,4},{4,0},{8,12},{12,8},{16,20},{20,16},{24,28},{28,24},{1,5},{5... | collective-permute-start | bytes 3317768 | tf_op jit(solution)/shard_map/ppermute | solution.py:686
  272.3 37.4 %collective-permute-start.33 = (bf16[288,768]{1,0:T(8,128)(2,1)}, bf16[288,768]{1,0:T(8,128)(2,1)S(1)}, u32[]{:S(2)}, u32[]{:S(2)}) collective-permute-start(bf16[288,768]{1,0:T(8,128)(2,1)} %get-tuple-element.160), channel_id=1, source_target_pairs={{0,8},{4,12},{8,0},{12,4},{16,24},{20,28},{24,16},{28,20},{1,9},{5... | collective-permute-start | bytes 1327112 | tf_op jit(solution)/shard_map/ppermute | solution.py:686
  272.4 37.4 %collective-permute-start.32 = (f32[3,288]{1,0:T(4,128)S(1)}, f32[3,288]{1,0:T(4,128)S(1)}, u32[]{:S(2)}, u32[]{:S(2)}) collective-permute-start(f32[3,288]{1,0:T(4,128)S(1)} %pad_maximum_fusion.6), channel_id=1, source_target_pairs={{0,8},{4,12},{8,0},{12,4},{16,24},{20,28},{24,16},{28,20},{1,9},{5... | collective-permute-start | bytes 10376 | tf_op jit(solution)/shard_map/ppermute | solution.py:686
  309.8 5.3 %collective-permute-start.35 = (bf16[2,1024,640]{2,1,0:T(8,128)(2,1)}, bf16[2,1024,640]{2,1,0:T(8,128)(2,1)}, u32[]{:S(2)}, u32[]{:S(2)}) collective-permute-start(bf16[2,1024,640]{2,1,0:T(8,128)(2,1)} %get-tuple-element.144), channel_id=1, source_target_pairs={{0,1},{1,0},{2,3},{3,2},{4,5},{5,4},{6,7},{7,6},{8,9},{9,8},{10,11... | collective-permute-start | bytes 7864328 | tf_op jit(solution)/shard_map/ppermute | solution.py:689
  309.9 43.7 %collective-permute-start.34 = (bf16[2,1024,640]{2,1,0:T(8,128)(2,1)}, bf16[2,1024,640]{2,1,0:T(8,128)(2,1)}, u32[]{:S(2)}, u32[]{:S(2)}) collective-permute-start(bf16[2,1024,640]{2,1,0:T(8,128)(2,1)} %get-tuple-element.142), channel_id=1, source_target_pairs={{0,1},{1,0},{2,3},{3,2},{4,5},{5,4},{6,7},{7,6},{8,9},{9,8},{10,11... | collective-permute-start | bytes 7864328 | tf_op jit(solution)/shard_map/ppermute | solution.py:689
  317.8 32.6 %collective-permute-start.36 = (bf16[1024,640]{1,0:T(8,128)(2,1)}, bf16[1024,640]{1,0:T(8,128)(2,1)}, u32[]{:S(2)}, u32[]{:S(2)}) collective-permute-start(bf16[1024,640]{1,0:T(8,128)(2,1)} %join.7), channel_id=1, source_target_pairs={{0,2},{1,3},{2,0},{3,1},{4,6},{5,7},{6,4},{7,5},{8,10},{9,11},{10,... | collective-permute-start | bytes 3932168 | tf_op jit(solution)/shard_map/ppermute | solution.py:689
  318.0 28.0 %collective-permute-start.37 = (bf16[2,288,960]{2,1,0:T(8,128)(2,1)}, bf16[2,288,960]{2,1,0:T(8,128)(2,1)S(1)}, u32[]{:S(2)}, u32[]{:S(2)}) collective-permute-start(bf16[2,288,960]{2,1,0:T(8,128)(2,1)} %get-tuple-element.135), channel_id=1, source_target_pairs={{0,4},{4,0},{8,12},{12,8},{16,20},{20,16},{24,28},{28,24},{1,5},{5... | collective-permute-start | bytes 3317768 | tf_op jit(solution)/shard_map/ppermute | solution.py:686
  318.9 28.4 %collective-permute-start.38 = (bf16[288,960]{1,0:T(8,128)(2,1)}, bf16[288,960]{1,0:T(8,128)(2,1)S(1)}, u32[]{:S(2)}, u32[]{:S(2)}) collective-permute-start(bf16[288,960]{1,0:T(8,128)(2,1)} %join.6), channel_id=1, source_target_pairs={{0,16},{4,20},{8,24},{12,28},{16,0},{20,4},{24,8},{28,12},{1,17},{... | collective-permute-start | bytes 1658888 | tf_op jit(solution)/shard_map/ppermute | solution.py:686
  356.2 30.9 %collective-permute-start.39 = (bf16[1024,640]{1,0:T(8,128)(2,1)}, bf16[1024,640]{1,0:T(8,128)(2,1)S(1)}, u32[]{:S(2)}, u32[]{:S(2)}) collective-permute-start(bf16[1024,640]{1,0:T(8,128)(2,1)} %join.10), channel_id=1, source_target_pairs={{0,2},{1,3},{2,0},{3,1},{4,6},{5,7},{6,4},{7,5},{8,10},{9,11},{10,... | collective-permute-start | bytes 3932168 | tf_op jit(solution)/shard_map/ppermute | solution.py:689
  358.0 44.6 %collective-permute-start.40 = (bf16[1024,640]{1,0:T(8,128)(2,1)}, bf16[1024,640]{1,0:T(8,128)(2,1)}, u32[]{:S(2)}, u32[]{:S(2)}) collective-permute-start(bf16[1024,640]{1,0:T(8,128)(2,1)} %join.9), channel_id=1, source_target_pairs={{0,8},{4,12},{8,0},{12,4},{16,24},{20,28},{24,16},{28,20},{1,9},{5... | collective-permute-start | bytes 3932168 | tf_op jit(solution)/shard_map/ppermute | solution.py:686
  366.9 47.0 %collective-permute-start.42 = (bf16[288,960]{1,0:T(8,128)(2,1)}, bf16[288,960]{1,0:T(8,128)(2,1)S(1)}, u32[]{:S(2)}, u32[]{:S(2)}) collective-permute-start(bf16[288,960]{1,0:T(8,128)(2,1)} %join.8), channel_id=1, source_target_pairs={{0,8},{4,12},{8,0},{12,4},{16,24},{20,28},{24,16},{28,20},{1,9},{5... | collective-permute-start | bytes 1658888 | tf_op jit(solution)/shard_map/ppermute | solution.py:686
  368.9 42.9 %collective-permute-start.41 = (bf16[288,960]{1,0:T(8,128)(2,1)}, bf16[288,960]{1,0:T(8,128)(2,1)}, u32[]{:S(2)}, u32[]{:S(2)}) collective-permute-start(bf16[288,960]{1,0:T(8,128)(2,1)} %join.11), channel_id=1, source_target_pairs={{0,16},{4,20},{8,24},{12,28},{16,0},{20,4},{24,8},{28,12},{1,17},{... | collective-permute-start | bytes 1658888 | tf_op jit(solution)/shard_map/ppermute | solution.py:686
  (17 other events, 140.5 us)

commit v6 on v5

--- a/solution.py
+++ b/solution.py
@@ -12,7 +12,7 @@
 SEGS = 8
 LANES = 128
 TM = 64
-ROWS = 256
+ROWS = 512
 EDGE = 16
 GAP = 8
 VMEM = 62 << 20

time: 420 us -> 420 us (level)
  no operation moved by 1% of the time
where the time goes in v6:
time: 420 us; the launch traced here: 419 us
  Pallas kernels  175 us (42%)
  waiting for transfers between devices  157 us (37%)
  starting transfers between devices  57.7 us (14%)
  other arithmetic  15 us (4%)
  local copies, waits for them, and re-layouts  13.3 us (3%)
    ppermute x32, waiting for transfers between devices, seq_to(): return lax.ppermute(v, 'seq', route)  132 us
    ppermute x32, starting transfers between devices, seq_to(): return lax.ppermute(v, 'seq', route)  49.7 us
    pallas_call x2, Pallas kernels, gates_and_totals(): pl.pallas_call(functools.partial(gates_kernel, plan), in_specs=[SMEM_SPEC...  45.1 us
    pallas_call x1, Pallas kernels, input_grads(): pl.pallas_call(xgrad_kernel, grid_spec=pltpu.PrefetchScalarGridSpec(num_s...  34.4 us
    pallas_call x2, Pallas kernels, weight_grads(): pl.pallas_call(functools.partial(wgrad_kernel, dw), grid_spec=pltpu.Prefe...  34.2 us
    pallas_call x2, Pallas kernels, finish(): pl.pallas_call(functools.partial(finish_kernel, n, up_at), in_specs=[SMEM...  25.1 us
    ppermute x10, waiting for transfers between devices, gate_to(): return lax.ppermute(v, 'gate', [(i, i ^ d_a * 2 + d_b) for i in range(m)])  24.2 us
    pallas_call x6, Pallas kernels, join(): pl.pallas_call(join_kernel, grid=(steps,), in_specs=[spec(v, at) for v, a...  14.8 us
  transfers between devices with their start and end apart: 43, of which 19 were waited for; matrix products, arithmetic and copies ran while one was open for 5% of the time, Pallas kernels for 39%

profile of v6, /device:TPU:0, one launch (start us, length us, event | category | flops | bytes accessed | tf_op | source)
XLA Modules:
  0.0 418.8 jit_solution(10177852291059932976)
XLA Ops:
  1.4 3.3 pack_weights.2
  4.7 3.0 collective-permute-start
  8.5 3.4 collective-permute-start.4
  15.2 2.9 collective-permute-done
  18.1 4.8 %collective-permute-start.8 = (bf16[1040,640]{1,0:T(8,128)(2,1)S(1)}, bf16[1040,640]{1,0:T(8,128)(2,1)}, u32[]{:S(2)}, u32[]{:S(2)}) collective-permute-start(bf16[1040,640]{1,0:T(8,128)(2,1)S(1)} %fusion.6.refs_4_), channel_id=1, source_target_pairs={{0,8},{4,12},{8,0},{12,4},{16,24},{20,28},{24,16},{28,20},{1,9},{5... | collective-permute-start | bytes 3993608 | tf_op jit(solution)/shard_map/ppermute | solution.py:686
  23.1 2.7 collective-permute-start.2
  25.7 17.0 %collective-permute-done.1.refs_1_ = bf16[2,288,768]{2,1,0:T(8,128)(2,1)S(1)} collective-permute-done((bf16[2,288,768]{2,1,0:T(8,128)(2,1)S(1)}, bf16[2,288,768]{2,1,0:T(8,128)(2,1)S(1)}, u32[]{:S(2)}, u32[]{:S(2)}) %collective-permute-start.1) | collective-permute-done | bytes 884768 | tf_op jit(solution)/shard_map/ppermute | solution.py:686
  43.5 26.2 %collective-permute-done.8.refs_8_ = bf16[1040,640]{1,0:T(8,128)(2,1)} collective-permute-done((bf16[1040,640]{1,0:T(8,128)(2,1)S(1)}, bf16[1040,640]{1,0:T(8,128)(2,1)}, u32[]{:S(2)}, u32[]{:S(2)}) %collective-permute-start.8) | collective-permute-done | bytes 1331232 | tf_op jit(solution)/shard_map/ppermute | solution.py:686
  72.0 5.1 %pack_up.1 = (bf16[1024,128]{1,0:T(8,128)(2,1)}, bf16[1024,128]{1,0:T(8,128)(2,1)}, bf16[1024,160]{1,0:T(8,128)(2,1)}, bf16[1024,256]{1,0:T(8,128)(2,1)}) custom-call(s32[5]{0:T(128)} %stack.91.place, bf16[1024,576]{1,0:T(8,128)(2,1)} %copy.13.up_ref), custom_call_target="tpu_custom_call" | custom-call | flops 1024 | bytes 1024 | tf_op jit(solution)/shard_map/pack_up/pallas_call | solution.py:114
  79.0 4.0 pack_weights.3
  83.0 3.3 collective-permute-done.11.refs_14_.up1
  86.4 6.3 %collective-permute-done.3.refs_3_ = bf16[2,288,768]{2,1,0:T(8,128)(2,1)} collective-permute-done((bf16[2,288,768]{2,1,0:T(8,128)(2,1)}, bf16[2,288,768]{2,1,0:T(8,128)(2,1)}, u32[]{:S(2)}, u32[]{:S(2)}) %collective-permute-start.3) | collective-permute-done | bytes 884768 | tf_op jit(solution)/shard_map/ppermute | solution.py:686
  92.7 6.2 %collective-permute-done.9.refs_9_ = bf16[1040,640]{1,0:T(8,128)(2,1)} collective-permute-done((bf16[1040,640]{1,0:T(8,128)(2,1)}, bf16[1040,640]{1,0:T(8,128)(2,1)}, u32[]{:S(2)}, u32[]{:S(2)}) %collective-permute-start.9) | collective-permute-done | bytes 1331232 | tf_op jit(solution)/shard_map/ppermute | solution.py:689
  98.9 2.2 pad_maximum_fusion.refs_0_
  102.3 2.6 collective-permute-start.18
  108.4 19.4 %gates_and_totals.2 = (f32[3,2048,128]{2,1,0:T(8,128)}, f32[2,3,8,128]{3,2,1,0:T(8,128)}, f32[2,3,128]{2,1,0:T(4,128)}, bf16[2048,2560]{1,0:T(8,128)(2,1)}, bf16...) custom-call(s32[5]{0:T(128)} %stack.91.place, bf16[2,288,768]{2,1,0:T(8,128)(2,1)} %copy-done.3, ...), custom_call_target="tpu_custom_call" | custom-call | flops 1024 | bytes 1024 | tf_op jit(solution)/shard_map/gates_and_totals/pallas_call | solution.py:293
  127.8 1.9 collective-permute-done.14.refs_1_
  130.1 2.8 collective-permute-start.16
  134.2 22.2 %collective-permute-done.16 = f32[2,3,128]{2,1,0:T(4,128)S(1)} collective-permute-done((f32[2,3,128]{2,1,0:T(4,128)}, f32[2,3,128]{2,1,0:T(4,128)S(1)}, u32[]{:S(2)}, u32[]{:S(2)}) %collective-permute-start.16) | collective-permute-done | bytes 3104 | tf_op jit(solution)/shard_map/ppermute | solution.py:686
  159.5 8.7 %finish.2 = (bf16[1024,128]{1,0:T(8,128)(2,1)}, bf16[1024,128]{1,0:T(8,128)(2,1)}, bf16[2048,768]{1,0:T(8,128)(2,1)}, f32[2,384]{1,0:T(2,128)}, bf16[32,768]{1,0:T(8,128)(2,1)}, /*index=5*/f32[1,384]{1,0:T(1,128)}) custom-call(s32[5]{0:T(128)} %stack.91.place, f32[3,2048,128]{2,1,0:T(8,128)} %get-tuple-element.92.g_ref, ...), custom_call_target="tpu_custom_call" | custom-call | flops 1024 | bytes 1024 | tf_op jit(solution)/shard_map/finish/pallas_call | solution.py:444
  168.2 15.2 %weight_grads.2 = (bf16[2,288,768]{2,1,0:T(8,128)(2,1)}, bf16[2,288,768]{2,1,0:T(8,128)(2,1)}, bf16[2,288,768]{2,1,0:T(8,128)(2,1)}, bf16[2,288,768]{2,1,0:T(8,128)(2,1)}) custom-call(s32[5]{0:T(128)} %stack.91.place, bf16[2048,2560]{1,0:T(8,128)(2,1)} %get-tuple-element.101.x_ref.refs_4_, bf16[32,2560]{1,0:T(8,128)(2,1)} %get-tuple-element.102.halo_ref.refs_5_, ...), custom_call_target="tpu_custom_call" | custom-call | flops 1024 | bytes 1024 | tf_op jit(solution)/shard_map/weight_grads/pallas_call | solution.py:488
  188.1 25.7 %gates_and_totals.3 = (f32[3,2048,160]{2,1,0:T(8,128)}, f32[2,3,8,160]{3,2,1,0:T(8,128)}, f32[2,3,160]{2,1,0:T(4,128)}, bf16[4,640,960]{2,1,0:T(8,128)(2,1)}) custom-call(s32[5]{0:T(128)} %stack.91.place, bf16[2,288,960]{2,1,0:T(8,128)(2,1)} %pad_maximum_fusion.refs_0_, bf16[2,288,960]{2,1,0:T(8,128)(2,1)} %collective-permute-done.14.refs_1_, ...), custom_call_target="tpu_custom_call" | custom-call | flops 1024 | bytes 1024 | tf_op jit(solution)/shard_map/gates_and_totals/pallas_call | solution.py:293
  214.7 3.5 collective-permute-start.23
  218.2 2.6 convert_add_fusion
  222.1 3.0 collective-permute-start.30
  225.1 16.4 %finish.3 = (bf16[1024,160]{1,0:T(8,128)(2,1)}, bf16[1024,384]{1,0:T(8,128)(2,1)}, bf16[2048,960]{1,0:T(8,128)(2,1)}, f32[2,480]{1,0:T(2,128)}, bf16[32,960]{1,0:T(8,128)(2,1)}, /*index=5*/f32[1,480]{1,0:T(1,128)}) custom-call(s32[5]{0:T(128)} %stack.91.place, f32[3,2048,160]{2,1,0:T(8,128)} %get-tuple-element.112.g_ref, ...), custom_call_target="tpu_custom_call" | custom-call | flops 1024 | bytes 1024 | tf_op jit(solution)/shard_map/finish/pallas_call | solution.py:444
  243.6 3.2 collective-permute-start.28
  246.7 18.9 %weight_grads.3 = (bf16[2,288,960]{2,1,0:T(8,128)(2,1)}, bf16[2,288,960]{2,1,0:T(8,128)(2,1)}, bf16[2,288,960]{2,1,0:T(8,128)(2,1)}, bf16[2,288,960]{2,1,0:T(8,128)(2,1)}) custom-call(s32[5]{0:T(128)} %stack.91.place, bf16[2048,2560]{1,0:T(8,128)(2,1)} %get-tuple-element.101.x_ref.refs_4_, bf16[32,2560]{1,0:T(8,128)(2,1)} %get-tuple-element.102.halo_ref.refs_5_, ...), custom_call_target="tpu_custom_call" | custom-call | flops 1024 | bytes 1024 | tf_op jit(solution)/shard_map/weight_grads/pallas_call | solution.py:488
  271.3 2.0 collective-permute-start.32
  274.5 34.4 %input_grads.1 = (bf16[2,1024,640]{2,1,0:T(8,128)(2,1)}, bf16[2,1024,640]{2,1,0:T(8,128)(2,1)}, bf16[2,1024,640]{2,1,0:T(8,128)(2,1)}, bf16[2,1024,640]{2,1,0:T(8,128)(2,1)}) custom-call(s32[5]{0:T(128)} %stack.91.place, bf16[2048,768]{1,0:T(8,128)(2,1)} %get-tuple-element.103.gg_ref.refs_0_, bf16[2048,960]{1,0:T(8,128)(2,1)} %get-tuple-element.126.gg_ref.refs_1_, ...), custom_call_target="tpu_custom_call" | custom-call | flops 1024 | bytes 1024 | tf_op jit(solution)/shard_map/input_grads/pallas_call | solution.py:555
  309.9 2.0 join.6
  311.9 2.3 collective-permute-done.35.refs_1_
  314.3 2.7 join.7
  318.0 2.9 collective-permute-start.38
  321.0 24.2 %collective-permute-done.37.refs_1_.refs_3_ = bf16[2,288,960]{2,1,0:T(8,128)(2,1)S(1)} collective-permute-done((bf16[2,288,960]{2,1,0:T(8,128)(2,1)}, bf16[2,288,960]{2,1,0:T(8,128)(2,1)S(1)}, u32[]{:S(2)}, u32[]{:S(2)}) %collective-permute-start.37) | collective-permute-done | bytes 1105952 | tf_op jit(solution)/shard_map/ppermute | solution.py:686
  347.3 2.3 join.8
  349.5 3.2 join.9
  352.7 2.7 join.10
  357.8 3.8 unpack_hidden.1
  361.6 2.4 copy.14
  364.0 2.0 join.11
  366.0 2.0 collective-permute-start.42
  369.5 2.0 add_bitcast_fusion
  371.4 14.9 %collective-permute-done.39 = bf16[1024,640]{1,0:T(8,128)(2,1)S(1)} collective-permute-done((bf16[1024,640]{1,0:T(8,128)(2,1)}, bf16[1024,640]{1,0:T(8,128)(2,1)S(1)}, u32[]{:S(2)}, u32[]{:S(2)}) %collective-permute-start.39) | collective-permute-done | bytes 1310752 | tf_op jit(solution)/shard_map/ppermute | solution.py:689
  386.3 15.5 %collective-permute-done.40 = bf16[1024,640]{1,0:T(8,128)(2,1)} collective-permute-done((bf16[1024,640]{1,0:T(8,128)(2,1)}, bf16[1024,640]{1,0:T(8,128)(2,1)}, u32[]{:S(2)}, u32[]{:S(2)}) %collective-permute-start.40) | collective-permute-done | bytes 1310752 | tf_op jit(solution)/shard_map/ppermute | solution.py:686
  405.0 5.9 %collective-permute-done.41.refs_4_ = bf16[288,960]{1,0:T(8,128)(2,1)} collective-permute-done((bf16[288,960]{1,0:T(8,128)(2,1)}, bf16[288,960]{1,0:T(8,128)(2,1)}, u32[]{:S(2)}, u32[]{:S(2)}) %collective-permute-start.41) | collective-permute-done | bytes 552992 | tf_op jit(solution)/shard_map/ppermute | solution.py:686
  410.9 2.1 collective-permute-done.42.refs_5_
  413.8 4.9 %unpack_weights.1 = (f32[3,288,576]{2,1,0:T(8,128)}, f32[3,288,576]{2,1,0:T(8,128)}) custom-call(s32[5]{0:T(128)} %stack.91.place, bf16[288,768]{1,0:T(8,128)(2,1)} %get-tuple-element.161.refs_0_, bf16[288,768]{1,0:T(8,128)(2,1)} %copy-done.15, bf16[2,288,960]{2,1,0:T(8,128)(2,1)} %get-tuple-element.147.refs_0_.refs_2_, bf16[2,288,960]{2,1,0:T(8,128)(2,1)} %copy-done.1, ...), custom_call_target="tpu_custom_call" | custom-call | flops 1024 | bytes 1024 | tf_op jit(solution)/shard_map/unpack_weights/pallas_call | solution.py:631
  (134 shorter events, 47.2 us)
Async XLA Ops:
  4.7 13.4 %collective-permute-start = (bf16[288,768]{1,0:T(8,128)(2,1)}, bf16[288,768]{1,0:T(8,128)(2,1)S(1)}, u32[]{:S(2)}, u32[]{:S(2)}) collective-permute-start(bf16[288,768]{1,0:T(8,128)(2,1)} %get-tuple-element.81), channel_id=1, source_target_pairs={{0,8},{4,12},{8,0},{12,4},{16,24},{20,28},{24,16},{28,20},{1,9},{5... | collective-permute-start | bytes 1327112 | tf_op jit(solution)/shard_map/ppermute | solution.py:686
  8.5 4.7 %collective-permute-start.4 = (bf16[1,576]{1,0:T(2,128)(2,1)S(1)}, bf16[1,576]{1,0:T(2,128)(2,1)S(1)}, u32[]{:S(2)}, u32[]{:S(2)}) collective-permute-start(bf16[1,576]{1,0:T(2,128)(2,1)S(1)} %slice.61), channel_id=1, source_target_pairs={{0,4},{4,8},{8,12},{12,16},{16,20},{20,24},{24,28},{1,5},{5,9},{9,... | collective-permute-start | bytes 3464 | tf_op jit(solution)/shard_map/ppermute | solution.py:694
  13.6 79.1 %copy-start = (bf16[1040,640]{1,0:T(8,128)(2,1)}, bf16[1040,640]{1,0:T(8,128)(2,1)S(1)}, u32[]{:S(2)}) copy-start(bf16[1040,640]{1,0:T(8,128)(2,1)S(1)} %fusion.6.refs_4_) | copy-start | bytes 3993604
  13.6 56.9 %copy-start.9 = (bf16[1024,576]{0,1:T(8,128)(2,1)S(1)}, bf16[1024,576]{0,1:T(8,128)(2,1)}, u32[]{:S(2)}) copy-start(bf16[1024,576]{0,1:T(8,128)(2,1)} %param.11) | copy-start | bytes 3538948
  13.6 29.9 %collective-permute-start.5 = (bf16[1040,640]{1,0:T(8,128)(2,1)S(1)}, bf16[1040,640]{1,0:T(8,128)(2,1)S(1)}, u32[]{:S(2)}, u32[]{:S(2)}) collective-permute-start(bf16[1040,640]{1,0:T(8,128)(2,1)S(1)} %fusion.6.refs_4_), channel_id=1, source_target_pairs={{0,2},{1,3},{2,0},{3,1},{4,6},{5,7},{6,4},{7,5},{8,10},{9,11},{10,... | collective-permute-start | bytes 3993608 | tf_op jit(solution)/shard_map/ppermute | solution.py:689
  18.1 51.6 %collective-permute-start.8 = (bf16[1040,640]{1,0:T(8,128)(2,1)S(1)}, bf16[1040,640]{1,0:T(8,128)(2,1)}, u32[]{:S(2)}, u32[]{:S(2)}) collective-permute-start(bf16[1040,640]{1,0:T(8,128)(2,1)S(1)} %fusion.6.refs_4_), channel_id=1, source_target_pairs={{0,8},{4,12},{8,0},{12,4},{16,24},{20,28},{24,16},{28,20},{1,9},{5... | collective-permute-start | bytes 3993608 | tf_op jit(solution)/shard_map/ppermute | solution.py:686
  23.0 46.7 %copy-start.3 = (bf16[2,288,768]{2,1,0:T(8,128)(2,1)}, bf16[2,288,768]{2,1,0:T(8,128)(2,1)S(1)}, u32[]{:S(2)}) copy-start(bf16[2,288,768]{2,1,0:T(8,128)(2,1)S(1)} %pad_maximum_fusion.1.refs_0_) | copy-start | bytes 2654212
  23.0 19.7 %collective-permute-start.1 = (bf16[2,288,768]{2,1,0:T(8,128)(2,1)S(1)}, bf16[2,288,768]{2,1,0:T(8,128)(2,1)S(1)}, u32[]{:S(2)}, u32[]{:S(2)}) collective-permute-start(bf16[2,288,768]{2,1,0:T(8,128)(2,1)S(1)} %pad_maximum_fusion.1.refs_0_), channel_id=1, source_target_pairs={{0,4},{4,0},{8,12},{12,8},{16,20},{20,16},{24,28},{28,24},{1,5},{5... | collective-permute-start | bytes 2654216 | tf_op jit(solution)/shard_map/ppermute | solution.py:686
  23.1 47.2 %collective-permute-start.2 = (bf16[2,288,768]{2,1,0:T(8,128)(2,1)S(1)}, bf16[2,288,768]{2,1,0:T(8,128)(2,1)}, u32[]{:S(2)}, u32[]{:S(2)}) collective-permute-start(bf16[2,288,768]{2,1,0:T(8,128)(2,1)S(1)} %pad_maximum_fusion.1.refs_0_), channel_id=1, source_target_pairs={{0,16},{4,20},{8,24},{12,28},{16,0},{20,4},{24,8},{28,12},{1,17},{... | collective-permute-start | bytes 2654216 | tf_op jit(solution)/shard_map/ppermute | solution.py:686
  42.7 27.5 %copy-start.12 = (bf16[2,288,768]{2,1,0:T(8,128)(2,1)}, bf16[2,288,768]{2,1,0:T(8,128)(2,1)S(1)}, u32[]{:S(2)}) copy-start(bf16[2,288,768]{2,1,0:T(8,128)(2,1)S(1)} %collective-permute-done.1.refs_1_) | copy-start | bytes 2654212
  43.5 26.7 %copy-start.5 = (bf16[1040,640]{1,0:T(8,128)(2,1)}, bf16[1040,640]{1,0:T(8,128)(2,1)S(1)}, u32[]{:S(2)}) copy-start(bf16[1040,640]{1,0:T(8,128)(2,1)S(1)} %collective-permute-done.5.refs_5_) | copy-start | bytes 3993604
  69.7 29.2 %collective-permute-start.9 = (bf16[1040,640]{1,0:T(8,128)(2,1)}, bf16[1040,640]{1,0:T(8,128)(2,1)}, u32[]{:S(2)}, u32[]{:S(2)}) collective-permute-start(bf16[1040,640]{1,0:T(8,128)(2,1)} %collective-permute-done.8.refs_8_), channel_id=1, source_target_pairs={{0,2},{1,3},{2,0},{3,1},{4,6},{5,7},{6,4},{7,5},{8,10},{9,11},{10,... | collective-permute-start | bytes 3993608 | tf_op jit(solution)/shard_map/ppermute | solution.py:689
  70.2 32.1 %collective-permute-start.10 = (bf16[1040,640]{1,0:T(8,128)(2,1)}, bf16[1040,640]{1,0:T(8,128)(2,1)}, u32[]{:S(2)}, u32[]{:S(2)}) collective-permute-start(bf16[1040,640]{1,0:T(8,128)(2,1)} %collective-permute-done.8.refs_8_), channel_id=1, source_target_pairs={{0,1},{1,0},{2,3},{3,2},{4,5},{5,4},{6,7},{7,6},{8,9},{9,8},{10,11... | collective-permute-start | bytes 3993608 | tf_op jit(solution)/shard_map/ppermute | solution.py:689
  70.2 22.4 %collective-permute-start.3 = (bf16[2,288,768]{2,1,0:T(8,128)(2,1)}, bf16[2,288,768]{2,1,0:T(8,128)(2,1)}, u32[]{:S(2)}, u32[]{:S(2)}) collective-permute-start(bf16[2,288,768]{2,1,0:T(8,128)(2,1)} %collective-permute-done.2.refs_2_), channel_id=1, source_target_pairs={{0,4},{4,0},{8,12},{12,8},{16,20},{20,16},{24,28},{28,24},{1,5},{5... | collective-permute-start | bytes 2654216 | tf_op jit(solution)/shard_map/ppermute | solution.py:686
  77.0 9.3 %collective-permute-start.11 = (bf16[1024,128]{1,0:T(8,128)(2,1)}, bf16[1024,128]{1,0:T(8,128)(2,1)S(1)}, u32[]{:S(2)}, u32[]{:S(2)}) collective-permute-start(bf16[1024,128]{1,0:T(8,128)(2,1)} %get-tuple-element.89), channel_id=1, source_target_pairs={{0,8},{4,12},{8,0},{12,4},{16,24},{20,28},{24,16},{28,20},{1,9},{5... | collective-permute-start | bytes 786440 | tf_op jit(solution)/shard_map/ppermute | solution.py:686
  82.9 16.0 %collective-permute-start.13 = (bf16[288,960]{1,0:T(8,128)(2,1)}, bf16[288,960]{1,0:T(8,128)(2,1)S(1)}, u32[]{:S(2)}, u32[]{:S(2)}) collective-permute-start(bf16[288,960]{1,0:T(8,128)(2,1)} %get-tuple-element.98), channel_id=1, source_target_pairs={{0,8},{4,12},{8,0},{12,4},{16,24},{20,28},{24,16},{28,20},{1,9},{5... | collective-permute-start | bytes 1658888 | tf_op jit(solution)/shard_map/ppermute | solution.py:686
  86.4 18.5 %collective-permute-start.7 = (bf16[1040,640]{1,0:T(8,128)(2,1)}, bf16[1040,640]{1,0:T(8,128)(2,1)}, u32[]{:S(2)}, u32[]{:S(2)}) collective-permute-start(bf16[1040,640]{1,0:T(8,128)(2,1)} %copy-done.5), channel_id=1, source_target_pairs={{0,1},{1,0},{2,3},{3,2},{4,5},{5,4},{6,7},{7,6},{8,9},{9,8},{10,11... | collective-permute-start | bytes 3993608 | tf_op jit(solution)/shard_map/ppermute | solution.py:689
  92.7 14.6 %collective-permute-start.6 = (bf16[1040,640]{1,0:T(8,128)(2,1)S(1)}, bf16[1040,640]{1,0:T(8,128)(2,1)S(1)}, u32[]{:S(2)}, u32[]{:S(2)}) collective-permute-start(bf16[1040,640]{1,0:T(8,128)(2,1)S(1)} %fusion.6.refs_4_), channel_id=1, source_target_pairs={{0,1},{1,0},{2,3},{3,2},{4,5},{5,4},{6,7},{7,6},{8,9},{9,8},{10,11... | collective-permute-start | bytes 3993608 | tf_op jit(solution)/shard_map/ppermute | solution.py:689
  98.9 9.5 %collective-permute-start.12 = (bf16[1040,640]{1,0:T(8,128)(2,1)}, bf16[1040,640]{1,0:T(8,128)(2,1)}, u32[]{:S(2)}, u32[]{:S(2)}) collective-permute-start(bf16[1040,640]{1,0:T(8,128)(2,1)} %collective-permute-done.9.refs_9_), channel_id=1, source_target_pairs={{0,1},{1,0},{2,3},{3,2},{4,5},{5,4},{6,7},{7,6},{8,9},{9,8},{10,11... | collective-permute-start | bytes 3993608 | tf_op jit(solution)/shard_map/ppermute | solution.py:689
  101.1 28.7 %collective-permute-start.14 = (bf16[2,288,960]{2,1,0:T(8,128)(2,1)}, bf16[2,288,960]{2,1,0:T(8,128)(2,1)}, u32[]{:S(2)}, u32[]{:S(2)}) collective-permute-start(bf16[2,288,960]{2,1,0:T(8,128)(2,1)} %pad_maximum_fusion.refs_0_), channel_id=1, source_target_pairs={{0,4},{4,0},{8,12},{12,8},{16,20},{20,16},{24,28},{28,24},{1,5},{5... | collective-permute-start | bytes 3317768 | tf_op jit(solution)/shard_map/ppermute | solution.py:686
  102.3 56.6 %collective-permute-start.18 = (bf16[2,288,960]{2,1,0:T(8,128)(2,1)}, bf16[2,288,960]{2,1,0:T(8,128)(2,1)}, u32[]{:S(2)}, u32[]{:S(2)}) collective-permute-start(bf16[2,288,960]{2,1,0:T(8,128)(2,1)} %pad_maximum_fusion.refs_0_), channel_id=1, source_target_pairs={{0,16},{4,20},{8,24},{12,28},{16,0},{20,4},{24,8},{28,12},{1,17},{... | collective-permute-start | bytes 3317768 | tf_op jit(solution)/shard_map/ppermute | solution.py:686
  104.9 54.0 %collective-permute-start.19 = (bf16[1024,256]{1,0:T(8,128)(2,1)}, bf16[1024,256]{1,0:T(8,128)(2,1)S(1)}, u32[]{:S(2)}, u32[]{:S(2)}) collective-permute-start(bf16[1024,256]{1,0:T(8,128)(2,1)} %get-tuple-element.109), channel_id=1, source_target_pairs={{0,8},{4,12},{8,0},{12,4},{16,24},{20,28},{24,16},{28,20},{1,9},{5... | collective-permute-start | bytes 1572872 | tf_op jit(solution)/shard_map/ppermute | solution.py:686
  129.8 4.4 %collective-permute-start.15 = (f32[2,3,128]{2,1,0:T(4,128)}, f32[2,3,128]{2,1,0:T(4,128)S(1)}, u32[]{:S(2)}, u32[]{:S(2)}) collective-permute-start(f32[2,3,128]{2,1,0:T(4,128)} %get-tuple-element.99), channel_id=1, source_target_pairs={{0,4},{4,0},{8,12},{12,8},{16,20},{20,16},{24,28},{28,24},{1,5},{5... | collective-permute-start | bytes 9224 | tf_op jit(solution)/shard_map/ppermute | solution.py:686
  130.1 26.3 %collective-permute-start.16 = (f32[2,3,128]{2,1,0:T(4,128)}, f32[2,3,128]{2,1,0:T(4,128)S(1)}, u32[]{:S(2)}, u32[]{:S(2)}) collective-permute-start(f32[2,3,128]{2,1,0:T(4,128)} %get-tuple-element.99), channel_id=1, source_target_pairs={{0,16},{4,20},{8,24},{12,28},{16,0},{20,4},{24,8},{28,12},{1,17},{... | collective-permute-start | bytes 9224 | tf_op jit(solution)/shard_map/ppermute | solution.py:686
  132.9 24.7 %collective-permute-start.17 = (f32[2,3,128]{2,1,0:T(4,128)}, f32[2,3,128]{2,1,0:T(4,128)S(1)}, u32[]{:S(2)}, u32[]{:S(2)}) collective-permute-start(f32[2,3,128]{2,1,0:T(4,128)} %get-tuple-element.99), channel_id=1, source_target_pairs={{0,20},{4,16},{8,28},{12,24},{16,4},{20,0},{24,12},{28,8},{1,21},{... | collective-permute-start | bytes 9224 | tf_op jit(solution)/shard_map/ppermute | solution.py:686
  158.9 28.2 %collective-permute-start.20 = (bf16[2,288,960]{2,1,0:T(8,128)(2,1)}, bf16[2,288,960]{2,1,0:T(8,128)(2,1)S(1)}, u32[]{:S(2)}, u32[]{:S(2)}) collective-permute-start(bf16[2,288,960]{2,1,0:T(8,128)(2,1)} %collective-permute-done.18.refs_2_), channel_id=1, source_target_pairs={{0,4},{4,0},{8,12},{12,8},{16,20},{20,16},{24,28},{28,24},{1,5},{5... | collective-permute-start | bytes 3317768 | tf_op jit(solution)/shard_map/ppermute | solution.py:686
  183.5 34.7 %collective-permute-start.24 = (bf16[2,288,768]{2,1,0:T(8,128)(2,1)}, bf16[2,288,768]{2,1,0:T(8,128)(2,1)}, u32[]{:S(2)}, u32[]{:S(2)}) collective-permute-start(bf16[2,288,768]{2,1,0:T(8,128)(2,1)} %get-tuple-element.105), channel_id=1, source_target_pairs={{0,4},{4,0},{8,12},{12,8},{16,20},{20,16},{24,28},{28,24},{1,5},{5... | collective-permute-start | bytes 2654216 | tf_op jit(solution)/shard_map/ppermute | solution.py:686
  213.7 7.0 %collective-permute-start.21 = (f32[2,3,160]{2,1,0:T(4,128)}, f32[2,3,160]{2,1,0:T(4,128)S(1)}, u32[]{:S(2)}, u32[]{:S(2)}) collective-permute-start(f32[2,3,160]{2,1,0:T(4,128)} %get-tuple-element.114), channel_id=1, source_target_pairs={{0,4},{4,0},{8,12},{12,8},{16,20},{20,16},{24,28},{28,24},{1,5},{5... | collective-permute-start | bytes 11528 | tf_op jit(solution)/shard_map/ppermute | solution.py:686
  214.4 6.4 %collective-permute-start.22 = (f32[2,3,160]{2,1,0:T(4,128)}, f32[2,3,160]{2,1,0:T(4,128)S(1)}, u32[]{:S(2)}, u32[]{:S(2)}) collective-permute-start(f32[2,3,160]{2,1,0:T(4,128)} %get-tuple-element.114), channel_id=1, source_target_pairs={{0,16},{4,20},{8,24},{12,28},{16,0},{20,4},{24,8},{28,12},{1,17},{... | collective-permute-start | bytes 11528 | tf_op jit(solution)/shard_map/ppermute | solution.py:686
  214.7 6.1 %collective-permute-start.23 = (f32[2,3,160]{2,1,0:T(4,128)}, f32[2,3,160]{2,1,0:T(4,128)S(1)}, u32[]{:S(2)}, u32[]{:S(2)}) collective-permute-start(f32[2,3,160]{2,1,0:T(4,128)} %get-tuple-element.114), channel_id=1, source_target_pairs={{0,20},{4,16},{8,28},{12,24},{16,4},{20,0},{24,12},{28,8},{1,21},{... | collective-permute-start | bytes 11528 | tf_op jit(solution)/shard_map/ppermute | solution.py:686
  221.4 44.3 %collective-permute-start.29 = (bf16[2,288,768]{2,1,0:T(8,128)(2,1)}, bf16[2,288,768]{2,1,0:T(8,128)(2,1)S(1)}, u32[]{:S(2)}, u32[]{:S(2)}) collective-permute-start(bf16[2,288,768]{2,1,0:T(8,128)(2,1)} %get-tuple-element.131), channel_id=1, source_target_pairs={{0,4},{4,0},{8,12},{12,8},{16,20},{20,16},{24,28},{28,24},{1,5},{5... | collective-permute-start | bytes 2654216 | tf_op jit(solution)/shard_map/ppermute | solution.py:686
  222.1 45.3 %collective-permute-start.30 = (bf16[2,288,768]{2,1,0:T(8,128)(2,1)}, bf16[2,288,768]{2,1,0:T(8,128)(2,1)}, u32[]{:S(2)}, u32[]{:S(2)}) collective-permute-start(bf16[2,288,768]{2,1,0:T(8,128)(2,1)} %convert_add_fusion), channel_id=1, source_target_pairs={{0,16},{4,20},{8,24},{12,28},{16,0},{20,4},{24,8},{28,12},{1,17},{... | collective-permute-start | bytes 2654216 | tf_op jit(solution)/shard_map/ppermute | solution.py:686
  242.3 26.6 %collective-permute-start.26 = (f32[3,864]{1,0:T(4,128)S(1)}, f32[3,864]{1,0:T(4,128)S(1)}, u32[]{:S(2)}, u32[]{:S(2)}) collective-permute-start(f32[3,864]{1,0:T(4,128)S(1)} %get-tuple-element.167), channel_id=1, source_target_pairs={{0,4},{4,0},{8,12},{12,8},{16,20},{20,16},{24,28},{28,24},{1,5},{5... | collective-permute-start | bytes 31112 | tf_op jit(solution)/shard_map/ppermute | solution.py:686
  242.9 26.0 %collective-permute-start.27 = (f32[3,864]{1,0:T(4,128)S(1)}, f32[3,864]{1,0:T(4,128)S(1)}, u32[]{:S(2)}, u32[]{:S(2)}) collective-permute-start(f32[3,864]{1,0:T(4,128)S(1)} %get-tuple-element.167), channel_id=1, source_target_pairs={{0,16},{4,20},{8,24},{12,28},{16,0},{20,4},{24,8},{28,12},{1,17},{... | collective-permute-start | bytes 31112 | tf_op jit(solution)/shard_map/ppermute | solution.py:686
  243.6 25.3 %collective-permute-start.28 = (f32[3,864]{1,0:T(4,128)S(1)}, f32[3,864]{1,0:T(4,128)S(1)}, u32[]{:S(2)}, u32[]{:S(2)}) collective-permute-start(f32[3,864]{1,0:T(4,128)S(1)} %get-tuple-element.167), channel_id=1, source_target_pairs={{0,20},{4,16},{8,28},{12,24},{16,4},{20,0},{24,12},{28,8},{1,21},{... | collective-permute-start | bytes 31112 | tf_op jit(solution)/shard_map/ppermute | solution.py:686
  265.7 43.2 %collective-permute-start.25 = (bf16[1024,384]{1,0:T(8,128)(2,1)}, bf16[1024,384]{1,0:T(8,128)(2,1)}, u32[]{:S(2)}, u32[]{:S(2)}) collective-permute-start(bf16[1024,384]{1,0:T(8,128)(2,1)} %get-tuple-element.125), channel_id=1, source_target_pairs={{0,8},{4,12},{8,0},{12,4},{16,24},{20,28},{24,16},{28,20},{1,9},{5... | collective-permute-start | bytes 2359304 | tf_op jit(solution)/shard_map/ppermute | solution.py:686
  268.9 40.0 %collective-permute-start.31 = (bf16[2,288,960]{2,1,0:T(8,128)(2,1)}, bf16[2,288,960]{2,1,0:T(8,128)(2,1)S(1)}, u32[]{:S(2)}, u32[]{:S(2)}) collective-permute-start(bf16[2,288,960]{2,1,0:T(8,128)(2,1)} %get-tuple-element.133), channel_id=1, source_target_pairs={{0,4},{4,0},{8,12},{12,8},{16,20},{20,16},{24,28},{28,24},{1,5},{5... | collective-permute-start | bytes 3317768 | tf_op jit(solution)/shard_map/ppermute | solution.py:686
  271.3 37.7 %collective-permute-start.33 = (bf16[288,768]{1,0:T(8,128)(2,1)}, bf16[288,768]{1,0:T(8,128)(2,1)S(1)}, u32[]{:S(2)}, u32[]{:S(2)}) collective-permute-start(bf16[288,768]{1,0:T(8,128)(2,1)} %get-tuple-element.160), channel_id=1, source_target_pairs={{0,8},{4,12},{8,0},{12,4},{16,24},{20,28},{24,16},{28,20},{1,9},{5... | collective-permute-start | bytes 1327112 | tf_op jit(solution)/shard_map/ppermute | solution.py:686
  271.3 37.6 %collective-permute-start.32 = (f32[3,288]{1,0:T(4,128)S(1)}, f32[3,288]{1,0:T(4,128)S(1)}, u32[]{:S(2)}, u32[]{:S(2)}) collective-permute-start(f32[3,288]{1,0:T(4,128)S(1)} %pad_maximum_fusion.6), channel_id=1, source_target_pairs={{0,8},{4,12},{8,0},{12,4},{16,24},{20,28},{24,16},{28,20},{1,9},{5... | collective-permute-start | bytes 10376 | tf_op jit(solution)/shard_map/ppermute | solution.py:686
  308.9 5.3 %collective-permute-start.35 = (bf16[2,1024,640]{2,1,0:T(8,128)(2,1)}, bf16[2,1024,640]{2,1,0:T(8,128)(2,1)}, u32[]{:S(2)}, u32[]{:S(2)}) collective-permute-start(bf16[2,1024,640]{2,1,0:T(8,128)(2,1)} %get-tuple-element.144), channel_id=1, source_target_pairs={{0,1},{1,0},{2,3},{3,2},{4,5},{5,4},{6,7},{7,6},{8,9},{9,8},{10,11... | collective-permute-start | bytes 7864328 | tf_op jit(solution)/shard_map/ppermute | solution.py:689
  309.0 43.7 %collective-permute-start.34 = (bf16[2,1024,640]{2,1,0:T(8,128)(2,1)}, bf16[2,1024,640]{2,1,0:T(8,128)(2,1)}, u32[]{:S(2)}, u32[]{:S(2)}) collective-permute-start(bf16[2,1024,640]{2,1,0:T(8,128)(2,1)} %get-tuple-element.142), channel_id=1, source_target_pairs={{0,1},{1,0},{2,3},{3,2},{4,5},{5,4},{6,7},{7,6},{8,9},{9,8},{10,11... | collective-permute-start | bytes 7864328 | tf_op jit(solution)/shard_map/ppermute | solution.py:689
  316.9 32.6 %collective-permute-start.36 = (bf16[1024,640]{1,0:T(8,128)(2,1)}, bf16[1024,640]{1,0:T(8,128)(2,1)}, u32[]{:S(2)}, u32[]{:S(2)}) collective-permute-start(bf16[1024,640]{1,0:T(8,128)(2,1)} %join.7), channel_id=1, source_target_pairs={{0,2},{1,3},{2,0},{3,1},{4,6},{5,7},{6,4},{7,5},{8,10},{9,11},{10,... | collective-permute-start | bytes 3932168 | tf_op jit(solution)/shard_map/ppermute | solution.py:689
  317.1 28.0 %collective-permute-start.37 = (bf16[2,288,960]{2,1,0:T(8,128)(2,1)}, bf16[2,288,960]{2,1,0:T(8,128)(2,1)S(1)}, u32[]{:S(2)}, u32[]{:S(2)}) collective-permute-start(bf16[2,288,960]{2,1,0:T(8,128)(2,1)} %get-tuple-element.135), channel_id=1, source_target_pairs={{0,4},{4,0},{8,12},{12,8},{16,20},{20,16},{24,28},{28,24},{1,5},{5... | collective-permute-start | bytes 3317768 | tf_op jit(solution)/shard_map/ppermute | solution.py:686
  318.0 28.4 %collective-permute-start.38 = (bf16[288,960]{1,0:T(8,128)(2,1)}, bf16[288,960]{1,0:T(8,128)(2,1)S(1)}, u32[]{:S(2)}, u32[]{:S(2)}) collective-permute-start(bf16[288,960]{1,0:T(8,128)(2,1)} %join.6), channel_id=1, source_target_pairs={{0,16},{4,20},{8,24},{12,28},{16,0},{20,4},{24,8},{28,12},{1,17},{... | collective-permute-start | bytes 1658888 | tf_op jit(solution)/shard_map/ppermute | solution.py:686
  355.4 30.9 %collective-permute-start.39 = (bf16[1024,640]{1,0:T(8,128)(2,1)}, bf16[1024,640]{1,0:T(8,128)(2,1)S(1)}, u32[]{:S(2)}, u32[]{:S(2)}) collective-permute-start(bf16[1024,640]{1,0:T(8,128)(2,1)} %join.10), channel_id=1, source_target_pairs={{0,2},{1,3},{2,0},{3,1},{4,6},{5,7},{6,4},{7,5},{8,10},{9,11},{10,... | collective-permute-start | bytes 3932168 | tf_op jit(solution)/shard_map/ppermute | solution.py:689
  357.1 44.6 %collective-permute-start.40 = (bf16[1024,640]{1,0:T(8,128)(2,1)}, bf16[1024,640]{1,0:T(8,128)(2,1)}, u32[]{:S(2)}, u32[]{:S(2)}) collective-permute-start(bf16[1024,640]{1,0:T(8,128)(2,1)} %join.9), channel_id=1, source_target_pairs={{0,8},{4,12},{8,0},{12,4},{16,24},{20,28},{24,16},{28,20},{1,9},{5... | collective-permute-start | bytes 3932168 | tf_op jit(solution)/shard_map/ppermute | solution.py:686
  366.0 47.0 %collective-permute-start.42 = (bf16[288,960]{1,0:T(8,128)(2,1)}, bf16[288,960]{1,0:T(8,128)(2,1)S(1)}, u32[]{:S(2)}, u32[]{:S(2)}) collective-permute-start(bf16[288,960]{1,0:T(8,128)(2,1)} %join.8), channel_id=1, source_target_pairs={{0,8},{4,12},{8,0},{12,4},{16,24},{20,28},{24,16},{28,20},{1,9},{5... | collective-permute-start | bytes 1658888 | tf_op jit(solution)/shard_map/ppermute | solution.py:686
  368.0 42.9 %collective-permute-start.41 = (bf16[288,960]{1,0:T(8,128)(2,1)}, bf16[288,960]{1,0:T(8,128)(2,1)}, u32[]{:S(2)}, u32[]{:S(2)}) collective-permute-start(bf16[288,960]{1,0:T(8,128)(2,1)} %join.11), channel_id=1, source_target_pairs={{0,16},{4,20},{8,24},{12,28},{16,0},{20,4},{24,8},{28,12},{1,17},{... | collective-permute-start | bytes 1658888 | tf_op jit(solution)/shard_map/ppermute | solution.py:686
  (17 other events, 140.5 us)
